TPU v7x, 512 devices: a whole 4x4x16 slice. The times are simulated.
512 devices in a mesh: row: 16 (over z), col: 32 (over x, y, core).
Axes of the slice: x: 4, y: 4, z: 16, core: 2. Of those that a mesh axis runs over, the one named last changes fastest.
Arguments:
- matrix: float32 [16384, 16384], P('row', 'col'), as said below
Outputs:
- factored: float32 [16384, 16384], P('row', 'col')
Inputs may be any that keep to these rules, and one draw needn't show every extreme that they name: matrix in natural order is symmetric positive definite.
All inputs are finite; a program needn't handle non-finite values.
Results may differ from a plain program's by a relative error of at most 0.0003.
Values sent between devices are 32-bit elements; how exact they have to be, the bound alone decides.
No kernel may reach another device: no remote copies, remote signals or barrier semaphores. Data moves between devices by JAX's collectives and lax.ppermute only.
A program may use at most 64 MiB of HBM per device.

v0:
```python
import jax
import jax.numpy as jnp
from jax import lax
from jax.sharding import PartitionSpec as P

TILE = 128
PANELS = 2


def broadcast(value, axis, source):
    kept = jnp.where(lax.axis_index(axis) == source, value, 0).astype(value.dtype)
    return lax.psum(kept, axis)


def trailing_product(lower_rows, lower_cols):
    return jnp.dot(
        lower_rows,
        lower_cols.T,
        precision=lax.Precision.HIGHEST,
        preferred_element_type=jnp.float32,
    )


def on_device(matrix):
    rows_count, cols_count = matrix.shape
    grid_rows = lax.axis_size("row")
    grid_cols = lax.axis_size("col")
    row_index = lax.axis_index("row")
    col_index = lax.axis_index("col")
    tile_rows = rows_count // TILE
    tile_cols = cols_count // TILE
    row_tiles = jnp.repeat(jnp.arange(tile_rows, dtype=jnp.int32) * grid_rows + row_index, TILE)
    col_tiles = jnp.repeat(jnp.arange(tile_cols, dtype=jnp.int32) * grid_cols + col_index, TILE)
    picks = (
        jnp.arange(tile_cols, dtype=jnp.int32) * (grid_cols // grid_rows) + col_index // grid_rows
    )
    working = matrix
    deferred = None
    for panel_index in range(PANELS):
        owner_row = panel_index % grid_rows
        local_tile = panel_index // grid_rows
        column_block = working[:, :TILE]
        own_factor = jnp.linalg.cholesky(column_block[local_tile * TILE : (local_tile + 1) * TILE])
        factor = broadcast(own_factor, "row", owner_row)
        solved_here = jax.scipy.linalg.solve_triangular(factor, column_block.T, lower=True).T
        solved = broadcast(solved_here, "col", panel_index)
        lower_rows = jnp.where(row_tiles[:, None] > panel_index, solved, jnp.float32(0.0))
        diag_slot = lower_rows[local_tile * TILE : (local_tile + 1) * TILE]
        panel_full = lower_rows.at[local_tile * TILE : (local_tile + 1) * TILE].set(
            jnp.where(row_index == owner_row, factor, diag_slot)
        )
        picked = jnp.take(panel_full.reshape(tile_rows, TILE, TILE), picks, axis=0).reshape(
            tile_cols * TILE, TILE
        )
        cols_here = broadcast(picked, "row", col_index % grid_rows)
        lower_cols = jnp.where(col_tiles[:, None] > panel_index, cols_here, jnp.float32(0.0))
        working = working.at[:, :TILE].set(
            jnp.where(col_index == panel_index, panel_full, working[:, :TILE])
        )
        working = working - trailing_product(lower_rows, lower_cols)
    return jnp.where(row_tiles[:, None] < col_tiles[None, :], jnp.float32(0.0), working)


def solution(mesh):
    in_specs = (P("row", "col"),)
    out_specs = P("row", "col")
    return jax.shard_map(
        on_device, mesh=mesh, in_specs=in_specs, out_specs=out_specs, check_vma=False
    )
```

profile of v0, /device:TPU:1, one launch (start us, length us, event | category | flops | bytes accessed | tf_op | source)
XLA Modules:
  0.0 873.9 jit_solution(6874097411262640506)
XLA Ops:
  6.5 0.0 all-reduce.7.cloned.1.call-start
  6.5 1.6 copy.22
  8.1 0.1 copy.10
  8.3 11.7 %cholesky.44 = f32[128,128]{1,0:T(8,128)S(1)} custom-call(f32[128,128]{1,0:T(8,128)S(1)} %fusion.19), custom_call_target="Cholesky" | custom-call | tf_op jit(solution)/shard_map/jit(cholesky)/cholesky | solution.py:43
  20.0 0.7 compare_reduce_fusion.1
  20.7 1.3 fusion.21
  22.1 0.0 all-reduce.7.cloned.1.call-update
  22.1 0.0 all-reduce.9.cloned.1.call-start
  22.2 0.1 bitcast_compare_fusion.2
  22.3 127.8 %all-reduce.7.cloned.1.call-done = f32[128,128]{1,0:T(8,128)} async-done(((f32[128,128]{1,0:T(8,128)}), f32[128,128]{1,0:T(8,128)}) %all-reduce.7.cloned.1.call-update) | async-done | bytes 65552 | tf_op jit(solution)/shard_map/psum | solution.py:12
  150.1 0.0 copy-start.2
  150.1 0.9 select_bitcast_fusion.1
  151.0 9.8 %custom-call.6 = f32[1,128,128]{1,2,0:T(8,128)S(1)} custom-call(f32[1,128,128]{2,1,0:T(8,128)S(1)} %select_bitcast_fusion.1), custom_call_target="InvertDiagBlocksLowerTriangular" | custom-call | tf_op jit(solution)/shard_map/jit(_solve_triangular)/triangular_solve | solution.py:45
  160.9 1.4 fusion.1
  162.2 0.0 all-reduce.9.cloned.1.call-update
  162.2 0.0 all-reduce.11.cloned.1.call-start
  162.3 0.6 compare_reduce_fusion.2
  162.9 0.1 bitcast_compare_fusion
  163.0 140.4 %all-reduce.9.cloned.1.call-done = f32[1024,128]{1,0:T(8,128)} async-done(((f32[1024,128]{1,0:T(8,128)}), f32[1024,128]{1,0:T(8,128)}) %all-reduce.9.cloned.1.call-update) | async-done | bytes 524304 | tf_op jit(solution)/shard_map/psum | solution.py:12
  303.4 1.2 broadcast_select_fusion.1
  304.7 0.0 copy-done.2
  304.7 0.6 gather_fusion
  305.3 0.8 select_select_fusion.3
  306.1 0.0 all-reduce.11.cloned.1.call-update
  306.1 0.2 all-reduce.13.cloned.1.call-start
  306.3 0.7 fusion.2
  307.1 125.1 %all-reduce.11.cloned.1.call-done = f32[512,128]{1,0:T(8,128)} async-done(((f32[512,128]{1,0:T(8,128)}), f32[512,128]{1,0:T(8,128)}) %all-reduce.11.cloned.1.call-update) | async-done | bytes 262160 | tf_op jit(solution)/shard_map/psum | solution.py:12
  432.1 2.8 convolution_subtract_fusion
  435.0 0.0 copy-start
  435.0 1.3 copy-done
  436.3 0.1 copy.5
  436.4 0.9 fusion.17
  437.3 0.1 copy.6
  437.4 11.7 %cholesky.55 = f32[128,128]{1,0:T(8,128)S(1)} custom-call(f32[128,128]{1,0:T(8,128)S(1)} %copy.6), custom_call_target="Cholesky" | custom-call | tf_op jit(solution)/shard_map/jit(cholesky)/cholesky | solution.py:43
  449.1 0.7 compare_reduce_fusion
  449.8 1.2 select_select_fusion.4
  451.0 0.0 all-reduce.13.cloned.1.call-update
  451.1 0.0 all-reduce.15.cloned.1.call-start
  451.1 128.6 %all-reduce.13.cloned.1.call-done = f32[128,128]{1,0:T(8,128)} async-done(((f32[128,128]{1,0:T(8,128)}), f32[128,128]{1,0:T(8,128)}) %all-reduce.13.cloned.1.call-update) | async-done | bytes 65552 | tf_op jit(solution)/shard_map/psum | solution.py:12
  579.7 0.0 copy-start.3
  579.7 0.9 select_bitcast_fusion
  580.6 9.8 %custom-call.7 = f32[1,128,128]{1,2,0:T(8,128)S(1)} custom-call(f32[1,128,128]{2,1,0:T(8,128)S(1)} %select_bitcast_fusion), custom_call_target="InvertDiagBlocksLowerTriangular" | custom-call | tf_op jit(solution)/shard_map/jit(_solve_triangular)/triangular_solve | solution.py:45
  590.5 2.4 fusion
  592.9 0.0 copy-start.1
  592.9 0.0 all-reduce.15.cloned.1.call-update
  592.9 0.0 all-reduce.17.cloned.1.call-start
  593.0 0.1 broadcast_bitcast_fusion.1
  593.0 0.1 broadcast_bitcast_fusion
  593.1 141.0 %all-reduce.15.cloned.1.call-done = f32[1024,128]{1,0:T(8,128)} async-done(((f32[1024,128]{1,0:T(8,128)}), f32[1024,128]{1,0:T(8,128)}) %all-reduce.15.cloned.1.call-update) | async-done | bytes 524304 | tf_op jit(solution)/shard_map/psum | solution.py:12
  734.1 1.2 broadcast_select_fusion
  735.4 0.0 copy-done.3
  735.4 0.6 gather_fusion.1
  736.0 0.8 select_select_fusion.2
  736.8 0.0 all-reduce.17.cloned.1.call-update
  736.8 0.0 copy-done.1
  736.8 0.7 fusion.3
  737.5 125.3 %all-reduce.17.cloned.1.call-done = f32[512,128]{1,0:T(8,128)} async-done(((f32[512,128]{1,0:T(8,128)}), f32[512,128]{1,0:T(8,128)}) %all-reduce.17.cloned.1.call-update) | async-done | bytes 262160 | tf_op jit(solution)/shard_map/psum | solution.py:12
  862.8 4.3 subtract_select_fusion
  (14 shorter events, 0.2 us)
Async XLA Ops:
  6.5 143.6 %all-reduce.7.cloned.1.call-start = ((), (), s32[]{:S(2)}) async-start(), calls=%async_computation | async-start | bytes 131072 | tf_op jit(solution)/shard_map/psum | solution.py:12
  22.1 281.3 %all-reduce.9.cloned.1.call-start = ((), (), s32[]{:S(2)}) async-start(), calls=%async_computation.1 | async-start | bytes 1048576 | tf_op jit(solution)/shard_map/psum | solution.py:12
  150.1 154.6 %copy-start.2 = (f32[128,128]{1,0:T(8,128)S(1)}, f32[128,128]{1,0:T(8,128)}, u32[]{:S(2)}) copy-start(f32[128,128]{1,0:T(8,128)} %all-reduce.7.cloned.1.call-done) | copy-start | bytes 196612
  162.2 269.9 %all-reduce.11.cloned.1.call-start = ((), (), s32[]{:S(2)}) async-start(), calls=%async_computation.2 | async-start | bytes 524288 | tf_op jit(solution)/shard_map/psum | solution.py:12
  306.1 273.6 %all-reduce.13.cloned.1.call-start = ((), (), s32[]{:S(2)}) async-start(), calls=%async_computation.3 | async-start | bytes 131072 | tf_op jit(solution)/shard_map/psum | solution.py:12
  435.0 1.3 copy-start
  451.1 283.0 %all-reduce.15.cloned.1.call-start = ((), (), s32[]{:S(2)}) async-start(), calls=%async_computation.4 | async-start | bytes 1048576 | tf_op jit(solution)/shard_map/psum | solution.py:12
  579.7 155.6 %copy-start.3 = (f32[128,128]{1,0:T(8,128)S(1)}, f32[128,128]{1,0:T(8,128)}, u32[]{:S(2)}) copy-start(f32[128,128]{1,0:T(8,128)} %all-reduce.13.cloned.1.call-done) | copy-start | bytes 196612
  592.9 143.9 %copy-start.1 = (f32[1024,512]{1,0:T(8,128)S(1)}, f32[1024,512]{1,0:T(8,128)}, u32[]{:S(2)}) copy-start(f32[1024,512]{1,0:T(8,128)} %copy-done) | copy-start | bytes 6291460
  592.9 269.9 %all-reduce.17.cloned.1.call-start = ((), (), s32[]{:S(2)}) async-start(), calls=%async_computation.5 | async-start | bytes 524288 | tf_op jit(solution)/shard_map/psum | solution.py:12
Sparse Core Ops, SparseCore 0:
  22.2 127.8 all-reduce.6
  162.4 140.9 all-reduce.8
  306.2 125.8 all-reduce.10
  451.2 128.4 all-reduce.12
  593.0 140.9 all-reduce.14
  736.9 125.8 all-reduce.16
where the time goes:
time: 883 us; the launch traced here: 874 us
  waiting for transfers between devices  788 us (89%)
  other arithmetic  56.1 us (6%)
  between operations  13.7 us (2%)
  matrix products  10.9 us (1%)
    psum x6, waiting for transfers between devices, broadcast(): return lax.psum(kept, axis)  788 us
    another operation x6, other arithmetic, on_device(): jnp.linalg.cholesky(column_block[local_tile * TILE:(local_tile + 1) * TILE])  24.9 us
    another operation x4, other arithmetic, on_device(): jax.scipy.linalg.solve_triangular(factor, column_block.T, lower=True)  21.5 us
  transfers between devices with their start and end apart: 6, of which 6 were waited for; matrix products, arithmetic and copies ran while one was open for 0% of the time, Pallas kernels for 0%

commit v1 on v0

v1 whole, which is shorter than its diff:
```python
import jax
import jax.numpy as jnp
from jax import lax
from jax.experimental import pallas as pl
from jax.experimental.pallas import tpu as pltpu
from jax.sharding import PartitionSpec as P

TILE = 128
PANELS = 2
WIDTH = TILE * PANELS
STRIP = 32
GROUP = 8
HIGHEST = lax.Precision.HIGHEST


def product(lhs, rhs, contract):
    return lax.dot_general(
        lhs, rhs, (contract, ((), ())), precision=HIGHEST, preferred_element_type=jnp.float32
    )


def eliminate(strip, pivot_lane):
    tiles = [strip[t * GROUP : (t + 1) * GROUP] for t in range(STRIP // GROUP)]
    sub_row = lax.broadcasted_iota(jnp.int32, (GROUP, 1), 0)
    scales = [jnp.ones((GROUP, 1), jnp.float32) for _ in tiles]
    for i in range(STRIP):
        lane = pivot_lane + i
        own, sub = divmod(i, GROUP)
        row = tiles[own][sub : sub + 1, :]
        pivot = tiles[own][sub : sub + 1, lane : lane + 1]
        inverse = 1.0 / pivot
        scales[own] = jnp.where(sub_row == sub, lax.rsqrt(pivot), scales[own])
        for t in range(own, STRIP // GROUP):
            factor = tiles[t][:, lane : lane + 1] * inverse
            if t == own:
                factor = jnp.where(sub_row > sub, factor, 0.0)
            tiles[t] = tiles[t] - factor * row
    return jnp.concatenate([tile * scale for tile, scale in zip(tiles, scales)], axis=0)


def inverse_factor_kernel(diag_ref, inverse_ref, work_ref):
    for p in range(PANELS):
        rows = slice(p * TILE, (p + 1) * TILE)
        work_ref[rows, :] = diag_ref[: TILE // GROUP, p].reshape(TILE, WIDTH)
    at_row = lax.broadcasted_iota(jnp.int32, (WIDTH, WIDTH), 0)
    at_col = lax.broadcasted_iota(jnp.int32, (WIDTH, WIDTH), 1)
    inverse_ref[...] = jnp.where(at_row == at_col, 1.0, 0.0).astype(jnp.float32)
    for start in range(0, WIDTH, STRIP):
        stop = start + STRIP
        first = start // TILE * TILE
        upper = WIDTH - first
        done = first + TILE
        strip = jnp.concatenate(
            [work_ref[start:stop, first:], inverse_ref[start:stop, :done]], axis=1
        )
        strip = eliminate(strip, start - first)
        inverse_ref[start:stop, :done] = strip[:, upper:]
        if stop < WIDTH:
            update = product(strip[:, :upper], strip, ((0,), (0,)))[stop - first :]
            work_ref[stop:, first:] = work_ref[stop:, first:] - update[:, :upper]
            inverse_ref[stop:, :done] = inverse_ref[stop:, :done] - update[:, upper:]


def inverse_factor(diag):
    return pl.pallas_call(
        inverse_factor_kernel,
        out_shape=jax.ShapeDtypeStruct((WIDTH, WIDTH), jnp.float32),
        scratch_shapes=[pltpu.VMEM((WIDTH, WIDTH), jnp.float32)],
        name="inverse_factor",
    )(diag)


def trailing_kernel(place_ref, matrix_ref, rows_ref, cols_ref, inverse_ref, out_ref, solved_ref):
    step = pl.program_id(0)
    grid_rows, grid_cols, row_index, col_index = (place_ref[k] for k in range(4))
    inverse = inverse_ref[...]
    tile_cols = matrix_ref.shape[1] // TILE

    @pl.when(step == 0)
    def _():
        cols = jnp.concatenate(
            [cols_ref[:, p].reshape(TILE, matrix_ref.shape[1]) for p in range(PANELS)], axis=0
        )
        solved_ref[...] = product(inverse, cols, ((1,), (0,)))

    raw = jnp.concatenate(
        [rows_ref[:, p, 0].reshape(TILE, TILE) for p in range(PANELS)], axis=1
    )
    lower = product(raw, inverse, ((1,), (1,)))
    trailing = matrix_ref[...] - product(lower, solved_ref[...], ((1,), (0,)))
    tile_row = step * grid_rows + row_index
    at_row = lax.broadcasted_iota(jnp.int32, (TILE, TILE), 0)
    at_col = lax.broadcasted_iota(jnp.int32, (TILE, TILE), 1)
    for b in range(tile_cols):
        span = slice(b * TILE, (b + 1) * TILE)
        tile_col = b * grid_cols + col_index
        value = trailing[:, span]
        for p in range(PANELS):
            value = jnp.where(tile_col == p, lower[:, p * TILE : (p + 1) * TILE], value)
        keep = (tile_row - tile_col) * TILE + at_row - at_col >= 0
        keep = keep | ((tile_row == tile_col) & (tile_col >= PANELS))
        out_ref[:, span] = jnp.where(keep, value, 0.0)


def trailing(place, matrix, rows, cols, inverse):
    rows_count, cols_count = matrix.shape
    peers, _, groups, _, _ = rows.shape
    parts = rows_count // TILE // groups
    return pl.pallas_call(
        trailing_kernel,
        grid=(rows_count // TILE,),
        out_shape=jax.ShapeDtypeStruct(matrix.shape, jnp.float32),
        in_specs=[
            pl.BlockSpec(memory_space=pltpu.SMEM),
            pl.BlockSpec((TILE, cols_count), lambda t: (t, 0)),
            pl.BlockSpec(
                (peers // parts, PANELS, 1, GROUP, TILE), lambda t: (t % parts, 0, t // parts, 0, 0)
            ),
            pl.BlockSpec(cols.shape, lambda t: (0, 0, 0, 0)),
            pl.BlockSpec(inverse.shape, lambda t: (0, 0)),
        ],
        out_specs=pl.BlockSpec((TILE, cols_count), lambda t: (t, 0)),
        scratch_shapes=[pltpu.VMEM((WIDTH, cols_count), jnp.float32)],
        name="trailing",
    )(place, matrix, rows, cols, inverse)


def exchange(chunks, axis):
    return lax.all_to_all(chunks, axis, 0, 0, tiled=True)


def to_all(part, axis):
    count = lax.axis_size(axis)
    return exchange(jnp.broadcast_to(part[None], (count, *part.shape)), axis)


def on_device(matrix):
    rows_count, cols_count = matrix.shape
    grid_rows = lax.axis_size("row")
    grid_cols = lax.axis_size("col")
    groups = rows_count // (grid_cols * GROUP)
    with jax.named_scope("scatter_rows"):
        panel = matrix[:, :TILE].reshape(groups, grid_cols, GROUP, TILE).transpose(1, 0, 2, 3)
        row_part = exchange(panel, "col")[:PANELS]
    with jax.named_scope("scatter_cols"):
        col_part = exchange(matrix[:TILE].reshape(grid_rows, GROUP, cols_count), "row")[:PANELS]
    with jax.named_scope("spread_diagonal"):
        own_diag = row_part[:, 0].transpose(1, 0, 2).reshape(GROUP, PANELS * TILE)
        diag_part = to_all(own_diag, "row")[:PANELS]
        diag = to_all(diag_part, "col")
    with jax.named_scope("gather_rows"):
        rows = to_all(row_part, "col")
    with jax.named_scope("gather_cols"):
        cols = to_all(col_part, "row")
    inverse = inverse_factor(diag)
    place = jnp.stack(
        [jnp.int32(grid_rows), jnp.int32(grid_cols), lax.axis_index("row"), lax.axis_index("col")]
    ).astype(jnp.int32)
    return trailing(place, matrix, rows, cols, inverse)


def solution(mesh):
    return jax.shard_map(
        on_device, mesh=mesh, in_specs=(P("row", "col"),), out_specs=P("row", "col"), check_vma=False
    )
```

time: 883 us -> 161 us (0.18)
  waiting for transfers between devices: 788 us -> 53.4 us
  other arithmetic: 56.1 us -> 0.56 us
  Pallas kernels: 0 us -> 37.7 us
  starting transfers between devices: 0.39 us -> 37.9 us
  blocking collectives: 0 us -> 21.3 us
  between operations: 13.7 us -> 0.09 us
  matrix products: 10.9 us -> 0 us
    psum x6 -> x0, waiting for transfers between devices: 788 us -> none  [broadcast(): return lax.psum(kept, axis)]
    all_to_all x0 -> x5, waiting for transfers between devices: none -> 53.4 us  [exchange(): return lax.all_to_all(chunks, axis, 0, 0, tiled=True)]
    another operation x11 -> x1, other arithmetic: 47 us -> 0.56 us  [on_device(): jnp.stack([jnp.int32(grid_rows), jnp.int32(grid_cols), lax.axis_index('ro...]
    all_to_all x0 -> x5, starting transfers between devices: none -> 37.9 us  [exchange(): return lax.all_to_all(chunks, axis, 0, 0, tiled=True)]
    pallas_call x0 -> x2, Pallas kernels: none -> 37.7 us  [the longest x1 26 us: inverse_factor(): pl.pallas_call(inverse_factor_kernel, out_shape=jax.ShapeDtypeStruct((WID...]
    all_to_all x0 -> x1, blocking collectives: none -> 21.3 us  [exchange(): return lax.all_to_all(chunks, axis, 0, 0, tiled=True)]
  transfers between devices with their start and end apart: 6 -> 5, of which waited for: 6 -> 4; matrix products, arithmetic and copies ran while one was open for 0% -> 1% of each run, Pallas kernels for 0% -> 16%
where the time goes in v1:
time: 161 us; the launch traced here: 158 us
  waiting for transfers between devices  53.4 us (33%)
  starting transfers between devices  37.9 us (24%)
  Pallas kernels  37.7 us (23%)
  blocking collectives  21.3 us (13%)
  local copies, waits for them, and re-layouts  7.24 us (4%)
    all_to_all x5, waiting for transfers between devices, exchange(): return lax.all_to_all(chunks, axis, 0, 0, tiled=True)  53.4 us
    all_to_all x5, starting transfers between devices, exchange(): return lax.all_to_all(chunks, axis, 0, 0, tiled=True)  37.9 us
    pallas_call x1, Pallas kernels, inverse_factor(): pl.pallas_call(inverse_factor_kernel, out_shape=jax.ShapeDtypeStruct((WID...  26 us
    all_to_all x1, blocking collectives, exchange(): return lax.all_to_all(chunks, axis, 0, 0, tiled=True)  21.3 us
    pallas_call x1, Pallas kernels, trailing(): pl.pallas_call(trailing_kernel, grid=(rows_count // TILE,), out_shape=jax...  11.7 us
    broadcast_in_dim x5, local copies, waits for them, and re-layouts, to_all(): return exchange(jnp.broadcast_to(part[None], (count, *part.shape)), axis)  3.61 us
  transfers between devices with their start and end apart: 5, of which 4 were waited for; matrix products, arithmetic and copies ran while one was open for 1% of the time, Pallas kernels for 16%

profile of v1, /device:TPU:1, one launch (start us, length us, event | category | flops | bytes accessed | tf_op | source)
XLA Modules:
  0.0 158.2 jit_solution(7561799606676813245)
XLA Ops:
  0.0 1.1 slice.19
  1.1 0.1 copy.4
  1.1 21.3 %all_to_all.30 = f32[32,4,8,128]{3,2,1,0:T(8,128)S(1)} all-to-all(f32[32,4,8,128]{3,2,1,0:T(8,128)S(1)} %bitcast.14), channel_id=1, replica_groups=mesh['row'=16,'col'=32] {'col'}, dimensions={0} | all-to-all | bytes 1048576 | tf_op jit(solution)/shard_map/scatter_rows/all_to_all | solution.py:129
  22.4 0.7 broadcast_in_dim.13
  23.1 13.7 %all-to-all-start.4 = ((f32[16,8,256]{2,1,0:T(8,128)}), f32[16,8,256]{2,1,0:T(8,128)S(1)}, u32[]{:S(2)}, u32[]{:S(2)}) async-start(f32[16,8,256]{2,1,0:T(8,128)} %broadcast_in_dim.13), calls=%async_computation.4 | async-start | bytes 262144 | tf_op jit(solution)/shard_map/spread_diagonal/all_to_all | solution.py:129
  36.7 1.7 %slice_bitcast_fusion = f32[16,8,512]{2,1,0:T(8,128)} fusion(f32[1024,512]{1,0:T(8,128)} %matrix_ref.1), kind=kLoop, calls=%fused_computation.1 | loop fusion | bytes 524288 | tf_op jit(solution)/shard_map/scatter_cols/reshape | solution.py:146
  38.4 11.1 %all-to-all-done.4 = f32[16,8,256]{2,1,0:T(8,128)S(1)} async-done(((f32[16,8,256]{2,1,0:T(8,128)}), f32[16,8,256]{2,1,0:T(8,128)S(1)}, u32[]{:S(2)}, u32[]{:S(2)}) %all-to-all-start.4) | async-done | bytes 131104 | tf_op jit(solution)/shard_map/spread_diagonal/all_to_all | solution.py:129
  49.5 6.0 %all-to-all-start.2 = ((f32[16,8,512]{2,1,0:T(8,128)}), f32[16,8,512]{2,1,0:T(8,128)S(1)}, u32[]{:S(2)}, u32[]{:S(2)}) async-start(f32[16,8,512]{2,1,0:T(8,128)} %slice_bitcast_fusion), calls=%async_computation.2 | async-start | bytes 524288 | tf_op jit(solution)/shard_map/scatter_cols/all_to_all | solution.py:129
  55.5 13.8 %all-to-all-done.2 = f32[16,8,512]{2,1,0:T(8,128)S(1)} async-done(((f32[16,8,512]{2,1,0:T(8,128)}), f32[16,8,512]{2,1,0:T(8,128)S(1)}, u32[]{:S(2)}, u32[]{:S(2)}) %all-to-all-start.2) | async-done | bytes 262176 | tf_op jit(solution)/shard_map/scatter_cols/all_to_all | solution.py:129
  69.3 0.9 broadcast_in_dim.14
  70.2 8.9 %all-to-all-start.5 = ((f32[32,2,8,256]{3,2,1,0:T(8,128)}), f32[32,2,8,256]{3,2,1,0:T(8,128)S(1)}, u32[]{:S(2)}, u32[]{:S(2)}) async-start(f32[32,2,8,256]{3,2,1,0:T(8,128)} %broadcast_in_dim.14), calls=%async_computation.5 | async-start | bytes 1048576 | tf_op jit(solution)/shard_map/spread_diagonal/all_to_all | solution.py:129
  79.1 11.7 %all-to-all-done.5.diag_ref = f32[32,2,8,256]{3,2,1,0:T(8,128)S(1)} async-done(((f32[32,2,8,256]{3,2,1,0:T(8,128)}), f32[32,2,8,256]{3,2,1,0:T(8,128)S(1)}, u32[]{:S(2)}, u32[]{:S(2)}) %all-to-all-start.5) | async-done | bytes 524320 | tf_op jit(solution)/shard_map/spread_diagonal/all_to_all | solution.py:129
  90.8 0.0 copy-start.2
  90.8 1.1 broadcast_in_dim.10
  92.0 3.7 %all-to-all-start.1 = ((f32[32,2,4,8,128]{4,3,2,1,0:T(8,128)}), f32[32,2,4,8,128]{4,3,2,1,0:T(8,128)S(1)}, u32[]{:S(2)}, u32[]{:S(2)}) async-start(f32[32,2,4,8,128]{4,3,2,1,0:T(8,128)} %broadcast_in_dim.10), calls=%async_computation.1 | async-start | bytes 2097152 | tf_op jit(solution)/shard_map/gather_rows/all_to_all | solution.py:129
  95.7 16.8 %all-to-all-done.1.rows_ref = f32[32,2,4,8,128]{4,3,2,1,0:T(8,128)S(1)} async-done(((f32[32,2,4,8,128]{4,3,2,1,0:T(8,128)}), f32[32,2,4,8,128]{4,3,2,1,0:T(8,128)S(1)}, u32[]{:S(2)}, u32[]{:S(2)}) %all-to-all-start.1) | async-done | bytes 1048608 | tf_op jit(solution)/shard_map/gather_rows/all_to_all | solution.py:129
  112.5 0.0 copy-start
  112.5 1.0 broadcast_in_dim.11
  113.4 0.0 copy-done.2
  113.4 5.7 %all-to-all-start.3 = ((f32[16,2,8,512]{3,2,1,0:T(8,128)}), f32[16,2,8,512]{3,2,1,0:T(8,128)S(1)}, u32[]{:S(2)}, u32[]{:S(2)}) async-start(f32[16,2,8,512]{3,2,1,0:T(8,128)} %broadcast_in_dim.11), calls=%async_computation.3 | async-start | bytes 1048576 | tf_op jit(solution)/shard_map/gather_cols/all_to_all | solution.py:129
  119.1 0.6 pad_add_fusion.place_ref
  119.7 26.0 %inverse_factor.1.inverse_ref = f32[256,256]{1,0:T(8,128)} custom-call(f32[32,2,8,256]{3,2,1,0:T(8,128)} %copy-done.2), custom_call_target="tpu_custom_call" | custom-call | tf_op jit(solution)/shard_map/inverse_factor/pallas_call | solution.py:65
  145.7 0.0 all-to-all-done.3.cols_ref
  145.7 0.0 copy-done
  145.7 0.0 copy-start.1
  145.7 0.8 copy-done.1
  146.5 11.7 %trailing.1 = f32[1024,512]{1,0:T(8,128)} custom-call(s32[4]{0:T(128)} %pad_add_fusion.place_ref, f32[1024,512]{1,0:T(8,128)} %matrix_ref.1, f32[32,2,4,8,128]{4,3,2,1,0:T(8,128)} %copy-done, f32[16,2,8,512]{3,2,1,0:T(8,128)} %copy-done.1, f32[256,256]{1,0:T(8,128)} %inverse_factor.1.inverse_ref), custom_call_target="tpu_custom_call" | custom-call | tf_op jit(solution)/shard_map/trailing/pallas_call | solution.py:109
  (4 shorter events, 0.0 us)
Async XLA Ops:
  23.1 26.5 %all-to-all-start.4 = ((f32[16,8,256]{2,1,0:T(8,128)}), f32[16,8,256]{2,1,0:T(8,128)S(1)}, u32[]{:S(2)}, u32[]{:S(2)}) async-start(f32[16,8,256]{2,1,0:T(8,128)} %broadcast_in_dim.13), calls=%async_computation.4 | async-start | bytes 262144 | tf_op jit(solution)/shard_map/spread_diagonal/all_to_all | solution.py:129
  49.5 19.8 %all-to-all-start.2 = ((f32[16,8,512]{2,1,0:T(8,128)}), f32[16,8,512]{2,1,0:T(8,128)S(1)}, u32[]{:S(2)}, u32[]{:S(2)}) async-start(f32[16,8,512]{2,1,0:T(8,128)} %slice_bitcast_fusion), calls=%async_computation.2 | async-start | bytes 524288 | tf_op jit(solution)/shard_map/scatter_cols/all_to_all | solution.py:129
  70.2 20.6 %all-to-all-start.5 = ((f32[32,2,8,256]{3,2,1,0:T(8,128)}), f32[32,2,8,256]{3,2,1,0:T(8,128)S(1)}, u32[]{:S(2)}, u32[]{:S(2)}) async-start(f32[32,2,8,256]{3,2,1,0:T(8,128)} %broadcast_in_dim.14), calls=%async_computation.5 | async-start | bytes 1048576 | tf_op jit(solution)/shard_map/spread_diagonal/all_to_all | solution.py:129
  90.8 22.6 %copy-start.2 = (f32[32,2,8,256]{3,2,1,0:T(8,128)}, f32[32,2,8,256]{3,2,1,0:T(8,128)S(1)}, u32[]{:S(2)}) copy-start(f32[32,2,8,256]{3,2,1,0:T(8,128)S(1)} %all-to-all-done.5.diag_ref) | copy-start | bytes 1572868
  92.0 20.5 %all-to-all-start.1 = ((f32[32,2,4,8,128]{4,3,2,1,0:T(8,128)}), f32[32,2,4,8,128]{4,3,2,1,0:T(8,128)S(1)}, u32[]{:S(2)}, u32[]{:S(2)}) async-start(f32[32,2,4,8,128]{4,3,2,1,0:T(8,128)} %broadcast_in_dim.10), calls=%async_computation.1 | async-start | bytes 2097152 | tf_op jit(solution)/shard_map/gather_rows/all_to_all | solution.py:129
  112.5 33.2 %copy-start = (f32[32,2,4,8,128]{4,3,2,1,0:T(8,128)}, f32[32,2,4,8,128]{4,3,2,1,0:T(8,128)S(1)}, u32[]{:S(2)}) copy-start(f32[32,2,4,8,128]{4,3,2,1,0:T(8,128)S(1)} %all-to-all-done.1.rows_ref) | copy-start | bytes 3145732
  113.4 32.3 %all-to-all-start.3 = ((f32[16,2,8,512]{3,2,1,0:T(8,128)}), f32[16,2,8,512]{3,2,1,0:T(8,128)S(1)}, u32[]{:S(2)}, u32[]{:S(2)}) async-start(f32[16,2,8,512]{3,2,1,0:T(8,128)} %broadcast_in_dim.11), calls=%async_computation.3 | async-start | bytes 1048576 | tf_op jit(solution)/shard_map/gather_cols/all_to_all | solution.py:129
  145.7 0.8 copy-start.1

commit v2 on v1

v2 whole, which is shorter than its diff:
```python
import jax
import jax.numpy as jnp
from jax import lax
from jax.experimental import pallas as pl
from jax.experimental.pallas import tpu as pltpu
from jax.sharding import PartitionSpec as P

TILE = 128
PANELS = 2
WIDTH = TILE * PANELS
STRIP = 64
GROUP = 8
HIGHEST = lax.Precision.HIGHEST


def product(lhs, rhs, contract):
    return lax.dot_general(
        lhs, rhs, (contract, ((), ())), precision=HIGHEST, preferred_element_type=jnp.float32
    )


def split(value):
    high = value.astype(jnp.bfloat16)
    return high, (value - high.astype(jnp.float32)).astype(jnp.bfloat16)


def eliminate(strip, pivot_lane):
    count, width = strip.shape
    tiles = [
        [strip[t * GROUP : (t + 1) * GROUP, v * TILE : (v + 1) * TILE] for v in range(width // TILE)]
        for t in range(count // GROUP)
    ]
    shape = (GROUP, TILE)
    sub_row = lax.broadcasted_iota(jnp.int32, shape, 0)
    pivots = [jnp.ones(shape, jnp.float32) for _ in tiles]
    for i in range(count):
        block, lane = divmod(pivot_lane + i, TILE)
        own, sub = divmod(i, GROUP)
        below = range(own, count // GROUP)
        columns = [jnp.broadcast_to(tiles[t][block][:, lane : lane + 1], shape) for t in below]
        pivot = jnp.broadcast_to(columns[0][sub : sub + 1], shape)
        pivots[own] = jnp.where(sub_row == sub, pivot, pivots[own])
        inverse = 1.0 / pivot
        rows = [jnp.broadcast_to(part[sub : sub + 1], shape) * inverse for part in tiles[own]]
        columns[0] = jnp.where(sub_row > sub, columns[0], 0.0)
        for t, column in zip(below, columns):
            tiles[t] = [part - column * row for part, row in zip(tiles[t], rows)]
    scaled = []
    for parts, pivot in zip(tiles, pivots):
        scale = lax.rsqrt(pivot)
        scaled.append(jnp.concatenate([part * scale for part in parts], axis=1))
    return jnp.concatenate(scaled, axis=0)


def inverse_factor_kernel(diag_ref, inverse_ref, work_ref):
    for p in range(PANELS):
        rows = slice(p * TILE, (p + 1) * TILE)
        work_ref[rows, :] = diag_ref[:, p].reshape(TILE, WIDTH)
    at_row = lax.broadcasted_iota(jnp.int32, (WIDTH, WIDTH), 0)
    at_col = lax.broadcasted_iota(jnp.int32, (WIDTH, WIDTH), 1)
    inverse_ref[...] = jnp.where(at_row == at_col, 1.0, 0.0).astype(jnp.float32)
    for start in range(0, WIDTH, STRIP):
        stop = start + STRIP
        first = start // TILE * TILE
        upper = WIDTH - first
        done = first + TILE
        strip = jnp.concatenate(
            [work_ref[start:stop, first:], inverse_ref[start:stop, :done]], axis=1
        )
        strip = eliminate(strip, start - first)
        inverse_ref[start:stop, :done] = strip[:, upper:]
        if stop < WIDTH:
            update = product(strip[:, :upper], strip, ((0,), (0,)))[stop - first :]
            work_ref[stop:, first:] = work_ref[stop:, first:] - update[:, :upper]
            inverse_ref[stop:, :done] = inverse_ref[stop:, :done] - update[:, upper:]


def inverse_factor(diag):
    return pl.pallas_call(
        inverse_factor_kernel,
        grid=(1,),
        out_shape=jax.ShapeDtypeStruct((WIDTH, WIDTH), jnp.float32),
        in_specs=[pl.BlockSpec((TILE // GROUP, *diag.shape[1:]), lambda _: (0, 0, 0, 0))],
        out_specs=pl.BlockSpec((WIDTH, WIDTH), lambda _: (0, 0)),
        scratch_shapes=[pltpu.VMEM((WIDTH, WIDTH), jnp.float32)],
        cost_estimate=pl.CostEstimate(
            flops=4 * WIDTH**3, bytes_accessed=12 * WIDTH**2, transcendentals=0
        ),
        name="inverse_factor",
    )(diag)


def solve_rows_kernel(rows_ref, inverse_ref, lower_ref):
    raw = jnp.concatenate(
        [
            jnp.concatenate([rows_ref[:, p, g].reshape(-1, TILE) for p in range(PANELS)], axis=1)
            for g in range(rows_ref.shape[2])
        ],
        axis=0,
    )
    lower_ref[...] = product(raw, inverse_ref[...], ((1,), (1,)))


def solve_rows(rows, inverse):
    count = rows.shape[0] * rows.shape[2] * GROUP
    return pl.pallas_call(
        solve_rows_kernel,
        out_shape=jax.ShapeDtypeStruct((count, WIDTH), jnp.float32),
        cost_estimate=pl.CostEstimate(
            flops=12 * count * WIDTH**2, bytes_accessed=8 * count * WIDTH, transcendentals=0
        ),
        name="solve_rows",
    )(rows, inverse)


def trailing_kernel(place_ref, matrix_ref, lower_ref, cols_ref, inverse_ref, out_ref, solved_ref):
    step = pl.program_id(0)
    grid_rows, grid_cols, row_index, col_index = (place_ref[k] for k in range(4))
    rows_here, cols_count = matrix_ref.shape

    @pl.when(step == 0)
    def _():
        cols = jnp.concatenate(
            [cols_ref[:, p].reshape(TILE, cols_count) for p in range(PANELS)], axis=0
        )
        high, low = split(product(inverse_ref[...], cols, ((1,), (0,))))
        solved_ref[0 * WIDTH : 1 * WIDTH, :] = high
        solved_ref[1 * WIDTH : 2 * WIDTH, :] = low
        solved_ref[2 * WIDTH : 3 * WIDTH, :] = high

    high, low = split(lower_ref[...])
    update = jnp.dot(
        jnp.concatenate([high, high, low], axis=1),
        solved_ref[...],
        preferred_element_type=jnp.float32,
    )
    at_row = lax.broadcasted_iota(jnp.int32, (TILE, TILE), 0)
    at_col = lax.broadcasted_iota(jnp.int32, (TILE, TILE), 1)
    for t in range(rows_here // TILE):
        tile_row = (step * (rows_here // TILE) + t) * grid_rows + row_index
        down = slice(t * TILE, (t + 1) * TILE)
        for b in range(cols_count // TILE):
            across = slice(b * TILE, (b + 1) * TILE)
            tile_col = b * grid_cols + col_index
            value = matrix_ref[down, across] - update[down, across]
            for p in range(PANELS):
                panel = lower_ref[down, p * TILE : (p + 1) * TILE]
                value = jnp.where(tile_col == p, panel, value)
            keep = (tile_row - tile_col) * TILE + at_row - at_col >= 0
            keep = keep | ((tile_row == tile_col) & (tile_col >= PANELS))
            out_ref[down, across] = jnp.where(keep, value, 0.0)


def trailing(place, matrix, lower, cols, inverse):
    rows_count, cols_count = matrix.shape
    rows_step = 2 * TILE
    return pl.pallas_call(
        trailing_kernel,
        grid=(rows_count // rows_step,),
        out_shape=jax.ShapeDtypeStruct(matrix.shape, jnp.float32),
        in_specs=[
            pl.BlockSpec(memory_space=pltpu.SMEM),
            pl.BlockSpec((rows_step, cols_count), lambda t: (t, 0)),
            pl.BlockSpec((rows_step, WIDTH), lambda t: (t, 0)),
            pl.BlockSpec(cols.shape, lambda t: (0, 0, 0, 0)),
            pl.BlockSpec(inverse.shape, lambda t: (0, 0)),
        ],
        out_specs=pl.BlockSpec((rows_step, cols_count), lambda t: (t, 0)),
        scratch_shapes=[pltpu.VMEM((3 * WIDTH, cols_count), jnp.bfloat16)],
        name="trailing",
    )(place, matrix, lower, cols, inverse)


def exchange(chunks, axis):
    return lax.all_to_all(chunks, axis, 0, 0, tiled=True)


def to_all(part, axis):
    count = lax.axis_size(axis)
    return exchange(jnp.broadcast_to(part[None], (count, *part.shape)), axis)


def on_device(matrix):
    rows_count, cols_count = matrix.shape
    grid_rows = lax.axis_size("row")
    grid_cols = lax.axis_size("col")
    groups = rows_count // (grid_cols * GROUP)
    with jax.named_scope("scatter_rows"):
        panel = matrix[:, :TILE].reshape(groups, grid_cols, GROUP, TILE).transpose(1, 0, 2, 3)
        row_part = exchange(panel, "col")[:PANELS]
    with jax.named_scope("gather_rows"):
        rows = lax.all_gather(row_part, "col")
    with jax.named_scope("scatter_cols"):
        own_diag = row_part[:, 0].transpose(1, 0, 2).reshape(1, GROUP, PANELS * TILE)
        to_rows = jnp.concatenate(
            [
                matrix[:TILE].reshape(grid_rows, GROUP, cols_count),
                jnp.broadcast_to(own_diag, (grid_rows, *own_diag.shape[1:])),
            ],
            axis=2,
        )
        from_rows = exchange(to_rows, "row")[:PANELS]
        col_part = from_rows[:, :, :cols_count]
        diag_part = from_rows[:, :, cols_count:]
    with jax.named_scope("spread_diagonal"):
        diag = to_all(diag_part, "col")
    with jax.named_scope("gather_cols"):
        diag, col_part = lax.optimization_barrier((diag, col_part))
        cols = to_all(col_part, "row")
    inverse = inverse_factor(diag)
    lower = solve_rows(rows, inverse)
    place = jnp.stack(
        [jnp.int32(grid_rows), jnp.int32(grid_cols), lax.axis_index("row"), lax.axis_index("col")]
    ).astype(jnp.int32)
    return trailing(place, matrix, lower, cols, inverse)


def solution(mesh):
    return jax.shard_map(
        on_device, mesh=mesh, in_specs=(P("row", "col"),), out_specs=P("row", "col"), check_vma=False
    )
```

time: 161 us -> 148 us (0.919); the launches traced: 158 us -> 147 us
  waiting for transfers between devices: 53.4 us -> 23.8 us
  starting transfers between devices: 37.9 us -> 24.3 us
  between operations: 0.09 us -> 13.5 us
  blocking collectives: 21.3 us -> 33 us
  Pallas kernels: 37.7 us -> 45.5 us
    all_to_all x5 -> x3, waiting for transfers between devices: 53.4 us -> 21.6 us  [exchange(): return lax.all_to_all(chunks, axis, 0, 0, tiled=True)]
    all_to_all x5 -> x3, starting transfers between devices: 37.9 us -> 24.3 us  [exchange(): return lax.all_to_all(chunks, axis, 0, 0, tiled=True)]
    all_to_all x1, blocking collectives: 21.3 us -> 33 us  [exchange(): return lax.all_to_all(chunks, axis, 0, 0, tiled=True)]
    pallas_call x2 -> x3, Pallas kernels: 37.7 us -> 45.5 us  [the longest x1 36.6 us: inverse_factor(): pl.pallas_call(inverse_factor_kernel, grid=(1,), out_shape=jax.ShapeDtype...]
    all_gather x0 -> x1, waiting for transfers between devices: none -> 2.11 us  [on_device(): rows = lax.all_gather(row_part, 'col')]
    broadcast_in_dim x5 -> x2, local copies, waits for them, and re-layouts: 3.61 us -> 1.81 us  [to_all(): return exchange(jnp.broadcast_to(part[None], (count, *part.shape)), axis)]
  transfers between devices with their start and end apart: 5 -> 4, of which waited for: 4 -> 3; matrix products, arithmetic and copies ran while one was open for 1% -> 2% of each run, Pallas kernels for 16% -> 27%
where the time goes in v2:
time: 148 us; the launch traced here: 147 us
  Pallas kernels  45.5 us (31%)
  blocking collectives  33 us (22%)
  starting transfers between devices  24.3 us (16%)
  waiting for transfers between devices  23.8 us (16%)
  between operations  13.5 us (9%)
  local copies, waits for them, and re-layouts  6.15 us (4%)
    pallas_call x1, Pallas kernels, inverse_factor(): pl.pallas_call(inverse_factor_kernel, grid=(1,), out_shape=jax.ShapeDtype...  36.6 us
    all_to_all x1, blocking collectives, exchange(): return lax.all_to_all(chunks, axis, 0, 0, tiled=True)  33 us
    all_to_all x3, starting transfers between devices, exchange(): return lax.all_to_all(chunks, axis, 0, 0, tiled=True)  24.3 us
    all_to_all x3, waiting for transfers between devices, exchange(): return lax.all_to_all(chunks, axis, 0, 0, tiled=True)  21.6 us
    pallas_call x1, Pallas kernels, trailing(): pl.pallas_call(trailing_kernel, grid=(rows_count // rows_step,), out_shap...  5.63 us
    pallas_call x1, Pallas kernels, solve_rows(): pl.pallas_call(solve_rows_kernel, out_shape=jax.ShapeDtypeStruct((count,...  3.3 us
  transfers between devices with their start and end apart: 4, of which 3 were waited for; matrix products, arithmetic and copies ran while one was open for 2% of the time, Pallas kernels for 27%

profile of v2, /device:TPU:1, one launch (start us, length us, event | category | flops | bytes accessed | tf_op | source)
XLA Modules:
  0.0 147.0 jit_solution(7941883263500135951)
XLA Ops:
  6.5 1.1 slice.22
  7.6 0.9 copy.4
  8.5 10.4 %all-to-all-start = ((f32[32,4,8,128]{3,2,1,0:T(8,128)}), f32[32,4,8,128]{3,2,1,0:T(8,128)S(1)}, u32[]{:S(2)}, u32[]{:S(2)}) async-start(f32[32,4,8,128]{3,2,1,0:T(8,128)} %copy.4), calls=%async_computation | async-start | bytes 1048576 | tf_op jit(solution)/shard_map/scatter_rows/all_to_all | solution.py:175
  18.9 1.0 slice_bitcast_fusion
  19.9 10.8 %all-to-all-done = f32[32,4,8,128]{3,2,1,0:T(8,128)S(1)} async-done(((f32[32,4,8,128]{3,2,1,0:T(8,128)}), f32[32,4,8,128]{3,2,1,0:T(8,128)S(1)}, u32[]{:S(2)}, u32[]{:S(2)}) %all-to-all-start) | async-done | bytes 524320 | tf_op jit(solution)/shard_map/scatter_rows/all_to_all | solution.py:175
  30.7 33.0 %all_to_all.20 = f32[16,8,768]{2,1,0:T(8,128)S(1)} all-to-all(f32[16,8,768]{2,1,0:T(8,128)S(1)} %pad_maximum_fusion), channel_id=1, replica_groups=mesh['row'=16,'col'=32] {'row'}, dimensions={0} | all-to-all | bytes 786432 | tf_op jit(solution)/shard_map/scatter_cols/all_to_all | solution.py:175
  63.7 0.9 broadcast_in_dim.10
  64.6 8.8 %all-to-all-start.2 = ((f32[32,2,8,256]{3,2,1,0:T(8,128)}), f32[32,2,8,256]{3,2,1,0:T(8,128)S(1)}, u32[]{:S(2)}, u32[]{:S(2)}) async-start(f32[32,2,8,256]{3,2,1,0:T(8,128)} %broadcast_in_dim.10), calls=%async_computation.2 | async-start | bytes 1048576 | tf_op jit(solution)/shard_map/spread_diagonal/all_to_all | solution.py:175
  73.4 0.0 all-gather.3.cloned.1.call-start
  73.5 0.6 slice.28
  74.1 0.1 all-gather.3.cloned.1.call-update
  74.2 10.9 %all-to-all-done.2.diag_ref = f32[32,2,8,256]{3,2,1,0:T(8,128)S(1)} async-done(((f32[32,2,8,256]{3,2,1,0:T(8,128)}), f32[32,2,8,256]{3,2,1,0:T(8,128)S(1)}, u32[]{:S(2)}, u32[]{:S(2)}) %all-to-all-start.2) | async-done | bytes 524320 | tf_op jit(solution)/shard_map/spread_diagonal/all_to_all | solution.py:175
  85.0 0.0 copy-start.1
  85.0 1.0 broadcast_in_dim.22
  86.0 5.0 %all-to-all-start.3 = ((f32[16,2,8,512]{3,2,1,0:T(8,128)}), f32[16,2,8,512]{3,2,1,0:T(8,128)S(1)}, u32[]{:S(2)}, u32[]{:S(2)}) async-start(f32[16,2,8,512]{3,2,1,0:T(8,128)} %broadcast_in_dim.22), calls=%async_computation.3 | async-start | bytes 1048576 | tf_op jit(solution)/shard_map/gather_cols/all_to_all | solution.py:175
  91.0 0.7 pad_add_fusion.place_ref
  91.7 0.0 copy-done.1
  91.7 36.6 %inverse_factor.1.inverse_ref = f32[256,256]{1,0:T(8,128)} custom-call(f32[32,2,8,256]{3,2,1,0:T(8,128)} %copy-done.1), custom_call_target="tpu_custom_call" | custom-call | flops 67108864 | bytes 786432 | tf_op jit(solution)/shard_map/inverse_factor/pallas_call | solution.py:79
  128.3 2.1 %all-gather.3.cloned.1.call-done = f32[64,4,8,128]{3,2,1,0:T(8,128)} async-done(((f32[2,4,8,128]{3,2,1,0:T(8,128)}), f32[64,4,8,128]{3,2,1,0:T(8,128)}) %all-gather.3.cloned.1.call-update) | async-done | bytes 1048592 | tf_op jit(solution)/shard_map/gather_rows/all_gather | solution.py:192
  130.4 3.3 %solve_rows.1.lower_ref = f32[1024,256]{1,0:T(8,128)} custom-call(f32[32,2,4,8,128]{4,3,2,1,0:T(8,128)} %bitcast.15, f32[256,256]{1,0:T(8,128)} %inverse_factor.1.inverse_ref), custom_call_target="tpu_custom_call" | custom-call | flops 805306368 | bytes 2097152 | tf_op jit(solution)/shard_map/solve_rows/pallas_call | solution.py:106
  133.7 0.0 all-to-all-done.3.cols_ref
  133.7 0.0 copy-start
  133.7 0.8 copy-done
  134.5 5.6 %trailing.1 = f32[1024,512]{1,0:T(8,128)} custom-call(s32[4]{0:T(128)} %pad_add_fusion.place_ref, f32[1024,512]{1,0:T(8,128)} %matrix_ref.1, f32[1024,256]{1,0:T(8,128)} %solve_rows.1.lower_ref, f32[16,2,8,512]{3,2,1,0:T(8,128)} %copy-done, f32[256,256]{1,0:T(8,128)} %inverse_factor.1.inverse_ref), custom_call_target="tpu_custom_call" | custom-call | tf_op jit(solution)/shard_map/trailing/pallas_call | solution.py:157
  (5 shorter events, 0.0 us)
Async XLA Ops:
  8.5 22.2 %all-to-all-start = ((f32[32,4,8,128]{3,2,1,0:T(8,128)}), f32[32,4,8,128]{3,2,1,0:T(8,128)S(1)}, u32[]{:S(2)}, u32[]{:S(2)}) async-start(f32[32,4,8,128]{3,2,1,0:T(8,128)} %copy.4), calls=%async_computation | async-start | bytes 1048576 | tf_op jit(solution)/shard_map/scatter_rows/all_to_all | solution.py:175
  64.6 20.5 %all-to-all-start.2 = ((f32[32,2,8,256]{3,2,1,0:T(8,128)}), f32[32,2,8,256]{3,2,1,0:T(8,128)S(1)}, u32[]{:S(2)}, u32[]{:S(2)}) async-start(f32[32,2,8,256]{3,2,1,0:T(8,128)} %broadcast_in_dim.10), calls=%async_computation.2 | async-start | bytes 1048576 | tf_op jit(solution)/shard_map/spread_diagonal/all_to_all | solution.py:175
  73.4 57.0 %all-gather.3.cloned.1.call-start = ((), (), s32[]{:S(2)}) async-start(), calls=%async_computation.4 | async-start | bytes 1081344 | tf_op jit(solution)/shard_map/gather_rows/all_gather | solution.py:192
  85.0 6.7 %copy-start.1 = (f32[32,2,8,256]{3,2,1,0:T(8,128)}, f32[32,2,8,256]{3,2,1,0:T(8,128)S(1)}, u32[]{:S(2)}) copy-start(f32[32,2,8,256]{3,2,1,0:T(8,128)S(1)} %all-to-all-done.2.diag_ref) | copy-start | bytes 1572868
  86.0 47.7 %all-to-all-start.3 = ((f32[16,2,8,512]{3,2,1,0:T(8,128)}), f32[16,2,8,512]{3,2,1,0:T(8,128)S(1)}, u32[]{:S(2)}, u32[]{:S(2)}) async-start(f32[16,2,8,512]{3,2,1,0:T(8,128)} %broadcast_in_dim.22), calls=%async_computation.3 | async-start | bytes 1048576 | tf_op jit(solution)/shard_map/gather_cols/all_to_all | solution.py:175
  133.7 0.8 copy-start
Sparse Core Ops, SparseCore 0:
  77.4 52.9 all-gather.2

commit v3 on v2

--- a/solution.py
+++ b/solution.py
@@ -8,7 +8,7 @@
 TILE = 128
 PANELS = 2
 WIDTH = TILE * PANELS
-STRIP = 64
+STRIP = 32
 GROUP = 8
 HIGHEST = lax.Precision.HIGHEST
 
@@ -25,37 +25,30 @@
 
 
 def eliminate(strip, pivot_lane):
-    count, width = strip.shape
-    tiles = [
-        [strip[t * GROUP : (t + 1) * GROUP, v * TILE : (v + 1) * TILE] for v in range(width // TILE)]
-        for t in range(count // GROUP)
-    ]
-    shape = (GROUP, TILE)
-    sub_row = lax.broadcasted_iota(jnp.int32, shape, 0)
-    pivots = [jnp.ones(shape, jnp.float32) for _ in tiles]
-    for i in range(count):
-        block, lane = divmod(pivot_lane + i, TILE)
+    tiles = [strip[t * GROUP : (t + 1) * GROUP] for t in range(STRIP // GROUP)]
+    sub_row = lax.broadcasted_iota(jnp.int32, (GROUP, 1), 0)
+    scales = [jnp.ones((GROUP, 1), jnp.float32) for _ in tiles]
+    for i in range(STRIP):
+        lane = pivot_lane + i
         own, sub = divmod(i, GROUP)
-        below = range(own, count // GROUP)
-        columns = [jnp.broadcast_to(tiles[t][block][:, lane : lane + 1], shape) for t in below]
-        pivot = jnp.broadcast_to(columns[0][sub : sub + 1], shape)
-        pivots[own] = jnp.where(sub_row == sub, pivot, pivots[own])
+        row = tiles[own][sub : sub + 1, :]
+        pivot = tiles[own][sub : sub + 1, lane : lane + 1]
         inverse = 1.0 / pivot
-        rows = [jnp.broadcast_to(part[sub : sub + 1], shape) * inverse for part in tiles[own]]
-        columns[0] = jnp.where(sub_row > sub, columns[0], 0.0)
-        for t, column in zip(below, columns):
-            tiles[t] = [part - column * row for part, row in zip(tiles[t], rows)]
-    scaled = []
-    for parts, pivot in zip(tiles, pivots):
-        scale = lax.rsqrt(pivot)
-        scaled.append(jnp.concatenate([part * scale for part in parts], axis=1))
-    return jnp.concatenate(scaled, axis=0)
+        scales[own] = jnp.where(sub_row == sub, lax.rsqrt(pivot), scales[own])
+        for t in range(own, STRIP // GROUP):
+            factor = tiles[t][:, lane : lane + 1] * inverse
+            if t == own:
+                factor = jnp.where(sub_row > sub, factor, 0.0)
+            tiles[t] = tiles[t] - factor * row
+    return jnp.concatenate([tile * scale for tile, scale in zip(tiles, scales)], axis=0)
 
 
 def inverse_factor_kernel(diag_ref, inverse_ref, work_ref):
+    half = diag_ref.shape[0] // PANELS
     for p in range(PANELS):
-        rows = slice(p * TILE, (p + 1) * TILE)
-        work_ref[rows, :] = diag_ref[:, p].reshape(TILE, WIDTH)
+        for q in range(PANELS):
+            part = diag_ref[q * half : (q + 1) * half, 0, p].reshape(TILE, TILE)
+            work_ref[p * TILE : (p + 1) * TILE, q * TILE : (q + 1) * TILE] = part
     at_row = lax.broadcasted_iota(jnp.int32, (WIDTH, WIDTH), 0)
     at_col = lax.broadcasted_iota(jnp.int32, (WIDTH, WIDTH), 1)
     inverse_ref[...] = jnp.where(at_row == at_col, 1.0, 0.0).astype(jnp.float32)
@@ -80,7 +73,7 @@
         inverse_factor_kernel,
         grid=(1,),
         out_shape=jax.ShapeDtypeStruct((WIDTH, WIDTH), jnp.float32),
-        in_specs=[pl.BlockSpec((TILE // GROUP, *diag.shape[1:]), lambda _: (0, 0, 0, 0))],
+        in_specs=[pl.BlockSpec((diag.shape[0], 1, *diag.shape[2:]), lambda _: (0, 0, 0, 0, 0))],
         out_specs=pl.BlockSpec((WIDTH, WIDTH), lambda _: (0, 0)),
         scratch_shapes=[pltpu.VMEM((WIDTH, WIDTH), jnp.float32)],
         cost_estimate=pl.CostEstimate(
@@ -90,19 +83,23 @@
     )(diag)
 
 
-def solve_rows_kernel(rows_ref, inverse_ref, lower_ref):
-    raw = jnp.concatenate(
-        [
-            jnp.concatenate([rows_ref[:, p, g].reshape(-1, TILE) for p in range(PANELS)], axis=1)
-            for g in range(rows_ref.shape[2])
-        ],
-        axis=0,
-    )
-    lower_ref[...] = product(raw, inverse_ref[...], ((1,), (1,)))
-
-
-def solve_rows(rows, inverse):
-    count = rows.shape[0] * rows.shape[2] * GROUP
+def solve_rows_kernel(first_ref, rest_ref, inverse_ref, lower_ref):
+    half = first_ref.shape[0] // PANELS
+    raw = []
+    for t in range(lower_ref.shape[0] // TILE):
+        group, tile = divmod(t, PANELS)
+        parts = []
+        for p in range(PANELS):
+            side = (tile + p) % PANELS
+            held = slice(side * half, (side + 1) * half)
+            part = first_ref[held, 1, p] if group == 0 else rest_ref[held, p, group - 1]
+            parts.append(part.reshape(TILE, TILE))
+        raw.append(jnp.concatenate(parts, axis=1))
+    lower_ref[...] = product(jnp.concatenate(raw, axis=0), inverse_ref[...], ((1,), (1,)))
+
+
+def solve_rows(first, rest, inverse):
+    count = rest.shape[0] * (rest.shape[2] + 1) * GROUP
     return pl.pallas_call(
         solve_rows_kernel,
         out_shape=jax.ShapeDtypeStruct((count, WIDTH), jnp.float32),
@@ -110,7 +107,7 @@
             flops=12 * count * WIDTH**2, bytes_accessed=8 * count * WIDTH, transcendentals=0
         ),
         name="solve_rows",
-    )(rows, inverse)
+    )(first, rest, inverse)
 
 
 def trailing_kernel(place_ref, matrix_ref, lower_ref, cols_ref, inverse_ref, out_ref, solved_ref):
@@ -184,33 +181,38 @@
     rows_count, cols_count = matrix.shape
     grid_rows = lax.axis_size("row")
     grid_cols = lax.axis_size("col")
+    col_index = lax.axis_index("col")
+    half = grid_cols // PANELS
     groups = rows_count // (grid_cols * GROUP)
     with jax.named_scope("scatter_rows"):
-        panel = matrix[:, :TILE].reshape(groups, grid_cols, GROUP, TILE).transpose(1, 0, 2, 3)
+        panel = matrix[:, :TILE].reshape(groups, PANELS, half, GROUP, TILE)
+        panel = jnp.where(col_index == 1, panel[:, ::-1], panel)
+        panel = panel.transpose(1, 2, 0, 3, 4).reshape(grid_cols, groups, GROUP, TILE)
         row_part = exchange(panel, "col")[:PANELS]
-    with jax.named_scope("gather_rows"):
-        rows = lax.all_gather(row_part, "col")
     with jax.named_scope("scatter_cols"):
-        own_diag = row_part[:, 0].transpose(1, 0, 2).reshape(1, GROUP, PANELS * TILE)
+        own_diag = jnp.where(col_index < half, row_part[0, 0], row_part[1, 0])
         to_rows = jnp.concatenate(
             [
                 matrix[:TILE].reshape(grid_rows, GROUP, cols_count),
-                jnp.broadcast_to(own_diag, (grid_rows, *own_diag.shape[1:])),
+                jnp.broadcast_to(own_diag[None], (grid_rows, GROUP, TILE)),
             ],
             axis=2,
         )
         from_rows = exchange(to_rows, "row")[:PANELS]
         col_part = from_rows[:, :, :cols_count]
         diag_part = from_rows[:, :, cols_count:]
+    with jax.named_scope("gather_rows"):
+        rest = lax.all_gather(row_part[:, 1:], "col")
     with jax.named_scope("spread_diagonal"):
-        diag = to_all(diag_part, "col")
+        diag_part, rest = lax.optimization_barrier((diag_part, rest))
+        first = to_all(jnp.stack([diag_part, row_part[:, 0]]), "col")
     with jax.named_scope("gather_cols"):
-        diag, col_part = lax.optimization_barrier((diag, col_part))
+        first, col_part = lax.optimization_barrier((first, col_part))
         cols = to_all(col_part, "row")
-    inverse = inverse_factor(diag)
-    lower = solve_rows(rows, inverse)
+    inverse = inverse_factor(first)
+    lower = solve_rows(first, rest, inverse)
     place = jnp.stack(
-        [jnp.int32(grid_rows), jnp.int32(grid_cols), lax.axis_index("row"), lax.axis_index("col")]
+        [jnp.int32(grid_rows), jnp.int32(grid_cols), lax.axis_index("row"), col_index]
     ).astype(jnp.int32)
     return trailing(place, matrix, lower, cols, inverse)
 

time: 148 us -> 130 us (0.88)
  starting transfers between devices: 24.3 us -> 39.6 us
  between operations: 13.5 us -> 0.11 us
  Pallas kernels: 45.5 us -> 34.9 us
  blocking collectives: 33 us -> 25.5 us
  other arithmetic: 0.7 us -> 2.27 us
    all_to_all x1 -> x0, blocking collectives: 33 us -> none  [exchange(): return lax.all_to_all(chunks, axis, 0, 0, tiled=True)]
    all_gather x0 -> x1, blocking collectives: none -> 25.5 us  [on_device(): rest = lax.all_gather(row_part[:, 1:], 'col')]
    all_to_all x3 -> x4, starting transfers between devices: 24.3 us -> 39.6 us  [exchange(): return lax.all_to_all(chunks, axis, 0, 0, tiled=True)]
    pallas_call x1, Pallas kernels: 36.6 us -> 25.9 us  [inverse_factor(): pl.pallas_call(inverse_factor_kernel, grid=(1,), out_shape=jax.ShapeDtype...]
    all_gather x1 -> x0, waiting for transfers between devices: 2.11 us -> none  [on_device(): rows = lax.all_gather(row_part, 'col')]
    all_to_all x3 -> x4, waiting for transfers between devices: 21.6 us -> 22.4 us  [exchange(): return lax.all_to_all(chunks, axis, 0, 0, tiled=True)]
  transfers between devices with their start and end apart: 4 -> 4, of which waited for: 3 -> 2; matrix products, arithmetic and copies ran while one was open for 2% -> 1% of each run, Pallas kernels for 27% -> 23%
where the time goes in v3:
time: 130 us
  starting transfers between devices  39.6 us (30%)
  Pallas kernels  34.9 us (27%)
  blocking collectives  25.5 us (20%)
  waiting for transfers between devices  22.4 us (17%)
  local copies, waits for them, and re-layouts  4.76 us (4%)
  other arithmetic  2.27 us (2%)
    all_to_all x4, starting transfers between devices, exchange(): return lax.all_to_all(chunks, axis, 0, 0, tiled=True)  39.6 us
    pallas_call x1, Pallas kernels, inverse_factor(): pl.pallas_call(inverse_factor_kernel, grid=(1,), out_shape=jax.ShapeDtype...  25.9 us
    all_gather x1, blocking collectives, on_device(): rest = lax.all_gather(row_part[:, 1:], 'col')  25.5 us
    all_to_all x4, waiting for transfers between devices, exchange(): return lax.all_to_all(chunks, axis, 0, 0, tiled=True)  22.4 us
    pallas_call x1, Pallas kernels, trailing(): pl.pallas_call(trailing_kernel, grid=(rows_count // rows_step,), out_shap...  5.63 us
    pallas_call x1, Pallas kernels, solve_rows(): pl.pallas_call(solve_rows_kernel, out_shape=jax.ShapeDtypeStruct((count,...  3.35 us
  transfers between devices with their start and end apart: 4, of which 2 were waited for; matrix products, arithmetic and copies ran while one was open for 1% of the time, Pallas kernels for 23%

profile of v3, /device:TPU:1, one launch (start us, length us, event | category | flops | bytes accessed | tf_op | source)
XLA Modules:
  0.0 129.5 jit_solution(9766940428722066629)
XLA Ops:
  0.0 1.1 slice.33
  1.1 0.1 copy.5
  1.1 0.8 reverse_select_fusion
  2.0 10.4 %all-to-all-start = ((f32[32,4,8,128]{3,2,1,0:T(8,128)}), f32[32,4,8,128]{3,2,1,0:T(8,128)S(1)}, u32[]{:S(2)}, u32[]{:S(2)}) async-start(f32[32,4,8,128]{3,2,1,0:T(8,128)} %bitcast.5), calls=%async_computation | async-start | bytes 1048576 | tf_op jit(solution)/shard_map/scatter_rows/all_to_all | solution.py:172
  12.4 1.0 slice_bitcast_fusion
  13.4 10.8 %all-to-all-done = f32[32,4,8,128]{3,2,1,0:T(8,128)S(1)} async-done(((f32[32,4,8,128]{3,2,1,0:T(8,128)}), f32[32,4,8,128]{3,2,1,0:T(8,128)S(1)}, u32[]{:S(2)}, u32[]{:S(2)}) %all-to-all-start) | async-done | bytes 524320 | tf_op jit(solution)/shard_map/scatter_rows/all_to_all | solution.py:172
  24.2 0.8 pad_maximum_fusion
  24.9 13.0 %all-to-all-start.1 = ((f32[16,8,640]{2,1,0:T(8,128)}), f32[16,8,640]{2,1,0:T(8,128)S(1)}, u32[]{:S(2)}, u32[]{:S(2)}) async-start(f32[16,8,640]{2,1,0:T(8,128)} %pad_maximum_fusion), calls=%async_computation.1 | async-start | bytes 655360 | tf_op jit(solution)/shard_map/scatter_cols/all_to_all | solution.py:172
  37.9 25.5 %all-gather = f32[64,3,8,128]{3,2,1,0:T(8,128)} all-gather(f32[2,3,8,128]{3,2,1,0:T(8,128)S(1)} %slice.43), channel_id=2, replica_groups=mesh['row'=16,'col'=32] {'col'}, dimensions={0}, use_global_device_ids=true | all-gather | bytes 811008 | tf_op jit(solution)/shard_map/gather_rows/all_gather | solution.py:205
  63.4 0.0 all-to-all-done.1
  63.4 0.9 broadcast_in_dim.7
  64.3 4.5 %all-to-all-start.2 = ((f32[32,2,2,8,128]{4,3,2,1,0:T(8,128)}), f32[32,2,2,8,128]{4,3,2,1,0:T(8,128)S(1)}, u32[]{:S(2)}, u32[]{:S(2)}) async-start(f32[32,2,2,8,128]{4,3,2,1,0:T(8,128)} %broadcast_in_dim.7), calls=%async_computation.2 | async-start | bytes 1048576 | tf_op jit(solution)/shard_map/spread_diagonal/all_to_all | solution.py:172
  68.8 11.6 %all-to-all-done.2.diag_ref.first_ref = f32[32,2,2,8,128]{4,3,2,1,0:T(8,128)S(1)} async-done(((f32[32,2,2,8,128]{4,3,2,1,0:T(8,128)}), f32[32,2,2,8,128]{4,3,2,1,0:T(8,128)S(1)}, u32[]{:S(2)}, u32[]{:S(2)}) %all-to-all-start.2) | async-done | bytes 524320 | tf_op jit(solution)/shard_map/spread_diagonal/all_to_all | solution.py:172
  80.4 0.0 copy-start.1
  80.4 1.0 broadcast_in_dim.8
  81.3 11.8 %all-to-all-start.3 = ((f32[16,2,8,512]{3,2,1,0:T(8,128)}), f32[16,2,8,512]{3,2,1,0:T(8,128)S(1)}, u32[]{:S(2)}, u32[]{:S(2)}) async-start(f32[16,2,8,512]{3,2,1,0:T(8,128)} %broadcast_in_dim.8), calls=%async_computation.3 | async-start | bytes 1048576 | tf_op jit(solution)/shard_map/gather_cols/all_to_all | solution.py:172
  93.1 0.7 pad_add_fusion.place_ref
  93.8 0.0 copy-done.1
  93.8 25.9 %inverse_factor.1.inverse_ref = f32[256,256]{1,0:T(8,128)} custom-call(f32[32,2,2,8,128]{4,3,2,1,0:T(8,128)} %copy-done.1), custom_call_target="tpu_custom_call" | custom-call | flops 67108864 | bytes 786432 | tf_op jit(solution)/shard_map/inverse_factor/pallas_call | solution.py:72
  119.7 3.4 %solve_rows.1.lower_ref = f32[1024,256]{1,0:T(8,128)} custom-call(f32[32,2,2,8,128]{4,3,2,1,0:T(8,128)} %copy-done.1, f32[32,2,3,8,128]{4,3,2,1,0:T(8,128)} %bitcast.15, f32[256,256]{1,0:T(8,128)} %inverse_factor.1.inverse_ref), custom_call_target="tpu_custom_call" | custom-call | flops 805306368 | bytes 2097152 | tf_op jit(solution)/shard_map/solve_rows/pallas_call | solution.py:103
  123.1 0.0 all-to-all-done.3.cols_ref
  123.1 0.0 copy-start
  123.1 0.8 copy-done
  123.9 5.6 %trailing.1 = f32[1024,512]{1,0:T(8,128)} custom-call(s32[4]{0:T(128)} %pad_add_fusion.place_ref, f32[1024,512]{1,0:T(8,128)} %matrix_ref.1, f32[1024,256]{1,0:T(8,128)} %solve_rows.1.lower_ref, f32[16,2,8,512]{3,2,1,0:T(8,128)} %copy-done, f32[256,256]{1,0:T(8,128)} %inverse_factor.1.inverse_ref), custom_call_target="tpu_custom_call" | custom-call | tf_op jit(solution)/shard_map/trailing/pallas_call | solution.py:154
  (7 shorter events, 0.0 us)
Async XLA Ops:
  2.0 22.2 %all-to-all-start = ((f32[32,4,8,128]{3,2,1,0:T(8,128)}), f32[32,4,8,128]{3,2,1,0:T(8,128)S(1)}, u32[]{:S(2)}, u32[]{:S(2)}) async-start(f32[32,4,8,128]{3,2,1,0:T(8,128)} %bitcast.5), calls=%async_computation | async-start | bytes 1048576 | tf_op jit(solution)/shard_map/scatter_rows/all_to_all | solution.py:172
  24.9 38.5 %all-to-all-start.1 = ((f32[16,8,640]{2,1,0:T(8,128)}), f32[16,8,640]{2,1,0:T(8,128)S(1)}, u32[]{:S(2)}, u32[]{:S(2)}) async-start(f32[16,8,640]{2,1,0:T(8,128)} %pad_maximum_fusion), calls=%async_computation.1 | async-start | bytes 655360 | tf_op jit(solution)/shard_map/scatter_cols/all_to_all | solution.py:172
  64.3 16.1 %all-to-all-start.2 = ((f32[32,2,2,8,128]{4,3,2,1,0:T(8,128)}), f32[32,2,2,8,128]{4,3,2,1,0:T(8,128)S(1)}, u32[]{:S(2)}, u32[]{:S(2)}) async-start(f32[32,2,2,8,128]{4,3,2,1,0:T(8,128)} %broadcast_in_dim.7), calls=%async_computation.2 | async-start | bytes 1048576 | tf_op jit(solution)/shard_map/spread_diagonal/all_to_all | solution.py:172
  80.4 13.4 %copy-start.1 = (f32[32,2,2,8,128]{4,3,2,1,0:T(8,128)}, f32[32,2,2,8,128]{4,3,2,1,0:T(8,128)S(1)}, u32[]{:S(2)}) copy-start(f32[32,2,2,8,128]{4,3,2,1,0:T(8,128)S(1)} %all-to-all-done.2.diag_ref.first_ref) | copy-start | bytes 1572868
  81.3 41.7 %all-to-all-start.3 = ((f32[16,2,8,512]{3,2,1,0:T(8,128)}), f32[16,2,8,512]{3,2,1,0:T(8,128)S(1)}, u32[]{:S(2)}, u32[]{:S(2)}) async-start(f32[16,2,8,512]{3,2,1,0:T(8,128)} %broadcast_in_dim.8), calls=%async_computation.3 | async-start | bytes 1048576 | tf_op jit(solution)/shard_map/gather_cols/all_to_all | solution.py:172
  123.1 0.8 copy-start

commit v4 on v3

--- a/solution.py
+++ b/solution.py
@@ -8,7 +8,7 @@
 TILE = 128
 PANELS = 2
 WIDTH = TILE * PANELS
-STRIP = 32
+STRIP = 64
 GROUP = 8
 HIGHEST = lax.Precision.HIGHEST
 
@@ -25,29 +25,49 @@
 
 
 def eliminate(strip, pivot_lane):
-    tiles = [strip[t * GROUP : (t + 1) * GROUP] for t in range(STRIP // GROUP)]
-    sub_row = lax.broadcasted_iota(jnp.int32, (GROUP, 1), 0)
-    scales = [jnp.ones((GROUP, 1), jnp.float32) for _ in tiles]
-    for i in range(STRIP):
-        lane = pivot_lane + i
-        own, sub = divmod(i, GROUP)
-        row = tiles[own][sub : sub + 1, :]
-        pivot = tiles[own][sub : sub + 1, lane : lane + 1]
-        inverse = 1.0 / pivot
-        scales[own] = jnp.where(sub_row == sub, lax.rsqrt(pivot), scales[own])
-        for t in range(own, STRIP // GROUP):
-            factor = tiles[t][:, lane : lane + 1] * inverse
-            if t == own:
-                factor = jnp.where(sub_row > sub, factor, 0.0)
-            tiles[t] = tiles[t] - factor * row
-    return jnp.concatenate([tile * scale for tile, scale in zip(tiles, scales)], axis=0)
+    count, width = strip.shape
+    shape = (GROUP, TILE)
+    tiles = [
+        [strip[t * GROUP : (t + 1) * GROUP, v * TILE : (v + 1) * TILE] for v in range(width // TILE)]
+        for t in range(count // GROUP)
+    ]
+    sub_row = lax.broadcasted_iota(jnp.int32, shape, 0)
+
+    def over_lanes(tile, lane):
+        return jnp.broadcast_to(tile[:, lane : lane + 1], shape)
+
+    def over_rows(tile, row):
+        return jnp.broadcast_to(tile[row : row + 1], shape)
+
+    scaled = []
+    for own in range(len(tiles)):
+        block, lane = divmod(pivot_lane + GROUP * own, TILE)
+        columns = [
+            [over_lanes(parts[block], lane + k) for k in range(GROUP)] for parts in tiles[own:]
+        ]
+        pivots = jnp.ones(shape, jnp.float32)
+        for k in range(GROUP):
+            pivot_row = {j: over_rows(columns[0][j], k) for j in range(k, GROUP)}
+            inverse = 1.0 / pivot_row[k]
+            pivots = jnp.where(sub_row == k, pivot_row[k], pivots)
+            rows = [over_rows(part, k) for part in tiles[own]]
+            for t, column in enumerate(columns, own):
+                factor = column[k] * inverse
+                for j in range(k + 1, GROUP):
+                    column[j] = column[j] - factor * pivot_row[j]
+                if t == own:
+                    factor = jnp.where(sub_row > k, factor, 0.0)
+                tiles[t] = [part - factor * row for part, row in zip(tiles[t], rows)]
+        scale = lax.rsqrt(pivots)
+        scaled.append(jnp.concatenate([part * scale for part in tiles[own]], axis=1))
+    return jnp.concatenate(scaled, axis=0)
 
 
 def inverse_factor_kernel(diag_ref, inverse_ref, work_ref):
     half = diag_ref.shape[0] // PANELS
     for p in range(PANELS):
         for q in range(PANELS):
-            part = diag_ref[q * half : (q + 1) * half, 0, p].reshape(TILE, TILE)
+            part = diag_ref[q * half : (q + 1) * half, p, 0].reshape(TILE, TILE)
             work_ref[p * TILE : (p + 1) * TILE, q * TILE : (q + 1) * TILE] = part
     at_row = lax.broadcasted_iota(jnp.int32, (WIDTH, WIDTH), 0)
     at_col = lax.broadcasted_iota(jnp.int32, (WIDTH, WIDTH), 1)
@@ -68,38 +88,37 @@
             inverse_ref[stop:, :done] = inverse_ref[stop:, :done] - update[:, upper:]
 
 
-def inverse_factor(diag):
+def inverse_factor(held):
     return pl.pallas_call(
         inverse_factor_kernel,
         grid=(1,),
         out_shape=jax.ShapeDtypeStruct((WIDTH, WIDTH), jnp.float32),
-        in_specs=[pl.BlockSpec((diag.shape[0], 1, *diag.shape[2:]), lambda _: (0, 0, 0, 0, 0))],
+        in_specs=[pl.BlockSpec((*held.shape[:2], 1, GROUP, TILE), lambda _: (0, 0, 0, 0, 0))],
         out_specs=pl.BlockSpec((WIDTH, WIDTH), lambda _: (0, 0)),
         scratch_shapes=[pltpu.VMEM((WIDTH, WIDTH), jnp.float32)],
         cost_estimate=pl.CostEstimate(
             flops=4 * WIDTH**3, bytes_accessed=12 * WIDTH**2, transcendentals=0
         ),
         name="inverse_factor",
-    )(diag)
-
-
-def solve_rows_kernel(first_ref, rest_ref, inverse_ref, lower_ref):
-    half = first_ref.shape[0] // PANELS
+    )(held)
+
+
+def solve_rows_kernel(held_ref, inverse_ref, lower_ref):
+    half = held_ref.shape[0] // PANELS
     raw = []
     for t in range(lower_ref.shape[0] // TILE):
         group, tile = divmod(t, PANELS)
         parts = []
         for p in range(PANELS):
             side = (tile + p) % PANELS
-            held = slice(side * half, (side + 1) * half)
-            part = first_ref[held, 1, p] if group == 0 else rest_ref[held, p, group - 1]
+            part = held_ref[side * half : (side + 1) * half, p, group + 1]
             parts.append(part.reshape(TILE, TILE))
         raw.append(jnp.concatenate(parts, axis=1))
     lower_ref[...] = product(jnp.concatenate(raw, axis=0), inverse_ref[...], ((1,), (1,)))
 
 
-def solve_rows(first, rest, inverse):
-    count = rest.shape[0] * (rest.shape[2] + 1) * GROUP
+def solve_rows(held, inverse):
+    count = held.shape[0] * (held.shape[2] - 1) * GROUP
     return pl.pallas_call(
         solve_rows_kernel,
         out_shape=jax.ShapeDtypeStruct((count, WIDTH), jnp.float32),
@@ -107,7 +126,7 @@
             flops=12 * count * WIDTH**2, bytes_accessed=8 * count * WIDTH, transcendentals=0
         ),
         name="solve_rows",
-    )(first, rest, inverse)
+    )(held, inverse)
 
 
 def trailing_kernel(place_ref, matrix_ref, lower_ref, cols_ref, inverse_ref, out_ref, solved_ref):
@@ -202,15 +221,12 @@
         col_part = from_rows[:, :, :cols_count]
         diag_part = from_rows[:, :, cols_count:]
     with jax.named_scope("gather_rows"):
-        rest = lax.all_gather(row_part[:, 1:], "col")
-    with jax.named_scope("spread_diagonal"):
-        diag_part, rest = lax.optimization_barrier((diag_part, rest))
-        first = to_all(jnp.stack([diag_part, row_part[:, 0]]), "col")
+        held = to_all(jnp.concatenate([diag_part[:, None], row_part], axis=1), "col")
     with jax.named_scope("gather_cols"):
-        first, col_part = lax.optimization_barrier((first, col_part))
-        cols = to_all(col_part, "row")
-    inverse = inverse_factor(first)
-    lower = solve_rows(first, rest, inverse)
+        cols = lax.all_gather(col_part, "row")
+    held, cols = lax.optimization_barrier((held, cols))
+    inverse = inverse_factor(held)
+    lower = solve_rows(held, inverse)
     place = jnp.stack(
         [jnp.int32(grid_rows), jnp.int32(grid_cols), lax.axis_index("row"), col_index]
     ).astype(jnp.int32)

time: 130 us -> 120 us (0.923)
  the two profiles are of different devices: /device:TPU:1 before, /device:TPU:12 now
where the time goes in v4:
time: 120 us
  blocking collectives  35.3 us (29%)
  starting transfers between devices  29.5 us (25%)
  waiting for transfers between devices  29.5 us (25%)
  Pallas kernels  18.9 us (16%)
  local copies, waits for them, and re-layouts  5.12 us (4%)
  other arithmetic  1.46 us (1%)
    all_gather x1, blocking collectives, on_device(): cols = lax.all_gather(col_part, 'row')  35.3 us
    all_to_all x3, waiting for transfers between devices, exchange(): return lax.all_to_all(chunks, axis, 0, 0, tiled=True)  29.5 us
    all_to_all x3, starting transfers between devices, exchange(): return lax.all_to_all(chunks, axis, 0, 0, tiled=True)  29.5 us
    pallas_call x1, Pallas kernels, inverse_factor(): pl.pallas_call(inverse_factor_kernel, grid=(1,), out_shape=jax.ShapeDtype...  9.9 us
    pallas_call x1, Pallas kernels, trailing(): pl.pallas_call(trailing_kernel, grid=(rows_count // rows_step,), out_shap...  5.63 us
    pallas_call x1, Pallas kernels, solve_rows(): pl.pallas_call(solve_rows_kernel, out_shape=jax.ShapeDtypeStruct((count,...  3.33 us
  transfers between devices with their start and end apart: 3, of which 2 were waited for; matrix products, arithmetic and copies ran while one was open for 1% of the time, Pallas kernels for 0%

profile of v4, /device:TPU:12, one launch (start us, length us, event | category | flops | bytes accessed | tf_op | source)
XLA Modules:
  0.0 119.8 jit_solution(2644011676509395824)
XLA Ops:
  0.0 1.1 slice.27
  1.1 0.9 copy.4
  2.0 9.4 %all-to-all-start = ((f32[32,4,8,128]{3,2,1,0:T(8,128)}), f32[32,4,8,128]{3,2,1,0:T(8,128)S(1)}, u32[]{:S(2)}, u32[]{:S(2)}) async-start(f32[32,4,8,128]{3,2,1,0:T(8,128)} %bitcast.5), calls=%async_computation | async-start | bytes 1048576 | tf_op jit(solution)/shard_map/scatter_rows/all_to_all | solution.py:191
  11.4 1.0 slice_bitcast_fusion
  12.4 7.4 %all-to-all-done = f32[32,4,8,128]{3,2,1,0:T(8,128)S(1)} async-done(((f32[32,4,8,128]{3,2,1,0:T(8,128)}), f32[32,4,8,128]{3,2,1,0:T(8,128)S(1)}, u32[]{:S(2)}, u32[]{:S(2)}) %all-to-all-start) | async-done | bytes 524320 | tf_op jit(solution)/shard_map/scatter_rows/all_to_all | solution.py:191
  19.8 0.8 pad_maximum_fusion
  20.5 13.3 %all-to-all-start.1 = ((f32[16,8,640]{2,1,0:T(8,128)}), f32[16,8,640]{2,1,0:T(8,128)S(1)}, u32[]{:S(2)}, u32[]{:S(2)}) async-start(f32[16,8,640]{2,1,0:T(8,128)} %pad_maximum_fusion), calls=%async_computation.1 | async-start | bytes 655360 | tf_op jit(solution)/shard_map/scatter_cols/all_to_all | solution.py:191
  33.9 22.1 %all-to-all-done.1 = f32[16,8,640]{2,1,0:T(8,128)S(1)} async-done(((f32[16,8,640]{2,1,0:T(8,128)}), f32[16,8,640]{2,1,0:T(8,128)S(1)}, u32[]{:S(2)}, u32[]{:S(2)}) %all-to-all-start.1) | async-done | bytes 327712 | tf_op jit(solution)/shard_map/scatter_cols/all_to_all | solution.py:191
  56.0 1.1 broadcast_in_dim.8
  57.2 6.7 %all-to-all-start.2 = ((f32[32,2,5,8,128]{4,3,2,1,0:T(8,128)}), f32[32,2,5,8,128]{4,3,2,1,0:T(8,128)S(1)}, u32[]{:S(2)}, u32[]{:S(2)}) async-start(f32[32,2,5,8,128]{4,3,2,1,0:T(8,128)} %broadcast_in_dim.8), calls=%async_computation.2 | async-start | bytes 2621440 | tf_op jit(solution)/shard_map/gather_rows/all_to_all | solution.py:191
  63.9 0.7 pad_add_fusion.place_ref
  64.5 35.3 %all-gather = f32[32,8,512]{2,1,0:T(8,128)} all-gather(f32[2,8,512]{2,1,0:T(8,128)S(1)} %slice.37), channel_id=2, replica_groups=mesh['row'=16,'col'=32] {'row'}, dimensions={0}, use_global_device_ids=true | all-gather | bytes 557056 | tf_op jit(solution)/shard_map/gather_cols/all_gather | solution.py:226
  99.8 0.0 all-to-all-done.2.diag_ref.held_ref
  99.8 0.0 copy-start
  99.8 1.1 copy-done
  100.9 9.9 %inverse_factor.1.inverse_ref = f32[256,256]{1,0:T(8,128)} custom-call(f32[32,2,5,8,128]{4,3,2,1,0:T(8,128)} %copy-done), custom_call_target="tpu_custom_call" | custom-call | flops 67108864 | bytes 786432 | tf_op jit(solution)/shard_map/inverse_factor/pallas_call | solution.py:92
  110.8 3.3 %solve_rows.1.lower_ref = f32[1024,256]{1,0:T(8,128)} custom-call(f32[32,2,5,8,128]{4,3,2,1,0:T(8,128)} %copy-done, f32[256,256]{1,0:T(8,128)} %inverse_factor.1.inverse_ref), custom_call_target="tpu_custom_call" | custom-call | flops 805306368 | bytes 2097152 | tf_op jit(solution)/shard_map/solve_rows/pallas_call | solution.py:122
  114.1 5.6 %trailing.1 = f32[1024,512]{1,0:T(8,128)} custom-call(s32[4]{0:T(128)} %pad_add_fusion.place_ref, f32[1024,512]{1,0:T(8,128)} %matrix_ref.1, f32[1024,256]{1,0:T(8,128)} %solve_rows.1.lower_ref, f32[16,2,8,512]{3,2,1,0:T(8,128)} %bitcast.15, f32[256,256]{1,0:T(8,128)} %inverse_factor.1.inverse_ref), custom_call_target="tpu_custom_call" | custom-call | tf_op jit(solution)/shard_map/trailing/pallas_call | solution.py:173
  (7 shorter events, 0.1 us)
Async XLA Ops:
  2.0 17.8 %all-to-all-start = ((f32[32,4,8,128]{3,2,1,0:T(8,128)}), f32[32,4,8,128]{3,2,1,0:T(8,128)S(1)}, u32[]{:S(2)}, u32[]{:S(2)}) async-start(f32[32,4,8,128]{3,2,1,0:T(8,128)} %bitcast.5), calls=%async_computation | async-start | bytes 1048576 | tf_op jit(solution)/shard_map/scatter_rows/all_to_all | solution.py:191
  20.5 35.5 %all-to-all-start.1 = ((f32[16,8,640]{2,1,0:T(8,128)}), f32[16,8,640]{2,1,0:T(8,128)S(1)}, u32[]{:S(2)}, u32[]{:S(2)}) async-start(f32[16,8,640]{2,1,0:T(8,128)} %pad_maximum_fusion), calls=%async_computation.1 | async-start | bytes 655360 | tf_op jit(solution)/shard_map/scatter_cols/all_to_all | solution.py:191
  57.2 42.7 %all-to-all-start.2 = ((f32[32,2,5,8,128]{4,3,2,1,0:T(8,128)}), f32[32,2,5,8,128]{4,3,2,1,0:T(8,128)S(1)}, u32[]{:S(2)}, u32[]{:S(2)}) async-start(f32[32,2,5,8,128]{4,3,2,1,0:T(8,128)} %broadcast_in_dim.8), calls=%async_computation.2 | async-start | bytes 2621440 | tf_op jit(solution)/shard_map/gather_rows/all_to_all | solution.py:191
  99.8 1.1 copy-start

commit v5 on v4

--- a/solution.py
+++ b/solution.py
@@ -64,11 +64,8 @@
 
 
 def inverse_factor_kernel(diag_ref, inverse_ref, work_ref):
-    half = diag_ref.shape[0] // PANELS
     for p in range(PANELS):
-        for q in range(PANELS):
-            part = diag_ref[q * half : (q + 1) * half, p, 0].reshape(TILE, TILE)
-            work_ref[p * TILE : (p + 1) * TILE, q * TILE : (q + 1) * TILE] = part
+        work_ref[p * TILE : (p + 1) * TILE, :] = diag_ref[:, p].reshape(TILE, WIDTH)
     at_row = lax.broadcasted_iota(jnp.int32, (WIDTH, WIDTH), 0)
     at_col = lax.broadcasted_iota(jnp.int32, (WIDTH, WIDTH), 1)
     inverse_ref[...] = jnp.where(at_row == at_col, 1.0, 0.0).astype(jnp.float32)
@@ -88,37 +85,35 @@
             inverse_ref[stop:, :done] = inverse_ref[stop:, :done] - update[:, upper:]
 
 
-def inverse_factor(held):
+def inverse_factor(spread):
+    last = spread.shape[-1] // WIDTH - 1
     return pl.pallas_call(
         inverse_factor_kernel,
         grid=(1,),
         out_shape=jax.ShapeDtypeStruct((WIDTH, WIDTH), jnp.float32),
-        in_specs=[pl.BlockSpec((*held.shape[:2], 1, GROUP, TILE), lambda _: (0, 0, 0, 0, 0))],
+        in_specs=[pl.BlockSpec((*spread.shape[:-1], WIDTH), lambda _: (0, 0, 0, last))],
         out_specs=pl.BlockSpec((WIDTH, WIDTH), lambda _: (0, 0)),
         scratch_shapes=[pltpu.VMEM((WIDTH, WIDTH), jnp.float32)],
         cost_estimate=pl.CostEstimate(
             flops=4 * WIDTH**3, bytes_accessed=12 * WIDTH**2, transcendentals=0
         ),
         name="inverse_factor",
-    )(held)
+    )(spread)
 
 
 def solve_rows_kernel(held_ref, inverse_ref, lower_ref):
     half = held_ref.shape[0] // PANELS
     raw = []
     for t in range(lower_ref.shape[0] // TILE):
-        group, tile = divmod(t, PANELS)
-        parts = []
-        for p in range(PANELS):
-            side = (tile + p) % PANELS
-            part = held_ref[side * half : (side + 1) * half, p, group + 1]
-            parts.append(part.reshape(TILE, TILE))
+        group, side = divmod(t, PANELS)
+        held = slice(side * half, (side + 1) * half)
+        parts = [held_ref[held, p, group].reshape(TILE, TILE) for p in range(PANELS)]
         raw.append(jnp.concatenate(parts, axis=1))
     lower_ref[...] = product(jnp.concatenate(raw, axis=0), inverse_ref[...], ((1,), (1,)))
 
 
 def solve_rows(held, inverse):
-    count = held.shape[0] * (held.shape[2] - 1) * GROUP
+    count = held.shape[0] * held.shape[2] * GROUP
     return pl.pallas_call(
         solve_rows_kernel,
         out_shape=jax.ShapeDtypeStruct((count, WIDTH), jnp.float32),
@@ -178,7 +173,7 @@
             pl.BlockSpec(memory_space=pltpu.SMEM),
             pl.BlockSpec((rows_step, cols_count), lambda t: (t, 0)),
             pl.BlockSpec((rows_step, WIDTH), lambda t: (t, 0)),
-            pl.BlockSpec(cols.shape, lambda t: (0, 0, 0, 0)),
+            pl.BlockSpec((*cols.shape[:-1], cols_count), lambda t: (0, 0, 0, 0)),
             pl.BlockSpec(inverse.shape, lambda t: (0, 0)),
         ],
         out_specs=pl.BlockSpec((rows_step, cols_count), lambda t: (t, 0)),
@@ -200,37 +195,27 @@
     rows_count, cols_count = matrix.shape
     grid_rows = lax.axis_size("row")
     grid_cols = lax.axis_size("col")
-    col_index = lax.axis_index("col")
-    half = grid_cols // PANELS
     groups = rows_count // (grid_cols * GROUP)
+    with jax.named_scope("scatter_cols"):
+        to_rows = matrix[:TILE].reshape(grid_rows, GROUP, cols_count)
+        col_part = exchange(to_rows, "row")[:PANELS]
     with jax.named_scope("scatter_rows"):
-        panel = matrix[:, :TILE].reshape(groups, PANELS, half, GROUP, TILE)
-        panel = jnp.where(col_index == 1, panel[:, ::-1], panel)
-        panel = panel.transpose(1, 2, 0, 3, 4).reshape(grid_cols, groups, GROUP, TILE)
-        row_part = exchange(panel, "col")[:PANELS]
-    with jax.named_scope("scatter_cols"):
-        own_diag = jnp.where(col_index < half, row_part[0, 0], row_part[1, 0])
-        to_rows = jnp.concatenate(
-            [
-                matrix[:TILE].reshape(grid_rows, GROUP, cols_count),
-                jnp.broadcast_to(own_diag[None], (grid_rows, GROUP, TILE)),
-            ],
-            axis=2,
-        )
-        from_rows = exchange(to_rows, "row")[:PANELS]
-        col_part = from_rows[:, :, :cols_count]
-        diag_part = from_rows[:, :, cols_count:]
+        panel = matrix[:, :TILE].reshape(groups, grid_cols, GROUP, TILE).transpose(1, 0, 2, 3)
+        own_diag = jnp.broadcast_to(col_part[None, :, :, :TILE], (grid_cols, PANELS, GROUP, TILE))
+        from_cols = exchange(jnp.concatenate([panel, own_diag], axis=1), "col")[:PANELS]
+        row_part = from_cols[:, :groups]
+        diag_part = from_cols[:, groups:].transpose(1, 2, 0, 3).reshape(PANELS, GROUP, WIDTH)
     with jax.named_scope("gather_rows"):
-        held = to_all(jnp.concatenate([diag_part[:, None], row_part], axis=1), "col")
+        held = to_all(row_part, "col")
     with jax.named_scope("gather_cols"):
-        cols = lax.all_gather(col_part, "row")
-    held, cols = lax.optimization_barrier((held, cols))
-    inverse = inverse_factor(held)
+        spread = lax.all_gather(jnp.concatenate([col_part, diag_part], axis=2), "row")
+    held, spread = lax.optimization_barrier((held, spread))
+    inverse = inverse_factor(spread)
     lower = solve_rows(held, inverse)
     place = jnp.stack(
-        [jnp.int32(grid_rows), jnp.int32(grid_cols), lax.axis_index("row"), col_index]
+        [jnp.int32(grid_rows), jnp.int32(grid_cols), lax.axis_index("row"), lax.axis_index("col")]
     ).astype(jnp.int32)
-    return trailing(place, matrix, lower, cols, inverse)
+    return trailing(place, matrix, lower, spread, inverse)
 
 
 def solution(mesh):

time: 120 us -> 118 us (0.983)
  the two profiles are of different devices: /device:TPU:12 before, /device:TPU:2 now
where the time goes in v5:
time: 118 us
  blocking collectives  55.7 us (47%)
  starting transfers between devices  21.2 us (18%)
  Pallas kernels  19 us (16%)
  waiting for transfers between devices  18.3 us (16%)
  local copies, waits for them, and re-layouts  2.94 us (2%)
    all_gather x1, blocking collectives, on_device(): lax.all_gather(jnp.concatenate([col_part, diag_part], axis=2), 'row')  36.3 us
    all_to_all x2, starting transfers between devices, exchange(): return lax.all_to_all(chunks, axis, 0, 0, tiled=True)  21.2 us
    all_to_all x1, blocking collectives, exchange(): return lax.all_to_all(chunks, axis, 0, 0, tiled=True)  19.5 us
    all_to_all x2, waiting for transfers between devices, exchange(): return lax.all_to_all(chunks, axis, 0, 0, tiled=True)  18.3 us
    pallas_call x1, Pallas kernels, inverse_factor(): pl.pallas_call(inverse_factor_kernel, grid=(1,), out_shape=jax.ShapeDtype...  10.1 us
    pallas_call x1, Pallas kernels, trailing(): pl.pallas_call(trailing_kernel, grid=(rows_count // rows_step,), out_shap...  5.63 us
    pallas_call x1, Pallas kernels, solve_rows(): pl.pallas_call(solve_rows_kernel, out_shape=jax.ShapeDtypeStruct((count,...  3.26 us
  transfers between devices with their start and end apart: 2, of which 1 were waited for; matrix products, arithmetic and copies ran while one was open for 1% of the time, Pallas kernels for 0%

profile of v5, /device:TPU:2, one launch (start us, length us, event | category | flops | bytes accessed | tf_op | source)
XLA Modules:
  0.0 117.9 jit_solution(14254292323141695515)
XLA Ops:
  0.0 0.0 slice-start
  0.0 1.7 %slice_bitcast_fusion = f32[16,8,512]{2,1,0:T(8,128)} fusion(f32[1024,512]{1,0:T(8,128)} %matrix_ref.1), kind=kLoop, calls=%fused_computation.2 | loop fusion | bytes 524288 | tf_op jit(solution)/shard_map/scatter_cols/reshape | solution.py:200
  1.7 15.2 %all-to-all-start = ((f32[16,8,512]{2,1,0:T(8,128)}), f32[16,8,512]{2,1,0:T(8,128)S(1)}, u32[]{:S(2)}, u32[]{:S(2)}) async-start(f32[16,8,512]{2,1,0:T(8,128)} %slice_bitcast_fusion), calls=%async_computation | async-start | bytes 524288 | tf_op jit(solution)/shard_map/scatter_cols/all_to_all | solution.py:186
  16.9 0.0 slice-done
  17.0 0.1 copy.8
  17.0 18.3 %all-to-all-done = f32[16,8,512]{2,1,0:T(8,128)S(1)} async-done(((f32[16,8,512]{2,1,0:T(8,128)}), f32[16,8,512]{2,1,0:T(8,128)S(1)}, u32[]{:S(2)}, u32[]{:S(2)}) %all-to-all-start) | async-done | bytes 262176 | tf_op jit(solution)/shard_map/scatter_cols/all_to_all | solution.py:186
  35.3 0.1 pad_maximum_fusion
  35.4 19.5 %all_to_all.15 = f32[32,6,8,128]{3,2,1,0:T(8,128)S(1)} all-to-all(f32[32,6,8,128]{3,2,1,0:T(8,128)S(1)} %pad_maximum_fusion), channel_id=1, replica_groups=mesh['row'=16,'col'=32] {'col'}, dimensions={0} | all-to-all | bytes 1572864 | tf_op jit(solution)/shard_map/scatter_rows/all_to_all | solution.py:186
  54.9 1.1 broadcast_in_dim.5
  56.0 6.0 %all-to-all-start.2 = ((f32[32,2,4,8,128]{4,3,2,1,0:T(8,128)}), f32[32,2,4,8,128]{4,3,2,1,0:T(8,128)S(1)}, u32[]{:S(2)}, u32[]{:S(2)}) async-start(f32[32,2,4,8,128]{4,3,2,1,0:T(8,128)} %broadcast_in_dim.5), calls=%async_computation.2 | async-start | bytes 2097152 | tf_op jit(solution)/shard_map/gather_rows/all_to_all | solution.py:186
  62.0 0.7 pad_add_fusion.place_ref
  62.7 36.3 %all-gather = f32[32,8,768]{2,1,0:T(8,128)} all-gather(f32[2,8,768]{2,1,0:T(8,128)S(1)} %pad_maximum_fusion.1), channel_id=2, replica_groups=mesh['row'=16,'col'=32] {'row'}, dimensions={0}, use_global_device_ids=true | all-gather | bytes 835584 | tf_op jit(solution)/shard_map/gather_cols/all_gather | solution.py:211
  98.9 0.0 all-to-all-done.2.held_ref
  98.9 0.0 copy-start
  99.0 10.1 %inverse_factor.1.inverse_ref = f32[256,256]{1,0:T(8,128)} custom-call(f32[16,2,8,768]{3,2,1,0:T(8,128)} %bitcast.14), custom_call_target="tpu_custom_call" | custom-call | flops 67108864 | bytes 786432 | tf_op jit(solution)/shard_map/inverse_factor/pallas_call | solution.py:90
  109.0 0.0 copy-done
  109.0 3.3 %solve_rows.1.lower_ref = f32[1024,256]{1,0:T(8,128)} custom-call(f32[32,2,4,8,128]{4,3,2,1,0:T(8,128)} %copy-done, f32[256,256]{1,0:T(8,128)} %inverse_factor.1.inverse_ref), custom_call_target="tpu_custom_call" | custom-call | flops 805306368 | bytes 2097152 | tf_op jit(solution)/shard_map/solve_rows/pallas_call | solution.py:117
  112.3 5.6 %trailing.1 = f32[1024,512]{1,0:T(8,128)} custom-call(s32[4]{0:T(128)} %pad_add_fusion.place_ref, f32[1024,512]{1,0:T(8,128)} %matrix_ref.1, f32[1024,256]{1,0:T(8,128)} %solve_rows.1.lower_ref, f32[16,2,8,768]{3,2,1,0:T(8,128)} %bitcast.15, f32[256,256]{1,0:T(8,128)} %inverse_factor.1.inverse_ref), custom_call_target="tpu_custom_call" | custom-call | tf_op jit(solution)/shard_map/trailing/pallas_call | solution.py:168
  (6 shorter events, 0.0 us)
Async XLA Ops:
  0.0 16.9 %slice-start = ((f32[1024,512]{1,0:T(8,128)}), f32[1024,128]{1,0:T(8,128)S(1)}, s32[]{:S(2)}) async-start(f32[1024,512]{1,0:T(8,128)} %matrix_ref.1), calls=%async_computation.3 | async-start | bytes 1048576 | tf_op jit(solution)/shard_map/scatter_rows/slice | solution.py:203
  1.7 33.6 %all-to-all-start = ((f32[16,8,512]{2,1,0:T(8,128)}), f32[16,8,512]{2,1,0:T(8,128)S(1)}, u32[]{:S(2)}, u32[]{:S(2)}) async-start(f32[16,8,512]{2,1,0:T(8,128)} %slice_bitcast_fusion), calls=%async_computation | async-start | bytes 524288 | tf_op jit(solution)/shard_map/scatter_cols/all_to_all | solution.py:186
  56.0 43.0 %all-to-all-start.2 = ((f32[32,2,4,8,128]{4,3,2,1,0:T(8,128)}), f32[32,2,4,8,128]{4,3,2,1,0:T(8,128)S(1)}, u32[]{:S(2)}, u32[]{:S(2)}) async-start(f32[32,2,4,8,128]{4,3,2,1,0:T(8,128)} %broadcast_in_dim.5), calls=%async_computation.2 | async-start | bytes 2097152 | tf_op jit(solution)/shard_map/gather_rows/all_to_all | solution.py:186
  98.9 10.1 %copy-start = (f32[32,2,4,8,128]{4,3,2,1,0:T(8,128)}, f32[32,2,4,8,128]{4,3,2,1,0:T(8,128)S(1)}, u32[]{:S(2)}) copy-start(f32[32,2,4,8,128]{4,3,2,1,0:T(8,128)S(1)} %all-to-all-done.2.held_ref) | copy-start | bytes 3145732

commit v6 on v4

--- a/solution.py
+++ b/solution.py
@@ -67,7 +67,7 @@
     half = diag_ref.shape[0] // PANELS
     for p in range(PANELS):
         for q in range(PANELS):
-            part = diag_ref[q * half : (q + 1) * half, p, 0].reshape(TILE, TILE)
+            part = diag_ref[q * half : (q + 1) * half, p].reshape(TILE, TILE)
             work_ref[p * TILE : (p + 1) * TILE, q * TILE : (q + 1) * TILE] = part
     at_row = lax.broadcasted_iota(jnp.int32, (WIDTH, WIDTH), 0)
     at_col = lax.broadcasted_iota(jnp.int32, (WIDTH, WIDTH), 1)
@@ -88,19 +88,16 @@
             inverse_ref[stop:, :done] = inverse_ref[stop:, :done] - update[:, upper:]
 
 
-def inverse_factor(held):
+def inverse_factor(diag):
     return pl.pallas_call(
         inverse_factor_kernel,
-        grid=(1,),
         out_shape=jax.ShapeDtypeStruct((WIDTH, WIDTH), jnp.float32),
-        in_specs=[pl.BlockSpec((*held.shape[:2], 1, GROUP, TILE), lambda _: (0, 0, 0, 0, 0))],
-        out_specs=pl.BlockSpec((WIDTH, WIDTH), lambda _: (0, 0)),
         scratch_shapes=[pltpu.VMEM((WIDTH, WIDTH), jnp.float32)],
         cost_estimate=pl.CostEstimate(
             flops=4 * WIDTH**3, bytes_accessed=12 * WIDTH**2, transcendentals=0
         ),
         name="inverse_factor",
-    )(held)
+    )(diag)
 
 
 def solve_rows_kernel(held_ref, inverse_ref, lower_ref):
@@ -111,14 +108,14 @@
         parts = []
         for p in range(PANELS):
             side = (tile + p) % PANELS
-            part = held_ref[side * half : (side + 1) * half, p, group + 1]
+            part = held_ref[side * half : (side + 1) * half, p, group]
             parts.append(part.reshape(TILE, TILE))
         raw.append(jnp.concatenate(parts, axis=1))
     lower_ref[...] = product(jnp.concatenate(raw, axis=0), inverse_ref[...], ((1,), (1,)))
 
 
 def solve_rows(held, inverse):
-    count = held.shape[0] * (held.shape[2] - 1) * GROUP
+    count = held.shape[0] * held.shape[2] * GROUP
     return pl.pallas_call(
         solve_rows_kernel,
         out_shape=jax.ShapeDtypeStruct((count, WIDTH), jnp.float32),
@@ -136,18 +133,35 @@
 
     @pl.when(step == 0)
     def _():
-        cols = jnp.concatenate(
-            [cols_ref[:, p].reshape(TILE, cols_count) for p in range(PANELS)], axis=0
+        half = cols_ref.shape[0] // PANELS
+        sides = [
+            jnp.concatenate(
+                [
+                    cols_ref[q * half : (q + 1) * half, b].reshape(TILE, TILE)
+                    for b in range(cols_ref.shape[1])
+                ],
+                axis=0,
+            )
+            for q in range(PANELS)
+        ]
+        low_half = col_index < half
+        raw = jnp.concatenate(
+            [
+                jnp.where(low_half, sides[0], sides[1]),
+                jnp.where(low_half, sides[1], sides[0]),
+            ],
+            axis=1,
         )
-        high, low = split(product(inverse_ref[...], cols, ((1,), (0,))))
-        solved_ref[0 * WIDTH : 1 * WIDTH, :] = high
-        solved_ref[1 * WIDTH : 2 * WIDTH, :] = low
-        solved_ref[2 * WIDTH : 3 * WIDTH, :] = high
+        high, low = split(product(raw, inverse_ref[...], ((1,), (1,))))
+        solved_ref[:, 0 * WIDTH : 1 * WIDTH] = high
+        solved_ref[:, 1 * WIDTH : 2 * WIDTH] = low
+        solved_ref[:, 2 * WIDTH : 3 * WIDTH] = high
 
     high, low = split(lower_ref[...])
-    update = jnp.dot(
+    update = lax.dot_general(
         jnp.concatenate([high, high, low], axis=1),
         solved_ref[...],
+        (((1,), (1,)), ((), ())),
         preferred_element_type=jnp.float32,
     )
     at_row = lax.broadcasted_iota(jnp.int32, (TILE, TILE), 0)
@@ -182,7 +196,7 @@
             pl.BlockSpec(inverse.shape, lambda t: (0, 0)),
         ],
         out_specs=pl.BlockSpec((rows_step, cols_count), lambda t: (t, 0)),
-        scratch_shapes=[pltpu.VMEM((3 * WIDTH, cols_count), jnp.bfloat16)],
+        scratch_shapes=[pltpu.VMEM((cols_count, 3 * WIDTH), jnp.bfloat16)],
         name="trailing",
     )(place, matrix, lower, cols, inverse)
 
@@ -208,24 +222,20 @@
         panel = jnp.where(col_index == 1, panel[:, ::-1], panel)
         panel = panel.transpose(1, 2, 0, 3, 4).reshape(grid_cols, groups, GROUP, TILE)
         row_part = exchange(panel, "col")[:PANELS]
-    with jax.named_scope("scatter_cols"):
-        own_diag = jnp.where(col_index < half, row_part[0, 0], row_part[1, 0])
-        to_rows = jnp.concatenate(
-            [
-                matrix[:TILE].reshape(grid_rows, GROUP, cols_count),
-                jnp.broadcast_to(own_diag[None], (grid_rows, GROUP, TILE)),
-            ],
-            axis=2,
-        )
-        from_rows = exchange(to_rows, "row")[:PANELS]
-        col_part = from_rows[:, :, :cols_count]
-        diag_part = from_rows[:, :, cols_count:]
     with jax.named_scope("gather_rows"):
-        held = to_all(jnp.concatenate([diag_part[:, None], row_part], axis=1), "col")
-    with jax.named_scope("gather_cols"):
-        cols = lax.all_gather(col_part, "row")
-    held, cols = lax.optimization_barrier((held, cols))
-    inverse = inverse_factor(held)
+        held = to_all(row_part, "col")
+    with jax.named_scope("gather_planes"):
+        planes = lax.all_gather(row_part, "row")
+        held, planes = lax.optimization_barrier((held, planes))
+    low_half = col_index < half
+    with jax.named_scope("spread_diagonal"):
+        own = planes[:PANELS, :, 0]
+        diag = to_all(jnp.where(low_half, own[:, 0], own[:, 1]), "col")
+    with jax.named_scope("exchange_cols"):
+        diag, planes = lax.optimization_barrier((diag, planes))
+        parts = jnp.where(low_half, planes.swapaxes(0, 1), planes.swapaxes(0, 1)[::-1])
+        cols = exchange(parts.reshape(grid_cols, groups, GROUP, TILE), "col")
+    inverse = inverse_factor(diag)
     lower = solve_rows(held, inverse)
     place = jnp.stack(
         [jnp.int32(grid_rows), jnp.int32(grid_cols), lax.axis_index("row"), col_index]

time: 120 us -> 106 us (0.88)
  the two profiles are of different devices: /device:TPU:12 before, /device:TPU:1 now
where the time goes in v6:
time: 106 us
  blocking collectives  74.7 us (70%)
  Pallas kernels  18.9 us (18%)
  starting transfers between devices  7.44 us (7%)
  local copies, waits for them, and re-layouts  3.91 us (4%)
    all_to_all x2, blocking collectives, exchange(): return lax.all_to_all(chunks, axis, 0, 0, tiled=True)  43.6 us
    all_gather x1, blocking collectives, on_device(): planes = lax.all_gather(row_part, 'row')  31.1 us
    pallas_call x1, Pallas kernels, inverse_factor(): pl.pallas_call(inverse_factor_kernel, out_shape=jax.ShapeDtypeStruct((WID...  9.9 us
    all_to_all x2, starting transfers between devices, exchange(): return lax.all_to_all(chunks, axis, 0, 0, tiled=True)  7.44 us
    pallas_call x1, Pallas kernels, trailing(): pl.pallas_call(trailing_kernel, grid=(rows_count // rows_step,), out_shap...  5.71 us
    pallas_call x1, Pallas kernels, solve_rows(): pl.pallas_call(solve_rows_kernel, out_shape=jax.ShapeDtypeStruct((count,...  3.26 us
  transfers between devices with their start and end apart: 2, of which 0 were waited for; matrix products, arithmetic and copies ran while one was open for 1% of the time, Pallas kernels for 12%

profile of v6, /device:TPU:1, one launch (start us, length us, event | category | flops | bytes accessed | tf_op | source)
XLA Modules:
  0.0 105.7 jit_solution(11472504274882427761)
XLA Ops:
  0.0 1.1 %slice.15 = f32[1024,128]{1,0:T(8,128)S(1)} slice(f32[1024,512]{1,0:T(8,128)} %matrix_ref.1), slice={[0:1024], [0:128]} | slice | bytes 1048576 | tf_op jit(solution)/shard_map/scatter_rows/slice | solution.py:221
  1.1 0.1 copy.6
  1.2 21.3 %all_to_all.20 = f32[32,4,8,128]{3,2,1,0:T(8,128)S(1)} all-to-all(f32[32,4,8,128]{3,2,1,0:T(8,128)S(1)} %bitcast.15), channel_id=1, replica_groups=mesh['row'=16,'col'=32] {'col'}, dimensions={0} | all-to-all | bytes 1048576 | tf_op jit(solution)/shard_map/scatter_rows/all_to_all | solution.py:205
  22.5 1.1 %broadcast_in_dim.6 = f32[32,2,4,8,128]{4,3,2,1,0:T(8,128)} broadcast(f32[2,4,8,128]{3,2,1,0:T(8,128)S(1)} %slice.20), dimensions={1,2,3,4} | broadcast | bytes 1081344 | tf_op jit(solution)/shard_map/gather_rows/broadcast_in_dim | solution.py:210
  23.6 3.7 %all-to-all-start.1 = ((f32[32,2,4,8,128]{4,3,2,1,0:T(8,128)}), f32[32,2,4,8,128]{4,3,2,1,0:T(8,128)S(1)}, u32[]{:S(2)}, u32[]{:S(2)}) async-start(f32[32,2,4,8,128]{4,3,2,1,0:T(8,128)} %broadcast_in_dim.6), calls=%async_computation.1 | async-start | bytes 2097152 | tf_op jit(solution)/shard_map/gather_rows/all_to_all | solution.py:205
  27.3 31.1 %all-gather = f32[32,4,8,128]{3,2,1,0:T(8,128)S(1)} all-gather(f32[2,4,8,128]{3,2,1,0:T(8,128)S(1)} %slice.20), channel_id=2, replica_groups=mesh['row'=16,'col'=32] {'row'}, dimensions={0}, use_global_device_ids=true | all-gather | bytes 557056 | tf_op jit(solution)/shard_map/gather_planes/all_gather | solution.py:228
  58.4 0.0 all-to-all-done.1.held_ref
  58.4 0.0 copy-start.1
  58.4 22.3 %all_to_all.21.diag_ref = f32[32,2,8,128]{3,2,1,0:T(8,128)} all-to-all(f32[32,2,8,128]{3,2,1,0:T(8,128)S(1)} %broadcast_in_dim.16), channel_id=1, replica_groups=mesh['row'=16,'col'=32] {'col'}, dimensions={0} | all-to-all | bytes 524288 | tf_op jit(solution)/shard_map/spread_diagonal/all_to_all | solution.py:205
  80.8 0.8 copy.8
  81.7 3.7 %all-to-all-start.3 = ((f32[32,4,8,128]{3,2,1,0:T(8,128)}), f32[32,4,8,128]{3,2,1,0:T(8,128)S(1)}, u32[]{:S(2)}, u32[]{:S(2)}) async-start(f32[32,4,8,128]{3,2,1,0:T(8,128)} %bitcast.9), calls=%async_computation.3 | async-start | bytes 1048576 | tf_op jit(solution)/shard_map/exchange_cols/all_to_all | solution.py:205
  85.4 0.6 pad_add_fusion.place_ref
  86.0 9.9 %inverse_factor.1.inverse_ref = f32[256,256]{1,0:T(8,128)} custom-call(f32[32,2,8,128]{3,2,1,0:T(8,128)} %all_to_all.21.diag_ref), custom_call_target="tpu_custom_call" | custom-call | flops 67108864 | bytes 786432 | tf_op jit(solution)/shard_map/inverse_factor/pallas_call | solution.py:92
  95.9 0.0 copy-done.1
  95.9 3.3 %solve_rows.1.lower_ref = f32[1024,256]{1,0:T(8,128)} custom-call(f32[32,2,4,8,128]{4,3,2,1,0:T(8,128)} %copy-done.1, f32[256,256]{1,0:T(8,128)} %inverse_factor.1.inverse_ref), custom_call_target="tpu_custom_call" | custom-call | flops 805306368 | bytes 2097152 | tf_op jit(solution)/shard_map/solve_rows/pallas_call | solution.py:119
  99.2 0.0 all-to-all-done.3.cols_ref
  99.2 0.0 copy-start
  99.2 0.8 copy-done
  100.0 5.7 %trailing.1 = f32[1024,512]{1,0:T(8,128)} custom-call(s32[4]{0:T(128)} %pad_add_fusion.place_ref, f32[1024,512]{1,0:T(8,128)} %matrix_ref.1, f32[1024,256]{1,0:T(8,128)} %solve_rows.1.lower_ref, f32[32,4,8,128]{3,2,1,0:T(8,128)} %copy-done, f32[256,256]{1,0:T(8,128)} %inverse_factor.1.inverse_ref), custom_call_target="tpu_custom_call" | custom-call | tf_op jit(solution)/shard_map/trailing/pallas_call | solution.py:187
  (6 shorter events, 0.1 us)
Async XLA Ops:
  23.6 34.8 %all-to-all-start.1 = ((f32[32,2,4,8,128]{4,3,2,1,0:T(8,128)}), f32[32,2,4,8,128]{4,3,2,1,0:T(8,128)S(1)}, u32[]{:S(2)}, u32[]{:S(2)}) async-start(f32[32,2,4,8,128]{4,3,2,1,0:T(8,128)} %broadcast_in_dim.6), calls=%async_computation.1 | async-start | bytes 2097152 | tf_op jit(solution)/shard_map/gather_rows/all_to_all | solution.py:205
  58.4 37.5 %copy-start.1 = (f32[32,2,4,8,128]{4,3,2,1,0:T(8,128)}, f32[32,2,4,8,128]{4,3,2,1,0:T(8,128)S(1)}, u32[]{:S(2)}) copy-start(f32[32,2,4,8,128]{4,3,2,1,0:T(8,128)S(1)} %all-to-all-done.1.held_ref) | copy-start | bytes 3145732
  81.7 17.5 %all-to-all-start.3 = ((f32[32,4,8,128]{3,2,1,0:T(8,128)}), f32[32,4,8,128]{3,2,1,0:T(8,128)S(1)}, u32[]{:S(2)}, u32[]{:S(2)}) async-start(f32[32,4,8,128]{3,2,1,0:T(8,128)} %bitcast.9), calls=%async_computation.3 | async-start | bytes 1048576 | tf_op jit(solution)/shard_map/exchange_cols/all_to_all | solution.py:205
  99.2 0.8 copy-start

commit v7 on v6

v7 whole, which is shorter than its diff:
```python
import functools

import jax
import jax.numpy as jnp
from jax import lax
from jax.experimental import pallas as pl
from jax.experimental.pallas import tpu as pltpu
from jax.sharding import PartitionSpec as P

TILE = 128
PANELS = 2
WIDTH = TILE * PANELS
STRIP = 64
GROUP = 8
HIGHEST = lax.Precision.HIGHEST


def product(lhs, rhs, contract):
    return lax.dot_general(
        lhs, rhs, (contract, ((), ())), precision=HIGHEST, preferred_element_type=jnp.float32
    )


def split(value):
    high = value.astype(jnp.bfloat16)
    return high, (value - high.astype(jnp.float32)).astype(jnp.bfloat16)


def eliminate(strip, pivot_lane):
    count, width = strip.shape
    shape = (GROUP, TILE)
    tiles = [
        [strip[t * GROUP : (t + 1) * GROUP, v * TILE : (v + 1) * TILE] for v in range(width // TILE)]
        for t in range(count // GROUP)
    ]
    sub_row = lax.broadcasted_iota(jnp.int32, shape, 0)

    def over_lanes(tile, lane):
        return jnp.broadcast_to(tile[:, lane : lane + 1], shape)

    def over_rows(tile, row):
        return jnp.broadcast_to(tile[row : row + 1], shape)

    scaled = []
    for own in range(len(tiles)):
        block, lane = divmod(pivot_lane + GROUP * own, TILE)
        columns = [
            [over_lanes(parts[block], lane + k) for k in range(GROUP)] for parts in tiles[own:]
        ]
        pivots = jnp.ones(shape, jnp.float32)
        for k in range(GROUP):
            pivot_row = {j: over_rows(columns[0][j], k) for j in range(k, GROUP)}
            inverse = 1.0 / pivot_row[k]
            pivots = jnp.where(sub_row == k, pivot_row[k], pivots)
            rows = [over_rows(part, k) for part in tiles[own]]
            for t, column in enumerate(columns, own):
                factor = column[k] * inverse
                for j in range(k + 1, GROUP):
                    column[j] = column[j] - factor * pivot_row[j]
                if t == own:
                    factor = jnp.where(sub_row > k, factor, 0.0)
                tiles[t] = [part - factor * row for part, row in zip(tiles[t], rows)]
        scale = lax.rsqrt(pivots)
        scaled.append(jnp.concatenate([part * scale for part in tiles[own]], axis=1))
    return jnp.concatenate(scaled, axis=0)


def panels_kernel(diag_ref, held_ref, inverse_ref, lower_ref, work_ref, raw_ref, sem):
    fetch = pltpu.make_async_copy(held_ref, raw_ref, sem)
    fetch.start()
    for p in range(PANELS):
        for q in range(PANELS):
            part = diag_ref[:, q, p].reshape(TILE, TILE)
            work_ref[p * TILE : (p + 1) * TILE, q * TILE : (q + 1) * TILE] = part
    at_row = lax.broadcasted_iota(jnp.int32, (WIDTH, WIDTH), 0)
    at_col = lax.broadcasted_iota(jnp.int32, (WIDTH, WIDTH), 1)
    inverse_ref[...] = jnp.where(at_row == at_col, 1.0, 0.0).astype(jnp.float32)
    tile_rows = lower_ref.shape[0] // TILE
    for start in range(0, WIDTH, STRIP):
        stop = start + STRIP
        first = start // TILE * TILE
        upper = WIDTH - first
        done = first + TILE
        strip = jnp.concatenate(
            [work_ref[start:stop, first:], inverse_ref[start:stop, :done]], axis=1
        )
        strip = eliminate(strip, start - first)
        inverse_ref[start:stop, :done] = strip[:, upper:]
        if stop < WIDTH:
            update = product(strip[:, :upper], strip, ((0,), (0,)))[stop - first :]
            work_ref[stop:, first:] = work_ref[stop:, first:] - update[:, :upper]
            inverse_ref[stop:, :done] = inverse_ref[stop:, :done] - update[:, upper:]
        if stop % TILE == 0:
            if first == 0:
                fetch.wait()
            raw = jnp.concatenate(
                [
                    jnp.concatenate(
                        [raw_ref[:, p, t].reshape(TILE, TILE) for t in range(tile_rows)], axis=0
                    )
                    for p in range(done // TILE)
                ],
                axis=1,
            )
            lower_ref[:, first:done] = product(raw, inverse_ref[first:done, :done], ((1,), (1,)))


def panels(diag, held):
    count = held.shape[0] * held.shape[2] * GROUP
    return pl.pallas_call(
        panels_kernel,
        out_shape=[
            jax.ShapeDtypeStruct((WIDTH, WIDTH), jnp.float32),
            jax.ShapeDtypeStruct((count, WIDTH), jnp.float32),
        ],
        in_specs=[pl.BlockSpec(memory_space=pltpu.VMEM), pl.BlockSpec(memory_space=pl.ANY)],
        scratch_shapes=[
            pltpu.VMEM((WIDTH, WIDTH), jnp.float32),
            pltpu.VMEM(held.shape, jnp.float32),
            pltpu.SemaphoreType.DMA,
        ],
        cost_estimate=pl.CostEstimate(
            flops=4 * WIDTH**3 + 12 * count * WIDTH**2,
            bytes_accessed=12 * WIDTH**2 + 8 * count * WIDTH,
            transcendentals=0,
        ),
        name="panels",
    )(diag, held)


def trailing_kernel(
    grid_rows, grid_cols, place_ref, matrix_ref, lower_ref, cols_ref, inverse_ref, out_ref, solved_ref
):
    step = pl.program_id(0)
    row_index, col_index = place_ref[0], place_ref[1]
    rows_here, cols_count = matrix_ref.shape
    tile_cols = cols_count // TILE
    tiles_here = rows_here // TILE

    @pl.when(step == 0)
    def _():
        raw = jnp.concatenate(
            [
                jnp.concatenate(
                    [cols_ref[:, p, b].reshape(TILE, TILE) for b in range(tile_cols)], axis=0
                )
                for p in range(PANELS)
            ],
            axis=1,
        )
        high, low = split(product(raw, inverse_ref[...], ((1,), (1,))))
        solved_ref[:, 0 * WIDTH : 1 * WIDTH] = high
        solved_ref[:, 1 * WIDTH : 2 * WIDTH] = low
        solved_ref[:, 2 * WIDTH : 3 * WIDTH] = high

    at_row = lax.broadcasted_iota(jnp.int32, (TILE, TILE), 0)
    at_col = lax.broadcasted_iota(jnp.int32, (TILE, TILE), 1)

    def rows_of(at):
        last_tile_row = ((at + 1) * tiles_here - 1) * grid_rows + grid_rows - 1
        reach = min(tile_cols, last_tile_row // grid_cols + 1)
        high, low = split(lower_ref[...])
        update = lax.dot_general(
            jnp.concatenate([high, high, low], axis=1),
            solved_ref[: reach * TILE, :],
            (((1,), (1,)), ((), ())),
            preferred_element_type=jnp.float32,
        )
        for t in range(tiles_here):
            tile_row = (at * tiles_here + t) * grid_rows + row_index
            down = slice(t * TILE, (t + 1) * TILE)
            for b in range(reach):
                across = slice(b * TILE, (b + 1) * TILE)
                tile_col = b * grid_cols + col_index
                value = matrix_ref[down, across] - update[down, across]
                keep = tile_row >= tile_col
                if b * grid_cols < PANELS:
                    for p in range(PANELS):
                        panel = lower_ref[down, p * TILE : (p + 1) * TILE]
                        value = jnp.where(tile_col == p, panel, value)
                    inner = (tile_row - tile_col) * TILE + at_row - at_col >= 0
                    keep = inner | ((tile_row == tile_col) & (tile_col >= PANELS))
                out_ref[down, across] = jnp.where(keep, value, 0.0)
        if reach < tile_cols:
            out_ref[:, reach * TILE :] = jnp.zeros((rows_here, cols_count - reach * TILE), jnp.float32)

    for at in range(pl.num_programs(0)):
        pl.when(step == at)(lambda at=at: rows_of(at))


def trailing(grid_rows, grid_cols, place, matrix, lower, cols, inverse):
    rows_count, cols_count = matrix.shape
    rows_step = 2 * TILE
    return pl.pallas_call(
        functools.partial(trailing_kernel, grid_rows, grid_cols),
        grid=(rows_count // rows_step,),
        out_shape=jax.ShapeDtypeStruct(matrix.shape, jnp.float32),
        in_specs=[
            pl.BlockSpec(memory_space=pltpu.SMEM),
            pl.BlockSpec((rows_step, cols_count), lambda t: (t, 0)),
            pl.BlockSpec((rows_step, WIDTH), lambda t: (t, 0)),
            pl.BlockSpec(cols.shape, lambda t: (0, 0, 0, 0, 0)),
            pl.BlockSpec(inverse.shape, lambda t: (0, 0)),
        ],
        out_specs=pl.BlockSpec((rows_step, cols_count), lambda t: (t, 0)),
        scratch_shapes=[pltpu.VMEM((cols_count, 3 * WIDTH), jnp.bfloat16)],
        name="trailing",
    )(place, matrix, lower, cols, inverse)


def exchange(chunks, axis):
    return lax.all_to_all(chunks, axis, 0, 0, tiled=True)


def to_all(part, axis):
    count = lax.axis_size(axis)
    return exchange(jnp.broadcast_to(part[None], (count, *part.shape)), axis)


def on_device(matrix):
    rows_count, cols_count = matrix.shape
    grid_rows = lax.axis_size("row")
    grid_cols = lax.axis_size("col")
    chips = grid_cols // PANELS
    tile_rows, tile_cols = rows_count // TILE, cols_count // TILE
    wraps = grid_cols // grid_rows
    place = jnp.stack([lax.axis_index("row"), lax.axis_index("col")]).astype(jnp.int32)
    with jax.named_scope("scatter_rows"):
        panel = matrix[:, :TILE].reshape(tile_rows, chips, GROUP, TILE).transpose(1, 0, 2, 3)
        same_core = [list(range(p, grid_cols, PANELS)) for p in range(PANELS)]
        piece = lax.all_to_all(panel, "col", 0, 0, tiled=True, axis_index_groups=same_core)[0]
        piece, place = lax.optimization_barrier((piece, place))
    with jax.named_scope("gather_rows"):
        held = to_all(piece, "col")
    with jax.named_scope("gather_planes"):
        planes = lax.all_gather(piece, "row")
        held, planes = lax.optimization_barrier((held, planes))
    with jax.named_scope("spread_diagonal"):
        diag = to_all(planes[:PANELS, 0], "col")
    with jax.named_scope("exchange_cols"):
        diag, planes = lax.optimization_barrier((diag, planes))
        parts = planes.reshape(grid_rows, tile_cols, wraps, GROUP, TILE).transpose(2, 0, 1, 3, 4)
        cols = exchange(parts.reshape(grid_cols, tile_cols, GROUP, TILE), "col")
    inverse, lower = panels(
        diag.reshape(chips, PANELS, *diag.shape[1:]), held.reshape(chips, PANELS, *held.shape[1:])
    )
    cols = cols.reshape(chips, PANELS, *cols.shape[1:])
    return trailing(grid_rows, grid_cols, place, matrix, lower, cols, inverse)


def solution(mesh):
    return jax.shard_map(
        on_device, mesh=mesh, in_specs=(P("row", "col"),), out_specs=P("row", "col"), check_vma=False
    )
```

time: 106 us -> 105 us (level)
  blocking collectives: 74.7 us -> 54.4 us
  starting transfers between devices: 7.44 us -> 18.8 us
  waiting for transfers between devices: 0.01 us -> 8.41 us
  Pallas kernels: 18.9 us -> 17.5 us
    all_to_all x2 -> x1, blocking collectives: 43.6 us -> 22.3 us  [exchange(): return lax.all_to_all(chunks, axis, 0, 0, tiled=True)]
    all_to_all x0 -> x1, waiting for transfers between devices: none -> 8.4 us  [on_device(): lax.all_to_all(panel, 'col', 0, 0, tiled=True, axis_index_groups=same_core)]
    all_to_all x0 -> x1, starting transfers between devices: none -> 7.58 us  [on_device(): lax.all_to_all(panel, 'col', 0, 0, tiled=True, axis_index_groups=same_core)]
    all_to_all x2, starting transfers between devices: 7.44 us -> 11.2 us  [exchange(): return lax.all_to_all(chunks, axis, 0, 0, tiled=True)]
    transpose x0 -> x2, local copies, waits for them, and re-layouts: none -> 1.72 us  [the longest x1 0.87 us: on_device(): planes.reshape(grid_rows, tile_cols, wraps, GROUP, TILE)]
    pallas_call x3 -> x2, Pallas kernels: 18.9 us -> 17.5 us  [the longest x1 12 us: panels(): pl.pallas_call(panels_kernel, out_shape=[jax.ShapeDtypeStruct((WIDTH, WID...]
  transfers between devices with their start and end apart: 2 -> 3, of which waited for: 0 -> 1; matrix products, arithmetic and copies ran while one was open for 1% -> 1% of each run, Pallas kernels for 12% -> 12%
where the time goes in v7:
time: 105 us; the launch traced here: 104 us
  blocking collectives  54.4 us (52%)
  starting transfers between devices  18.8 us (18%)
  Pallas kernels  17.5 us (17%)
  waiting for transfers between devices  8.41 us (8%)
  local copies, waits for them, and re-layouts  4.72 us (4%)
    all_gather x1, blocking collectives, on_device(): planes = lax.all_gather(piece, 'row')  32 us
    all_to_all x1, blocking collectives, exchange(): return lax.all_to_all(chunks, axis, 0, 0, tiled=True)  22.3 us
    pallas_call x1, Pallas kernels, panels(): pl.pallas_call(panels_kernel, out_shape=[jax.ShapeDtypeStruct((WIDTH, WID...  12 us
    all_to_all x2, starting transfers between devices, exchange(): return lax.all_to_all(chunks, axis, 0, 0, tiled=True)  11.2 us
    all_to_all x1, waiting for transfers between devices, on_device(): lax.all_to_all(panel, 'col', 0, 0, tiled=True, axis_index_groups=same_core)  8.4 us
    all_to_all x1, starting transfers between devices, on_device(): lax.all_to_all(panel, 'col', 0, 0, tiled=True, axis_index_groups=same_core)  7.58 us
    pallas_call x1, Pallas kernels, trailing(): pl.pallas_call(functools.partial(trailing_kernel, grid_rows, grid_cols),...  5.44 us
  transfers between devices with their start and end apart: 3, of which 1 were waited for; matrix products, arithmetic and copies ran while one was open for 1% of the time, Pallas kernels for 12%

profile of v7, /device:TPU:1, one launch (start us, length us, event | category | flops | bytes accessed | tf_op | source)
XLA Modules:
  0.0 104.5 jit_solution(12039638590359511770)
XLA Ops:
  0.0 1.1 %slice.9 = f32[1024,128]{1,0:T(8,128)S(1)} slice(f32[1024,512]{1,0:T(8,128)} %matrix_ref.1), slice={[0:1024], [0:128]} | slice | bytes 1048576 | tf_op jit(solution)/shard_map/scatter_rows/slice | solution.py:229
  1.1 0.8 copy.8
  1.9 7.6 %all-to-all-start = ((f32[16,8,8,128]{3,2,1,0:T(8,128)}), f32[16,8,8,128]{3,2,1,0:T(8,128)S(1)}, u32[]{:S(2)}, u32[]{:S(2)}) async-start(f32[16,8,8,128]{3,2,1,0:T(8,128)} %copy.8), calls=%async_computation | async-start | bytes 1048576 | tf_op jit(solution)/shard_map/scatter_rows/all_to_all | solution.py:231
  9.5 0.7 pad_add_fusion.place_ref
  10.2 8.4 %all-to-all-done = f32[16,8,8,128]{3,2,1,0:T(8,128)S(1)} async-done(((f32[16,8,8,128]{3,2,1,0:T(8,128)}), f32[16,8,8,128]{3,2,1,0:T(8,128)S(1)}, u32[]{:S(2)}, u32[]{:S(2)}) %all-to-all-start) | async-done | bytes 524320 | tf_op jit(solution)/shard_map/scatter_rows/all_to_all | solution.py:231
  18.6 1.1 %broadcast_in_dim.15 = f32[32,8,8,128]{3,2,1,0:T(8,128)} broadcast(f32[8,8,128]{2,1,0:T(8,128)S(1)} %slice_bitcast_fusion), dimensions={1,2,3} | broadcast | bytes 1081344 | tf_op jit(solution)/shard_map/gather_rows/broadcast_in_dim | solution.py:217
  19.7 7.4 %all-to-all-start.1 = ((f32[32,8,8,128]{3,2,1,0:T(8,128)}), f32[32,8,8,128]{3,2,1,0:T(8,128)S(1)}, u32[]{:S(2)}, u32[]{:S(2)}) async-start(f32[32,8,8,128]{3,2,1,0:T(8,128)} %broadcast_in_dim.15), calls=%async_computation.1 | async-start | bytes 2097152 | tf_op jit(solution)/shard_map/gather_rows/all_to_all | solution.py:212
  27.1 32.0 %all-gather = f32[128,8,128]{2,1,0:T(8,128)S(1)} all-gather(f32[8,8,128]{2,1,0:T(8,128)S(1)} %slice_bitcast_fusion), channel_id=2, replica_groups=mesh['row'=16,'col'=32] {'row'}, dimensions={0}, use_global_device_ids=true | all-gather | bytes 557056 | tf_op jit(solution)/shard_map/gather_planes/all_gather | solution.py:236
  59.1 0.0 all-to-all-done.1
  59.2 0.0 copy-start.1
  59.2 22.3 %all_to_all.20 = f32[32,2,8,128]{3,2,1,0:T(8,128)} all-to-all(f32[32,2,8,128]{3,2,1,0:T(8,128)S(1)} %broadcast_in_dim.18), channel_id=1, replica_groups=mesh['row'=16,'col'=32] {'col'}, dimensions={0} | all-to-all | bytes 524288 | tf_op jit(solution)/shard_map/spread_diagonal/all_to_all | solution.py:212
  81.5 0.9 copy.9
  82.4 3.7 %all-to-all-start.3 = ((f32[32,4,8,128]{3,2,1,0:T(8,128)}), f32[32,4,8,128]{3,2,1,0:T(8,128)S(1)}, u32[]{:S(2)}, u32[]{:S(2)}) async-start(f32[32,4,8,128]{3,2,1,0:T(8,128)} %bitcast.11), calls=%async_computation.3 | async-start | bytes 1048576 | tf_op jit(solution)/shard_map/exchange_cols/all_to_all | solution.py:212
  86.1 0.0 copy-done.1
  86.1 12.0 %panels.1 = (f32[256,256]{1,0:T(8,128)}, f32[1024,256]{1,0:T(8,128)}) custom-call(f32[16,2,2,8,128]{4,3,2,1,0:T(8,128)} %bitcast.22, f32[16,2,8,8,128]{4,3,2,1,0:T(8,128)} %bitcast.21), custom_call_target="tpu_custom_call" | custom-call | flops 872415232 | bytes 2883584 | tf_op jit(solution)/shard_map/panels/pallas_call | solution.py:110
  98.2 0.0 all-to-all-done.3
  98.2 0.0 copy-start
  98.2 0.8 copy-done
  99.0 5.4 %trailing.1 = f32[1024,512]{1,0:T(8,128)} custom-call(s32[2]{0:T(128)} %pad_add_fusion.place_ref, f32[1024,512]{1,0:T(8,128)} %matrix_ref.1, f32[1024,256]{1,0:T(8,128)} %get-tuple-element.18.lower_ref, f32[16,2,4,8,128]{4,3,2,1,0:T(8,128)} %bitcast.19, f32[256,256]{1,0:T(8,128)} %get-tuple-element.20.inverse_ref), custom_call_target="tpu_custom_call" | custom-call | tf_op jit(solution)/shard_map/trailing/pallas_call | solution.py:194
  (3 shorter events, 0.0 us)
Async XLA Ops:
  1.9 16.7 %all-to-all-start = ((f32[16,8,8,128]{3,2,1,0:T(8,128)}), f32[16,8,8,128]{3,2,1,0:T(8,128)S(1)}, u32[]{:S(2)}, u32[]{:S(2)}) async-start(f32[16,8,8,128]{3,2,1,0:T(8,128)} %copy.8), calls=%async_computation | async-start | bytes 1048576 | tf_op jit(solution)/shard_map/scatter_rows/all_to_all | solution.py:231
  19.7 39.5 %all-to-all-start.1 = ((f32[32,8,8,128]{3,2,1,0:T(8,128)}), f32[32,8,8,128]{3,2,1,0:T(8,128)S(1)}, u32[]{:S(2)}, u32[]{:S(2)}) async-start(f32[32,8,8,128]{3,2,1,0:T(8,128)} %broadcast_in_dim.15), calls=%async_computation.1 | async-start | bytes 2097152 | tf_op jit(solution)/shard_map/gather_rows/all_to_all | solution.py:212
  59.2 27.0 %copy-start.1 = (f32[32,8,8,128]{3,2,1,0:T(8,128)}, f32[32,8,8,128]{3,2,1,0:T(8,128)S(1)}, u32[]{:S(2)}) copy-start(f32[32,8,8,128]{3,2,1,0:T(8,128)S(1)} %all-to-all-done.1) | copy-start | bytes 3145732
  82.4 15.8 %all-to-all-start.3 = ((f32[32,4,8,128]{3,2,1,0:T(8,128)}), f32[32,4,8,128]{3,2,1,0:T(8,128)S(1)}, u32[]{:S(2)}, u32[]{:S(2)}) async-start(f32[32,4,8,128]{3,2,1,0:T(8,128)} %bitcast.11), calls=%async_computation.3 | async-start | bytes 1048576 | tf_op jit(solution)/shard_map/exchange_cols/all_to_all | solution.py:212
  98.2 0.8 copy-start

commit v8 on v7

--- a/solution.py
+++ b/solution.py
@@ -12,6 +12,7 @@
 WIDTH = TILE * PANELS
 STRIP = 64
 GROUP = 8
+STEP = 2
 HIGHEST = lax.Precision.HIGHEST
 
 
@@ -65,8 +66,10 @@
     return jnp.concatenate(scaled, axis=0)
 
 
-def panels_kernel(diag_ref, held_ref, inverse_ref, lower_ref, work_ref, raw_ref, sem):
-    fetch = pltpu.make_async_copy(held_ref, raw_ref, sem)
+def panels_kernel(
+    wraps, diag_ref, held_ref, inverse_ref, lower_hbm_ref, work_ref, raw_ref, lower_ref, sems
+):
+    fetch = pltpu.make_async_copy(held_ref, raw_ref, sems.at[0])
     fetch.start()
     for p in range(PANELS):
         for q in range(PANELS):
@@ -76,6 +79,8 @@
     at_col = lax.broadcasted_iota(jnp.int32, (WIDTH, WIDTH), 1)
     inverse_ref[...] = jnp.where(at_row == at_col, 1.0, 0.0).astype(jnp.float32)
     tile_rows = lower_ref.shape[0] // TILE
+    sends = []
+    order = [t % wraps * (tile_rows // wraps) + t // wraps for t in range(tile_rows)]
     for start in range(0, WIDTH, STRIP):
         stop = start + STRIP
         first = start // TILE * TILE
@@ -96,83 +101,99 @@
             raw = jnp.concatenate(
                 [
                     jnp.concatenate(
-                        [raw_ref[:, p, t].reshape(TILE, TILE) for t in range(tile_rows)], axis=0
+                        [raw_ref[:, p, at].reshape(TILE, TILE) for at in order], axis=0
                     )
                     for p in range(done // TILE)
                 ],
                 axis=1,
             )
             lower_ref[:, first:done] = product(raw, inverse_ref[first:done, :done], ((1,), (1,)))
-
-
-def panels(diag, held):
+            send = pltpu.make_async_copy(
+                lower_ref.at[:, first:done], lower_hbm_ref.at[:, first:done], sems.at[done // TILE]
+            )
+            send.start()
+            sends.append(send)
+    for send in sends:
+        send.wait()
+
+
+def in_vmem(*arrays):
+    return [pltpu.with_memory_space_constraint(x, pltpu.VMEM) for x in arrays]
+
+
+def panels(wraps, diag, held):
     count = held.shape[0] * held.shape[2] * GROUP
+    vmem = pl.BlockSpec(memory_space=pltpu.VMEM)
     return pl.pallas_call(
-        panels_kernel,
+        functools.partial(panels_kernel, wraps),
         out_shape=[
-            jax.ShapeDtypeStruct((WIDTH, WIDTH), jnp.float32),
-            jax.ShapeDtypeStruct((count, WIDTH), jnp.float32),
-        ],
-        in_specs=[pl.BlockSpec(memory_space=pltpu.VMEM), pl.BlockSpec(memory_space=pl.ANY)],
+            pltpu.VMEM((WIDTH, WIDTH), jnp.float32),
+            pltpu.HBM((count, WIDTH), jnp.float32),
+        ],
+        in_specs=[vmem, pl.BlockSpec(memory_space=pltpu.HBM)],
+        out_specs=[vmem, pl.BlockSpec(memory_space=pltpu.HBM)],
         scratch_shapes=[
             pltpu.VMEM((WIDTH, WIDTH), jnp.float32),
             pltpu.VMEM(held.shape, jnp.float32),
-            pltpu.SemaphoreType.DMA,
+            pltpu.VMEM((count, WIDTH), jnp.float32),
+            pltpu.SemaphoreType.DMA((1 + PANELS,)),
         ],
         cost_estimate=pl.CostEstimate(
             flops=4 * WIDTH**3 + 12 * count * WIDTH**2,
             bytes_accessed=12 * WIDTH**2 + 8 * count * WIDTH,
             transcendentals=0,
         ),
+        compiler_params=pltpu.CompilerParams(vmem_limit_bytes=32 * 2**20),
         name="panels",
-    )(diag, held)
+    )(*in_vmem(diag), pltpu.with_memory_space_constraint(held, pltpu.HBM))
 
 
 def trailing_kernel(
-    grid_rows, grid_cols, place_ref, matrix_ref, lower_ref, cols_ref, inverse_ref, out_ref, solved_ref
+    grid_rows, grid_cols, place_ref, matrix_ref, lower_hbm_ref, cols_ref, inverse_ref, out_ref, lower_ref, done_ref, sems
 ):
-    step = pl.program_id(0)
+    fetch = pltpu.make_async_copy(lower_hbm_ref, lower_ref, sems.at[0])
+    fetch.start()
     row_index, col_index = place_ref[0], place_ref[1]
-    rows_here, cols_count = matrix_ref.shape
-    tile_cols = cols_count // TILE
-    tiles_here = rows_here // TILE
-
-    @pl.when(step == 0)
-    def _():
-        raw = jnp.concatenate(
-            [
-                jnp.concatenate(
-                    [cols_ref[:, p, b].reshape(TILE, TILE) for b in range(tile_cols)], axis=0
-                )
-                for p in range(PANELS)
-            ],
-            axis=1,
-        )
-        high, low = split(product(raw, inverse_ref[...], ((1,), (1,))))
-        solved_ref[:, 0 * WIDTH : 1 * WIDTH] = high
-        solved_ref[:, 1 * WIDTH : 2 * WIDTH] = low
-        solved_ref[:, 2 * WIDTH : 3 * WIDTH] = high
-
+    rows_count, cols_count = matrix_ref.shape
+    tile_rows, tile_cols = rows_count // TILE, cols_count // TILE
+    raw = jnp.concatenate(
+        [
+            jnp.concatenate(
+                [
+                    cols_ref[:, p, wrap, b].reshape(-1, TILE)
+                    for b in range(tile_cols)
+                    for wrap in range(cols_ref.shape[2])
+                ],
+                axis=0,
+            )
+            for p in range(PANELS)
+        ],
+        axis=1,
+    )
+    high, low = split(product(raw, inverse_ref[...], ((1,), (1,))))
+    solved = jnp.concatenate([high, low, high], axis=1)
+    fetch.wait()
     at_row = lax.broadcasted_iota(jnp.int32, (TILE, TILE), 0)
     at_col = lax.broadcasted_iota(jnp.int32, (TILE, TILE), 1)
-
-    def rows_of(at):
-        last_tile_row = ((at + 1) * tiles_here - 1) * grid_rows + grid_rows - 1
+    sends = []
+    for step in reversed(range(tile_rows // STEP)):
+        span = slice(step * STEP * TILE, (step + 1) * STEP * TILE)
+        last_tile_row = ((step + 1) * STEP - 1) * grid_rows + grid_rows - 1
         reach = min(tile_cols, last_tile_row // grid_cols + 1)
-        high, low = split(lower_ref[...])
+        high, low = split(lower_ref[span, :])
         update = lax.dot_general(
             jnp.concatenate([high, high, low], axis=1),
-            solved_ref[: reach * TILE, :],
+            solved[: reach * TILE],
             (((1,), (1,)), ((), ())),
             preferred_element_type=jnp.float32,
         )
-        for t in range(tiles_here):
-            tile_row = (at * tiles_here + t) * grid_rows + row_index
-            down = slice(t * TILE, (t + 1) * TILE)
+        for t in range(STEP):
+            tile_row = (step * STEP + t) * grid_rows + row_index
+            down = slice((step * STEP + t) * TILE, (step * STEP + t + 1) * TILE)
             for b in range(reach):
                 across = slice(b * TILE, (b + 1) * TILE)
                 tile_col = b * grid_cols + col_index
-                value = matrix_ref[down, across] - update[down, across]
+                value = matrix_ref[down, across] - update[t * TILE : (t + 1) * TILE, across]
                 keep = tile_row >= tile_col
                 if b * grid_cols < PANELS:
                     for p in range(PANELS):
@@ -180,30 +201,38 @@
                         value = jnp.where(tile_col == p, panel, value)
                     inner = (tile_row - tile_col) * TILE + at_row - at_col >= 0
                     keep = inner | ((tile_row == tile_col) & (tile_col >= PANELS))
-                out_ref[down, across] = jnp.where(keep, value, 0.0)
+                done_ref[down, across] = jnp.where(keep, value, 0.0)
         if reach < tile_cols:
-            out_ref[:, reach * TILE :] = jnp.zeros((rows_here, cols_count - reach * TILE), jnp.float32)
-
-    for at in range(pl.num_programs(0)):
-        pl.when(step == at)(lambda at=at: rows_of(at))
+            beyond = slice(reach * TILE, cols_count)
+            done_ref[span, beyond] = jnp.zeros((STEP * TILE, cols_count - reach * TILE), jnp.float32)
+        send = pltpu.make_async_copy(done_ref.at[span], out_ref.at[span], sems.at[step + 1])
+        send.start()
+        sends.append(send)
+    for send in sends:
+        send.wait()
 
 
 def trailing(grid_rows, grid_cols, place, matrix, lower, cols, inverse):
-    rows_count, cols_count = matrix.shape
-    rows_step = 2 * TILE
+    vmem = pl.BlockSpec(memory_space=pltpu.VMEM)
+    matrix, cols, inverse = in_vmem(matrix, cols, inverse)
+    lower = pltpu.with_memory_space_constraint(lower, pltpu.HBM)
     return pl.pallas_call(
         functools.partial(trailing_kernel, grid_rows, grid_cols),
-        grid=(rows_count // rows_step,),
         out_shape=jax.ShapeDtypeStruct(matrix.shape, jnp.float32),
         in_specs=[
             pl.BlockSpec(memory_space=pltpu.SMEM),
-            pl.BlockSpec((rows_step, cols_count), lambda t: (t, 0)),
-            pl.BlockSpec((rows_step, WIDTH), lambda t: (t, 0)),
-            pl.BlockSpec(cols.shape, lambda t: (0, 0, 0, 0, 0)),
-            pl.BlockSpec(inverse.shape, lambda t: (0, 0)),
-        ],
-        out_specs=pl.BlockSpec((rows_step, cols_count), lambda t: (t, 0)),
-        scratch_shapes=[pltpu.VMEM((cols_count, 3 * WIDTH), jnp.bfloat16)],
+            vmem,
+            pl.BlockSpec(memory_space=pltpu.HBM),
+            vmem,
+            vmem,
+        ],
+        out_specs=pl.BlockSpec(memory_space=pl.ANY),
+        scratch_shapes=[
+            pltpu.VMEM(lower.shape, jnp.float32),
+            pltpu.VMEM(matrix.shape, jnp.float32),
+            pltpu.SemaphoreType.DMA((matrix.shape[0] // (STEP * TILE) + 1,)),
+        ],
+        compiler_params=pltpu.CompilerParams(vmem_limit_bytes=32 * 2**20),
         name="trailing",
     )(place, matrix, lower, cols, inverse)
 
@@ -222,14 +251,14 @@
     grid_rows = lax.axis_size("row")
     grid_cols = lax.axis_size("col")
     chips = grid_cols // PANELS
-    tile_rows, tile_cols = rows_count // TILE, cols_count // TILE
+    tile_cols = cols_count // TILE
     wraps = grid_cols // grid_rows
     place = jnp.stack([lax.axis_index("row"), lax.axis_index("col")]).astype(jnp.int32)
     with jax.named_scope("scatter_rows"):
-        panel = matrix[:, :TILE].reshape(tile_rows, chips, GROUP, TILE).transpose(1, 0, 2, 3)
+        panel = matrix[:, :TILE].reshape(tile_cols, wraps, chips, GROUP, TILE)
+        panel = panel.transpose(2, 1, 0, 3, 4).reshape(chips, wraps * tile_cols, GROUP, TILE)
         same_core = [list(range(p, grid_cols, PANELS)) for p in range(PANELS)]
         piece = lax.all_to_all(panel, "col", 0, 0, tiled=True, axis_index_groups=same_core)[0]
-        piece, place = lax.optimization_barrier((piece, place))
     with jax.named_scope("gather_rows"):
         held = to_all(piece, "col")
     with jax.named_scope("gather_planes"):
@@ -239,12 +268,15 @@
         diag = to_all(planes[:PANELS, 0], "col")
     with jax.named_scope("exchange_cols"):
         diag, planes = lax.optimization_barrier((diag, planes))
-        parts = planes.reshape(grid_rows, tile_cols, wraps, GROUP, TILE).transpose(2, 0, 1, 3, 4)
-        cols = exchange(parts.reshape(grid_cols, tile_cols, GROUP, TILE), "col")
+        parts = planes.reshape(grid_cols, tile_cols, GROUP, TILE)
+        by_plane = [w * grid_rows + q for q in range(grid_rows) for w in range(wraps)]
+        cols = lax.all_to_all(parts, "col", 0, 0, tiled=True, axis_index_groups=[by_plane])
+        cols = cols.reshape(grid_rows // PANELS, PANELS, wraps, *cols.shape[1:])
     inverse, lower = panels(
-        diag.reshape(chips, PANELS, *diag.shape[1:]), held.reshape(chips, PANELS, *held.shape[1:])
-    )
-    cols = cols.reshape(chips, PANELS, *cols.shape[1:])
+        wraps,
+        diag.reshape(chips, PANELS, *diag.shape[1:]),
+        held.reshape(chips, PANELS, *held.shape[1:]),
+    )
     return trailing(grid_rows, grid_cols, place, matrix, lower, cols, inverse)
 
 

time: 105 us -> 104 us (level)
  blocking collectives: 54.4 us -> 73.7 us
  starting transfers between devices: 18.8 us -> 10.7 us
  waiting for transfers between devices: 8.41 us -> 0.48 us
  Pallas kernels: 17.5 us -> 15.1 us
  local copies, waits for them, and re-layouts: 4.72 us -> 2.95 us
    all_to_all x0 -> x1, blocking collectives: none -> 16.6 us  [on_device(): lax.all_to_all(panel, 'col', 0, 0, tiled=True, axis_index_groups=same_core)]
    all_to_all x1, waiting for transfers between devices: 8.4 us -> 0.48 us  [on_device(): lax.all_to_all(parts, 'col', 0, 0, tiled=True, axis_index_groups=[by_plane])]
    all_to_all x2 -> x1, starting transfers between devices: 11.2 us -> 6.81 us  [exchange(): return lax.all_to_all(chunks, axis, 0, 0, tiled=True)]
    all_to_all x1, starting transfers between devices: 7.58 us -> 3.87 us  [on_device(): lax.all_to_all(parts, 'col', 0, 0, tiled=True, axis_index_groups=[by_plane])]
    all_gather x1, blocking collectives: 32 us -> 34.3 us  [on_device(): planes = lax.all_gather(piece, 'row')]
    transpose x2 -> x1, local copies, waits for them, and re-layouts: 1.72 us -> 0.05 us  [on_device(): panel.transpose(2, 1, 0, 3, 4)]
    pallas_call x1, Pallas kernels: 5.44 us -> 4.15 us  [trailing(): pl.pallas_call(functools.partial(trailing_kernel, grid_rows, grid_cols),...]
    pallas_call x1, Pallas kernels: 12 us -> 11 us  [panels(): pl.pallas_call(functools.partial(panels_kernel, wraps), out_shape=[pltpu....]
  transfers between devices with their start and end apart: 3 -> 2, of which waited for: 1 -> 1; matrix products, arithmetic and copies ran while one was open for 1% -> 0% of each run, Pallas kernels for 12% -> 11%
where the time goes in v8:
time: 104 us; the launch traced here: 103 us
  blocking collectives  73.7 us (71%)
  Pallas kernels  15.1 us (15%)
  starting transfers between devices  10.7 us (10%)
  local copies, waits for them, and re-layouts  2.95 us (3%)
    all_gather x1, blocking collectives, on_device(): planes = lax.all_gather(piece, 'row')  34.3 us
    all_to_all x1, blocking collectives, exchange(): return lax.all_to_all(chunks, axis, 0, 0, tiled=True)  22.8 us
    all_to_all x1, blocking collectives, on_device(): lax.all_to_all(panel, 'col', 0, 0, tiled=True, axis_index_groups=same_core)  16.6 us
    pallas_call x1, Pallas kernels, panels(): pl.pallas_call(functools.partial(panels_kernel, wraps), out_shape=[pltpu....  11 us
    all_to_all x1, starting transfers between devices, exchange(): return lax.all_to_all(chunks, axis, 0, 0, tiled=True)  6.81 us
    pallas_call x1, Pallas kernels, trailing(): pl.pallas_call(functools.partial(trailing_kernel, grid_rows, grid_cols),...  4.15 us
    all_to_all x1, starting transfers between devices, on_device(): lax.all_to_all(parts, 'col', 0, 0, tiled=True, axis_index_groups=[by_plane])  3.87 us
  transfers between devices with their start and end apart: 2, of which 1 were waited for; matrix products, arithmetic and copies ran while one was open for 0% of the time, Pallas kernels for 11%

profile of v8, /device:TPU:1, one launch (start us, length us, event | category | flops | bytes accessed | tf_op | source)
XLA Modules:
  0.0 103.1 jit_solution(6486306657757603482)
XLA Ops:
  0.0 1.1 %slice.9 = f32[1024,128]{1,0:T(8,128)S(1)} slice(f32[1024,512]{1,0:T(8,128)} %matrix_ref.1), slice={[0:1024], [0:128]} | slice | bytes 1048576 | tf_op jit(solution)/shard_map/scatter_rows/slice | solution.py:258
  1.1 0.1 copy.3
  1.1 16.6 %all_to_all.20 = f32[16,8,8,128]{3,2,1,0:T(8,128)S(1)} all-to-all(f32[16,8,8,128]{3,2,1,0:T(8,128)S(1)} %bitcast.16), channel_id=1, replica_groups={{0,2,4,6,8,10,12,14,16,18,20,22,24,26,28,30},{1,3,5,7,9,11,13,15,17,19,..., dimensions={0} | all-to-all | bytes 1048576 | tf_op jit(solution)/shard_map/scatter_rows/all_to_all | solution.py:261
  17.7 1.1 %broadcast_in_dim.15 = f32[32,8,8,128]{3,2,1,0:T(8,128)} broadcast(f32[8,8,128]{2,1,0:T(8,128)S(1)} %get-tuple-element.18), dimensions={1,2,3} | broadcast | bytes 1081344 | tf_op jit(solution)/shard_map/gather_rows/broadcast_in_dim | solution.py:246
  18.8 6.8 %all-to-all-start.1 = ((f32[32,8,8,128]{3,2,1,0:T(8,128)}), f32[32,8,8,128]{3,2,1,0:T(8,128)S(1)}, u32[]{:S(2)}, u32[]{:S(2)}) async-start(f32[32,8,8,128]{3,2,1,0:T(8,128)} %broadcast_in_dim.15), calls=%async_computation.1 | async-start | bytes 2097152 | tf_op jit(solution)/shard_map/gather_rows/all_to_all | solution.py:241
  25.7 34.3 %all_gather.3 = f32[16,8,8,128]{3,2,1,0:T(8,128)} all-gather(f32[1,8,8,128]{3,2,1,0:T(8,128)S(1)} %get-tuple-element.17), channel_id=1, replica_groups=mesh['row'=16,'col'=32] {'row'}, dimensions={0}, use_global_device_ids=true | all-gather | bytes 557056 | tf_op jit(solution)/shard_map/gather_planes/all_gather | solution.py:265
  60.0 0.0 all-to-all-done.1
  60.0 0.0 copy-start.1
  60.0 0.7 slice_bitcast_fusion
  60.7 22.8 %all_to_all.21 = f32[32,2,8,128]{3,2,1,0:T(8,128)S(1)} all-to-all(f32[32,2,8,128]{3,2,1,0:T(8,128)S(1)} %broadcast_in_dim.17), channel_id=1, replica_groups=mesh['row'=16,'col'=32] {'col'}, dimensions={0} | all-to-all | bytes 524288 | tf_op jit(solution)/shard_map/spread_diagonal/all_to_all | solution.py:241
  83.5 0.0 copy-done.1
  83.5 0.0 copy-start
  83.5 3.9 %all-to-all-start.3 = ((f32[32,4,8,128]{3,2,1,0:T(8,128)}), f32[32,4,8,128]{3,2,1,0:T(8,128)S(1)}, u32[]{:S(2)}, u32[]{:S(2)}) async-start(f32[32,4,8,128]{3,2,1,0:T(8,128)} %bitcast.9), calls=%async_computation.3 | async-start | bytes 1048576 | tf_op jit(solution)/shard_map/exchange_cols/all_to_all | solution.py:273
  87.4 0.1 pad_add_fusion.place_ref
  87.5 11.0 %panels.1 = (f32[256,256]{1,0:T(8,128)S(1)}, f32[1024,256]{1,0:T(8,128)}) custom-call(f32[16,2,2,8,128]{4,3,2,1,0:T(8,128)S(1)} %bitcast.15, f32[16,2,8,8,128]{4,3,2,1,0:T(8,128)} %bitcast.18), custom_call_target="tpu_custom_call" | custom-call | flops 872415232 | bytes 2883584 | tf_op jit(solution)/shard_map/panels/pallas_call | solution.py:127
  98.5 0.5 all-to-all-done.3
  99.0 0.0 copy-done
  99.0 4.1 %trailing.1 = f32[1024,512]{1,0:T(8,128)} custom-call(s32[2]{0:T(128)S(1)} %pad_add_fusion.place_ref, f32[1024,512]{1,0:T(8,128)S(1)} %copy-done, f32[1024,256]{1,0:T(8,128)} %get-tuple-element.14.lower_hbm_ref, f32[8,2,2,4,8,128]{5,4,3,2,1,0:T(8,128)S(1)} %bitcast.14, f32[256,256]{1,0:T(8,128)S(1)} %get-tuple-element.16.inverse_ref), custom_call_target="tpu_custom_call" | custom-call | tf_op jit(solution)/shard_map/trailing/pallas_call | solution.py:219
  (2 shorter events, 0.0 us)
Async XLA Ops:
  18.8 41.2 %all-to-all-start.1 = ((f32[32,8,8,128]{3,2,1,0:T(8,128)}), f32[32,8,8,128]{3,2,1,0:T(8,128)S(1)}, u32[]{:S(2)}, u32[]{:S(2)}) async-start(f32[32,8,8,128]{3,2,1,0:T(8,128)} %broadcast_in_dim.15), calls=%async_computation.1 | async-start | bytes 2097152 | tf_op jit(solution)/shard_map/gather_rows/all_to_all | solution.py:241
  60.0 23.5 %copy-start.1 = (f32[32,8,8,128]{3,2,1,0:T(8,128)}, f32[32,8,8,128]{3,2,1,0:T(8,128)S(1)}, u32[]{:S(2)}) copy-start(f32[32,8,8,128]{3,2,1,0:T(8,128)S(1)} %all-to-all-done.1) | copy-start | bytes 3145732
  83.5 15.4 %copy-start = (f32[1024,512]{1,0:T(8,128)S(1)}, f32[1024,512]{1,0:T(8,128)}, u32[]{:S(2)}) copy-start(f32[1024,512]{1,0:T(8,128)} %matrix_ref.1) | copy-start | bytes 6291460
  83.5 15.4 %all-to-all-start.3 = ((f32[32,4,8,128]{3,2,1,0:T(8,128)}), f32[32,4,8,128]{3,2,1,0:T(8,128)S(1)}, u32[]{:S(2)}, u32[]{:S(2)}) async-start(f32[32,4,8,128]{3,2,1,0:T(8,128)} %bitcast.9), calls=%async_computation.3 | async-start | bytes 1048576 | tf_op jit(solution)/shard_map/exchange_cols/all_to_all | solution.py:273

commit v9 on v8

--- a/solution.py
+++ b/solution.py
@@ -67,10 +67,15 @@
 
 
 def panels_kernel(
-    wraps, diag_ref, held_ref, inverse_ref, lower_hbm_ref, work_ref, raw_ref, lower_ref, sems
+    wraps, place_ref, diag_ref, own_ref, other_ref, inverse_ref, lower_hbm_ref, work_ref, raw_ref, lower_ref, sems
 ):
-    fetch = pltpu.make_async_copy(held_ref, raw_ref, sems.at[0])
-    fetch.start()
+    core = lax.rem(place_ref[1], PANELS)
+    fetches = [
+        pltpu.make_async_copy(own_ref, raw_ref.at[core], sems.at[PANELS]),
+        pltpu.make_async_copy(other_ref, raw_ref.at[PANELS - 1 - core], sems.at[PANELS + 1]),
+    ]
+    for fetch in fetches:
+        fetch.start()
     for p in range(PANELS):
         for q in range(PANELS):
             part = diag_ref[:, q, p].reshape(TILE, TILE)
@@ -97,11 +102,12 @@
             inverse_ref[stop:, :done] = inverse_ref[stop:, :done] - update[:, upper:]
         if stop % TILE == 0:
             if first == 0:
-                fetch.wait()
+                for fetch in fetches:
+                    fetch.wait()
             raw = jnp.concatenate(
                 [
                     jnp.concatenate(
-                        [raw_ref[:, p, at].reshape(TILE, TILE) for at in order], axis=0
+                        [raw_ref[p, :, at].reshape(TILE, TILE) for at in order], axis=0
                     )
                     for p in range(done // TILE)
                 ],
@@ -109,7 +115,7 @@
             )
             lower_ref[:, first:done] = product(raw, inverse_ref[first:done, :done], ((1,), (1,)))
             send = pltpu.make_async_copy(
-                lower_ref.at[:, first:done], lower_hbm_ref.at[:, first:done], sems.at[done // TILE]
+                lower_ref.at[:, first:done], lower_hbm_ref.at[:, first:done], sems.at[first // TILE]
             )
             send.start()
             sends.append(send)
@@ -121,8 +127,13 @@
     return [pltpu.with_memory_space_constraint(x, pltpu.VMEM) for x in arrays]
 
 
-def panels(wraps, diag, held):
-    count = held.shape[0] * held.shape[2] * GROUP
+def in_hbm(*arrays):
+    return [pltpu.with_memory_space_constraint(x, pltpu.HBM) for x in arrays]
+
+
+def panels(wraps, place, diag, own, other):
+    count = own.shape[0] * own.shape[1] * GROUP
+    hbm = pl.BlockSpec(memory_space=pltpu.HBM)
     vmem = pl.BlockSpec(memory_space=pltpu.VMEM)
     return pl.pallas_call(
         functools.partial(panels_kernel, wraps),
@@ -130,13 +141,13 @@
             pltpu.VMEM((WIDTH, WIDTH), jnp.float32),
             pltpu.HBM((count, WIDTH), jnp.float32),
         ],
-        in_specs=[vmem, pl.BlockSpec(memory_space=pltpu.HBM)],
-        out_specs=[vmem, pl.BlockSpec(memory_space=pltpu.HBM)],
+        in_specs=[pl.BlockSpec(memory_space=pltpu.SMEM), vmem, hbm, hbm],
+        out_specs=[vmem, hbm],
         scratch_shapes=[
             pltpu.VMEM((WIDTH, WIDTH), jnp.float32),
-            pltpu.VMEM(held.shape, jnp.float32),
+            pltpu.VMEM((PANELS, *own.shape), jnp.float32),
             pltpu.VMEM((count, WIDTH), jnp.float32),
-            pltpu.SemaphoreType.DMA((1 + PANELS,)),
+            pltpu.SemaphoreType.DMA((2 * PANELS,)),
         ],
         cost_estimate=pl.CostEstimate(
             flops=4 * WIDTH**3 + 12 * count * WIDTH**2,
@@ -145,7 +156,7 @@
         ),
         compiler_params=pltpu.CompilerParams(vmem_limit_bytes=32 * 2**20),
         name="panels",
-    )(*in_vmem(diag), pltpu.with_memory_space_constraint(held, pltpu.HBM))
+    )(place, *in_vmem(diag), *in_hbm(own, other))
 
 
 def trailing_kernel(
@@ -215,7 +226,7 @@
 def trailing(grid_rows, grid_cols, place, matrix, lower, cols, inverse):
     vmem = pl.BlockSpec(memory_space=pltpu.VMEM)
     matrix, cols, inverse = in_vmem(matrix, cols, inverse)
-    lower = pltpu.with_memory_space_constraint(lower, pltpu.HBM)
+    (lower,) = in_hbm(lower)
     return pl.pallas_call(
         functools.partial(trailing_kernel, grid_rows, grid_cols),
         out_shape=jax.ShapeDtypeStruct(matrix.shape, jnp.float32),
@@ -260,23 +271,23 @@
         same_core = [list(range(p, grid_cols, PANELS)) for p in range(PANELS)]
         piece = lax.all_to_all(panel, "col", 0, 0, tiled=True, axis_index_groups=same_core)[0]
     with jax.named_scope("gather_rows"):
-        held = to_all(piece, "col")
+        copies = jnp.broadcast_to(piece[None], (chips, *piece.shape))
+        own = lax.all_to_all(copies, "col", 0, 0, tiled=True, axis_index_groups=same_core)
     with jax.named_scope("gather_planes"):
-        planes = lax.all_gather(piece, "row")
-        held, planes = lax.optimization_barrier((held, planes))
+        planes = lax.all_gather(piece, "row", tiled=True)
+        own, planes = lax.optimization_barrier((own, planes))
+        planes = planes.reshape(grid_rows, *piece.shape)
+    with jax.named_scope("swap_panels"):
+        other = lax.ppermute(own, "col", [(c, c ^ 1) for c in range(grid_cols)])
     with jax.named_scope("spread_diagonal"):
         diag = to_all(planes[:PANELS, 0], "col")
     with jax.named_scope("exchange_cols"):
         diag, planes = lax.optimization_barrier((diag, planes))
-        parts = planes.reshape(grid_cols, tile_cols, GROUP, TILE)
-        by_plane = [w * grid_rows + q for q in range(grid_rows) for w in range(wraps)]
-        cols = lax.all_to_all(parts, "col", 0, 0, tiled=True, axis_index_groups=[by_plane])
-        cols = cols.reshape(grid_rows // PANELS, PANELS, wraps, *cols.shape[1:])
-    inverse, lower = panels(
-        wraps,
-        diag.reshape(chips, PANELS, *diag.shape[1:]),
-        held.reshape(chips, PANELS, *held.shape[1:]),
-    )
+        parts = planes.reshape(grid_rows, wraps, tile_cols, GROUP, TILE).swapaxes(0, 1)
+        cols = exchange(parts.reshape(grid_cols, tile_cols, GROUP, TILE), "col")
+        cols = cols.reshape(chips, PANELS, 1, *cols.shape[1:])
+    diag = diag.reshape(chips, PANELS, *diag.shape[1:])
+    inverse, lower = panels(wraps, place, diag, own, other)
     return trailing(grid_rows, grid_cols, place, matrix, lower, cols, inverse)
 
 

time: 104 us -> 102 us (0.981)
  blocking collectives: 73.7 us -> 49.1 us
  starting transfers between devices: 10.7 us -> 25.7 us
  waiting for transfers between devices: 0.48 us -> 6.96 us
    all_to_all x1 -> x0, blocking collectives: 22.8 us -> none  [exchange(): return lax.all_to_all(chunks, axis, 0, 0, tiled=True)]
    all_to_all x1 -> x2, starting transfers between devices: 6.81 us -> 20 us  [exchange(): return lax.all_to_all(chunks, axis, 0, 0, tiled=True)]
    all_to_all x1 -> x2, waiting for transfers between devices: 0.01 us -> 6.96 us  [exchange(): return lax.all_to_all(chunks, axis, 0, 0, tiled=True)]
    ppermute x0 -> x1, starting transfers between devices: none -> 2.15 us  [on_device(): other = lax.ppermute(own, 'col', [(c, c ^ 1) for c in range(grid_cols)])]
    all_gather x1, blocking collectives: 34.3 us -> 32.5 us  [on_device(): planes = lax.all_gather(piece, 'row', tiled=True)]
  transfers between devices with their start and end apart: 2 -> 4, of which waited for: 1 -> 2; matrix products, arithmetic and copies ran while one was open for 0% -> 1% of each run, Pallas kernels for 11% -> 11%
where the time goes in v9:
time: 102 us; the launch traced here: 101 us
  blocking collectives  49.1 us (48%)
  starting transfers between devices  25.7 us (25%)
  Pallas kernels  15.7 us (15%)
  waiting for transfers between devices  6.96 us (7%)
  local copies, waits for them, and re-layouts  3.61 us (4%)
    all_gather x1, blocking collectives, on_device(): planes = lax.all_gather(piece, 'row', tiled=True)  32.5 us
    all_to_all x2, starting transfers between devices, exchange(): return lax.all_to_all(chunks, axis, 0, 0, tiled=True)  20 us
    all_to_all x1, blocking collectives, on_device(): lax.all_to_all(panel, 'col', 0, 0, tiled=True, axis_index_groups=same_core)  16.6 us
    pallas_call x1, Pallas kernels, panels(): pl.pallas_call(functools.partial(panels_kernel, wraps), out_shape=[pltpu....  11.5 us
    all_to_all x2, waiting for transfers between devices, exchange(): return lax.all_to_all(chunks, axis, 0, 0, tiled=True)  6.96 us
    pallas_call x1, Pallas kernels, trailing(): pl.pallas_call(functools.partial(trailing_kernel, grid_rows, grid_cols),...  4.15 us
    all_to_all x1, starting transfers between devices, on_device(): lax.all_to_all(copies, 'col', 0, 0, tiled=True, axis_index_groups=same_core)  3.57 us
    ppermute x1, starting transfers between devices, on_device(): other = lax.ppermute(own, 'col', [(c, c ^ 1) for c in range(grid_cols)])  2.15 us
  transfers between devices with their start and end apart: 4, of which 2 were waited for; matrix products, arithmetic and copies ran while one was open for 1% of the time, Pallas kernels for 11%

profile of v9, /device:TPU:1, one launch (start us, length us, event | category | flops | bytes accessed | tf_op | source)
XLA Modules:
  0.0 101.2 jit_solution(4413348174092049534)
XLA Ops:
  0.0 1.1 %slice.9 = f32[1024,128]{1,0:T(8,128)S(1)} slice(f32[1024,512]{1,0:T(8,128)} %matrix_ref.1), slice={[0:1024], [0:128]} | slice | bytes 1048576 | tf_op jit(solution)/shard_map/scatter_rows/slice | solution.py:269
  1.1 0.1 copy.8
  1.1 16.6 %all_to_all.20 = f32[16,8,8,128]{3,2,1,0:T(8,128)S(1)} all-to-all(f32[16,8,8,128]{3,2,1,0:T(8,128)S(1)} %bitcast.24), channel_id=1, replica_groups={{0,2,4,6,8,10,12,14,16,18,20,22,24,26,28,30},{1,3,5,7,9,11,13,15,17,19,..., dimensions={0} | all-to-all | bytes 1048576 | tf_op jit(solution)/shard_map/scatter_rows/all_to_all | solution.py:272
  17.7 0.8 broadcast_in_dim.15
  18.6 3.6 %all-to-all-start.1 = ((f32[16,8,8,128]{3,2,1,0:T(8,128)}), f32[16,8,8,128]{3,2,1,0:T(8,128)S(1)}, u32[]{:S(2)}, u32[]{:S(2)}) async-start(f32[16,8,8,128]{3,2,1,0:T(8,128)} %broadcast_in_dim.15), calls=%async_computation.1 | async-start | bytes 1048576 | tf_op jit(solution)/shard_map/gather_rows/all_to_all | solution.py:275
  22.2 32.5 %all-gather = f32[1,128,8,128]{3,2,0,1:T(8,128)S(1)} all-gather(f32[1,8,8,128]{3,2,0,1:T(8,128)S(1)} %get-tuple-element.17), channel_id=2, replica_groups=mesh['row'=16,'col'=32] {'row'}, dimensions={1}, use_global_device_ids=true | all-gather | bytes 557056 | tf_op jit(solution)/shard_map/gather_planes/all_gather | solution.py:277
  54.6 0.0 all-to-all-done.1.own_ref
  54.6 0.0 copy-start.1
  54.7 0.8 broadcast_in_dim.17
  55.4 16.1 %all-to-all-start.2 = ((f32[32,2,8,128]{3,2,1,0:T(8,128)}), f32[32,2,8,128]{3,2,1,0:T(8,128)S(1)}, u32[]{:S(2)}, u32[]{:S(2)}) async-start(f32[32,2,8,128]{3,2,1,0:T(8,128)} %broadcast_in_dim.17), calls=%async_computation.2 | async-start | bytes 524288 | tf_op jit(solution)/shard_map/spread_diagonal/all_to_all | solution.py:252
  71.6 2.1 %collective-permute-start = (f32[16,8,8,128]{3,2,1,0:T(8,128)S(1)}, f32[16,8,8,128]{3,2,1,0:T(8,128)}, u32[]{:S(2)}, u32[]{:S(2)}) collective-permute-start(f32[16,8,8,128]{3,2,1,0:T(8,128)S(1)} %all-to-all-done.1.own_ref), channel_id=1, source_target_pairs={{0,1},{1,0},{2,3},{3,2},{4,5},{5,4},{6,7},{7,6},{8,9},{9,8},{10,11... | collective-permute-start | bytes 1572872 | tf_op jit(solution)/shard_map/swap_panels/ppermute | solution.py:281
  73.7 6.8 %all-to-all-done.2 = f32[32,2,8,128]{3,2,1,0:T(8,128)S(1)} async-done(((f32[32,2,8,128]{3,2,1,0:T(8,128)}), f32[32,2,8,128]{3,2,1,0:T(8,128)S(1)}, u32[]{:S(2)}, u32[]{:S(2)}) %all-to-all-start.2) | async-done | bytes 262176 | tf_op jit(solution)/shard_map/spread_diagonal/all_to_all | solution.py:252
  80.6 0.8 copy.10
  81.4 0.0 copy-start
  81.4 3.9 %all-to-all-start.3 = ((f32[32,4,8,128]{3,2,1,0:T(8,128)}), f32[32,4,8,128]{3,2,1,0:T(8,128)S(1)}, u32[]{:S(2)}, u32[]{:S(2)}) async-start(f32[32,4,8,128]{3,2,1,0:T(8,128)} %bitcast.13), calls=%async_computation.3 | async-start | bytes 1048576 | tf_op jit(solution)/shard_map/exchange_cols/all_to_all | solution.py:252
  85.3 0.1 pad_add_fusion.place_ref
  85.4 0.0 collective-permute-done.other_ref
  85.4 0.0 copy-done.1
  85.4 11.5 %panels.1 = (f32[256,256]{1,0:T(8,128)S(1)}, f32[1024,256]{1,0:T(8,128)}) custom-call(s32[2]{0:T(128)S(1)} %pad_add_fusion.place_ref, f32[16,2,2,8,128]{4,3,2,1,0:T(8,128)S(1)} %bitcast.21, f32[16,8,8,128]{3,2,1,0:T(8,128)} %copy-done.1, f32[16,8,8,128]{3,2,1,0:T(8,128)} %collective-permute-done.other_ref), custom_call_target="tpu_custom_call" | custom-call | flops 872415232 | bytes 2883584 | tf_op jit(solution)/shard_map/panels/pallas_call | solution.py:138
  96.9 0.1 all-to-all-done.3
  97.0 0.0 copy-done
  97.0 4.1 %trailing.1 = f32[1024,512]{1,0:T(8,128)} custom-call(s32[2]{0:T(128)S(1)} %pad_add_fusion.place_ref, f32[1024,512]{1,0:T(8,128)S(1)} %copy-done, f32[1024,256]{1,0:T(8,128)} %get-tuple-element.14.lower_hbm_ref, f32[16,2,1,4,8,128]{5,4,3,2,1,0:T(8,128)S(1)} %bitcast.20, f32[256,256]{1,0:T(8,128)S(1)} %get-tuple-element.16.inverse_ref), custom_call_target="tpu_custom_call" | custom-call | tf_op jit(solution)/shard_map/trailing/pallas_call | solution.py:230
  (2 shorter events, 0.0 us)
Async XLA Ops:
  18.6 36.1 %all-to-all-start.1 = ((f32[16,8,8,128]{3,2,1,0:T(8,128)}), f32[16,8,8,128]{3,2,1,0:T(8,128)S(1)}, u32[]{:S(2)}, u32[]{:S(2)}) async-start(f32[16,8,8,128]{3,2,1,0:T(8,128)} %broadcast_in_dim.15), calls=%async_computation.1 | async-start | bytes 1048576 | tf_op jit(solution)/shard_map/gather_rows/all_to_all | solution.py:275
  54.6 30.7 %copy-start.1 = (f32[16,8,8,128]{3,2,1,0:T(8,128)}, f32[16,8,8,128]{3,2,1,0:T(8,128)S(1)}, u32[]{:S(2)}) copy-start(f32[16,8,8,128]{3,2,1,0:T(8,128)S(1)} %all-to-all-done.1.own_ref) | copy-start | bytes 1572868
  55.4 25.1 %all-to-all-start.2 = ((f32[32,2,8,128]{3,2,1,0:T(8,128)}), f32[32,2,8,128]{3,2,1,0:T(8,128)S(1)}, u32[]{:S(2)}, u32[]{:S(2)}) async-start(f32[32,2,8,128]{3,2,1,0:T(8,128)} %broadcast_in_dim.17), calls=%async_computation.2 | async-start | bytes 524288 | tf_op jit(solution)/shard_map/spread_diagonal/all_to_all | solution.py:252
  71.6 13.8 %collective-permute-start = (f32[16,8,8,128]{3,2,1,0:T(8,128)S(1)}, f32[16,8,8,128]{3,2,1,0:T(8,128)}, u32[]{:S(2)}, u32[]{:S(2)}) collective-permute-start(f32[16,8,8,128]{3,2,1,0:T(8,128)S(1)} %all-to-all-done.1.own_ref), channel_id=1, source_target_pairs={{0,1},{1,0},{2,3},{3,2},{4,5},{5,4},{6,7},{7,6},{8,9},{9,8},{10,11... | collective-permute-start | bytes 1572872 | tf_op jit(solution)/shard_map/swap_panels/ppermute | solution.py:281
  81.4 15.6 %copy-start = (f32[1024,512]{1,0:T(8,128)S(1)}, f32[1024,512]{1,0:T(8,128)}, u32[]{:S(2)}) copy-start(f32[1024,512]{1,0:T(8,128)} %matrix_ref.1) | copy-start | bytes 6291460
  81.4 15.6 %all-to-all-start.3 = ((f32[32,4,8,128]{3,2,1,0:T(8,128)}), f32[32,4,8,128]{3,2,1,0:T(8,128)S(1)}, u32[]{:S(2)}, u32[]{:S(2)}) async-start(f32[32,4,8,128]{3,2,1,0:T(8,128)} %bitcast.13), calls=%async_computation.3 | async-start | bytes 1048576 | tf_op jit(solution)/shard_map/exchange_cols/all_to_all | solution.py:252

commit v10 on v9

--- a/solution.py
+++ b/solution.py
@@ -37,27 +37,38 @@
     sub_row = lax.broadcasted_iota(jnp.int32, shape, 0)
 
     def over_lanes(tile, lane):
-        return jnp.broadcast_to(tile[:, lane : lane + 1], shape)
+        return [jnp.broadcast_to(tile[:, lane + k : lane + k + 1], shape) for k in range(GROUP)]
 
     def over_rows(tile, row):
         return jnp.broadcast_to(tile[row : row + 1], shape)
 
     scaled = []
+    carried = None
     for own in range(len(tiles)):
         block, lane = divmod(pivot_lane + GROUP * own, TILE)
-        columns = [
-            [over_lanes(parts[block], lane + k) for k in range(GROUP)] for parts in tiles[own:]
-        ]
+        columns = [over_lanes(parts[block], lane) for parts in tiles[own + 1 :]]
+        columns.insert(0, carried or over_lanes(tiles[own][block], lane))
+        ahead = own + 1 < len(tiles) and lane + GROUP < TILE
+        carried = None
+        if ahead:
+            beside = over_lanes(tiles[own][block], lane + GROUP)
+            carried = over_lanes(tiles[own + 1][block], lane + GROUP)
         pivots = jnp.ones(shape, jnp.float32)
         for k in range(GROUP):
             pivot_row = {j: over_rows(columns[0][j], k) for j in range(k, GROUP)}
             inverse = 1.0 / pivot_row[k]
             pivots = jnp.where(sub_row == k, pivot_row[k], pivots)
             rows = [over_rows(part, k) for part in tiles[own]]
+            if ahead:
+                beside_row = [over_rows(column, k) for column in beside]
             for t, column in enumerate(columns, own):
                 factor = column[k] * inverse
                 for j in range(k + 1, GROUP):
                     column[j] = column[j] - factor * pivot_row[j]
+                if ahead and t == own:
+                    beside = [kept - factor * row for kept, row in zip(beside, beside_row)]
+                if ahead and t == own + 1:
+                    carried = [kept - factor * row for kept, row in zip(carried, beside_row)]
                 if t == own:
                     factor = jnp.where(sub_row > k, factor, 0.0)
                 tiles[t] = [part - factor * row for part, row in zip(tiles[t], rows)]
@@ -248,6 +259,33 @@
     )(place, matrix, lower, cols, inverse)
 
 
+def by_wrap_kernel(planes_ref, parts_ref, sems):
+    copies = [
+        pltpu.make_async_copy(planes_ref.at[:, w], parts_ref.at[w], sems.at[w])
+        for w in range(parts_ref.shape[0])
+    ]
+    for copy in copies:
+        copy.start()
+    for copy in copies:
+        copy.wait()
+
+
+def by_wrap(planes):
+    count, wraps, *rest = planes.shape
+    return pl.pallas_call(
+        by_wrap_kernel,
+        out_shape=pltpu.HBM((wraps, count, *rest), planes.dtype),
+        in_specs=[pl.BlockSpec(memory_space=pltpu.VMEM)],
+        out_specs=pl.BlockSpec(memory_space=pltpu.HBM),
+        scratch_shapes=[pltpu.SemaphoreType.DMA((wraps,))],
+        cost_estimate=pl.CostEstimate(
+            flops=0, bytes_accessed=8 * planes.size, transcendentals=0
+        ),
+        compiler_params=pltpu.CompilerParams(vmem_limit_bytes=2**20),
+        name="by_wrap",
+    )(*in_vmem(planes))
+
+
 def exchange(chunks, axis):
     return lax.all_to_all(chunks, axis, 0, 0, tiled=True)
 
@@ -282,8 +320,8 @@
     with jax.named_scope("spread_diagonal"):
         diag = to_all(planes[:PANELS, 0], "col")
     with jax.named_scope("exchange_cols"):
-        diag, planes = lax.optimization_barrier((diag, planes))
-        parts = planes.reshape(grid_rows, wraps, tile_cols, GROUP, TILE).swapaxes(0, 1)
+        parts = by_wrap(planes.reshape(grid_rows, wraps, tile_cols, GROUP, TILE))
+        diag, parts = lax.optimization_barrier((diag, parts))
         cols = exchange(parts.reshape(grid_cols, tile_cols, GROUP, TILE), "col")
         cols = cols.reshape(chips, PANELS, 1, *cols.shape[1:])
     diag = diag.reshape(chips, PANELS, *diag.shape[1:])

time: 102 us -> 101 us (level)
    pallas_call x1, Pallas kernels: 11.5 us -> 10.1 us  [panels(): pl.pallas_call(functools.partial(panels_kernel, wraps), out_shape=[pltpu....]
  transfers between devices with their start and end apart: 4 -> 4, of which waited for: 2 -> 2; matrix products, arithmetic and copies ran while one was open for 1% -> 0% of each run, Pallas kernels for 11% -> 11%
where the time goes in v10:
time: 101 us; the launch traced here: 100 us
  blocking collectives  49.1 us (49%)
  starting transfers between devices  25.7 us (25%)
  Pallas kernels  15 us (15%)
  waiting for transfers between devices  7.57 us (7%)
  local copies, waits for them, and re-layouts  2.77 us (3%)
    all_gather x1, blocking collectives, on_device(): planes = lax.all_gather(piece, 'row', tiled=True)  32.5 us
    all_to_all x2, starting transfers between devices, exchange(): return lax.all_to_all(chunks, axis, 0, 0, tiled=True)  20 us
    all_to_all x1, blocking collectives, on_device(): lax.all_to_all(panel, 'col', 0, 0, tiled=True, axis_index_groups=same_core)  16.6 us
    pallas_call x1, Pallas kernels, panels(): pl.pallas_call(functools.partial(panels_kernel, wraps), out_shape=[pltpu....  10.1 us
    all_to_all x2, waiting for transfers between devices, exchange(): return lax.all_to_all(chunks, axis, 0, 0, tiled=True)  7.57 us
    pallas_call x1, Pallas kernels, trailing(): pl.pallas_call(functools.partial(trailing_kernel, grid_rows, grid_cols),...  4.15 us
    all_to_all x1, starting transfers between devices, on_device(): lax.all_to_all(copies, 'col', 0, 0, tiled=True, axis_index_groups=same_core)  3.57 us
    ppermute x1, starting transfers between devices, on_device(): other = lax.ppermute(own, 'col', [(c, c ^ 1) for c in range(grid_cols)])  2.15 us
  transfers between devices with their start and end apart: 4, of which 2 were waited for; matrix products, arithmetic and copies ran while one was open for 0% of the time, Pallas kernels for 11%

profile of v10, /device:TPU:1, one launch (start us, length us, event | category | flops | bytes accessed | tf_op | source)
XLA Modules:
  0.0 100.3 jit_solution(6079834586446242969)
XLA Ops:
  0.0 1.1 %slice.9 = f32[1024,128]{1,0:T(8,128)S(1)} slice(f32[1024,512]{1,0:T(8,128)} %matrix_ref.1), slice={[0:1024], [0:128]} | slice | bytes 1048576 | tf_op jit(solution)/shard_map/scatter_rows/slice | solution.py:307
  1.1 0.1 copy.4
  1.1 16.6 %all_to_all.20 = f32[16,8,8,128]{3,2,1,0:T(8,128)S(1)} all-to-all(f32[16,8,8,128]{3,2,1,0:T(8,128)S(1)} %bitcast.23), channel_id=1, replica_groups={{0,2,4,6,8,10,12,14,16,18,20,22,24,26,28,30},{1,3,5,7,9,11,13,15,17,19,..., dimensions={0} | all-to-all | bytes 1048576 | tf_op jit(solution)/shard_map/scatter_rows/all_to_all | solution.py:310
  17.7 0.8 broadcast_in_dim.15
  18.6 3.6 %all-to-all-start.1 = ((f32[16,8,8,128]{3,2,1,0:T(8,128)}), f32[16,8,8,128]{3,2,1,0:T(8,128)S(1)}, u32[]{:S(2)}, u32[]{:S(2)}) async-start(f32[16,8,8,128]{3,2,1,0:T(8,128)} %broadcast_in_dim.15), calls=%async_computation.1 | async-start | bytes 1048576 | tf_op jit(solution)/shard_map/gather_rows/all_to_all | solution.py:313
  22.2 32.5 %all-gather = f32[1,128,8,128]{3,2,0,1:T(8,128)S(1)} all-gather(f32[1,8,8,128]{3,2,0,1:T(8,128)S(1)} %get-tuple-element.17), channel_id=2, replica_groups=mesh['row'=16,'col'=32] {'row'}, dimensions={1}, use_global_device_ids=true | all-gather | bytes 557056 | tf_op jit(solution)/shard_map/gather_planes/all_gather | solution.py:315
  54.6 0.0 all-to-all-done.1.own_ref
  54.6 0.0 copy-start.1
  54.7 0.8 broadcast_in_dim.17
  55.4 16.1 %all-to-all-start.2 = ((f32[32,2,8,128]{3,2,1,0:T(8,128)}), f32[32,2,8,128]{3,2,1,0:T(8,128)S(1)}, u32[]{:S(2)}, u32[]{:S(2)}) async-start(f32[32,2,8,128]{3,2,1,0:T(8,128)} %broadcast_in_dim.17), calls=%async_computation.2 | async-start | bytes 524288 | tf_op jit(solution)/shard_map/spread_diagonal/all_to_all | solution.py:290
  71.6 2.1 %collective-permute-start = (f32[16,8,8,128]{3,2,1,0:T(8,128)S(1)}, f32[16,8,8,128]{3,2,1,0:T(8,128)}, u32[]{:S(2)}, u32[]{:S(2)}) collective-permute-start(f32[16,8,8,128]{3,2,1,0:T(8,128)S(1)} %all-to-all-done.1.own_ref), channel_id=1, source_target_pairs={{0,1},{1,0},{2,3},{3,2},{4,5},{5,4},{6,7},{7,6},{8,9},{9,8},{10,11... | collective-permute-start | bytes 1572872 | tf_op jit(solution)/shard_map/swap_panels/ppermute | solution.py:319
  73.7 0.8 by_wrap.1
  74.6 6.0 %all-to-all-done.2 = f32[32,2,8,128]{3,2,1,0:T(8,128)S(1)} async-done(((f32[32,2,8,128]{3,2,1,0:T(8,128)}), f32[32,2,8,128]{3,2,1,0:T(8,128)S(1)}, u32[]{:S(2)}, u32[]{:S(2)}) %all-to-all-start.2) | async-done | bytes 262176 | tf_op jit(solution)/shard_map/spread_diagonal/all_to_all | solution.py:290
  80.6 0.0 copy-start
  80.6 3.9 %all-to-all-start.3 = ((f32[32,4,8,128]{3,2,1,0:T(8,128)}), f32[32,4,8,128]{3,2,1,0:T(8,128)S(1)}, u32[]{:S(2)}, u32[]{:S(2)}) async-start(f32[32,4,8,128]{3,2,1,0:T(8,128)} %bitcast.22), calls=%async_computation.3 | async-start | bytes 1048576 | tf_op jit(solution)/shard_map/exchange_cols/all_to_all | solution.py:290
  84.5 0.1 pad_add_fusion.place_ref
  84.5 0.0 collective-permute-done.other_ref
  84.5 0.0 copy-done.1
  84.5 10.1 %panels.1 = (f32[256,256]{1,0:T(8,128)S(1)}, f32[1024,256]{1,0:T(8,128)}) custom-call(s32[2]{0:T(128)S(1)} %pad_add_fusion.place_ref, f32[16,2,2,8,128]{4,3,2,1,0:T(8,128)S(1)} %bitcast.21, f32[16,8,8,128]{3,2,1,0:T(8,128)} %copy-done.1, f32[16,8,8,128]{3,2,1,0:T(8,128)} %collective-permute-done.other_ref), custom_call_target="tpu_custom_call" | custom-call | flops 872415232 | bytes 2883584 | tf_op jit(solution)/shard_map/panels/pallas_call | solution.py:149
  94.6 1.6 %all-to-all-done.3 = f32[32,4,8,128]{3,2,1,0:T(8,128)S(1)} async-done(((f32[32,4,8,128]{3,2,1,0:T(8,128)}), f32[32,4,8,128]{3,2,1,0:T(8,128)S(1)}, u32[]{:S(2)}, u32[]{:S(2)}) %all-to-all-start.3) | async-done | bytes 524320 | tf_op jit(solution)/shard_map/exchange_cols/all_to_all | solution.py:290
  96.2 0.0 copy-done
  96.2 4.1 %trailing.1 = f32[1024,512]{1,0:T(8,128)} custom-call(s32[2]{0:T(128)S(1)} %pad_add_fusion.place_ref, f32[1024,512]{1,0:T(8,128)S(1)} %copy-done, f32[1024,256]{1,0:T(8,128)} %get-tuple-element.14.lower_hbm_ref, f32[16,2,1,4,8,128]{5,4,3,2,1,0:T(8,128)S(1)} %bitcast.20, f32[256,256]{1,0:T(8,128)S(1)} %get-tuple-element.16.inverse_ref), custom_call_target="tpu_custom_call" | custom-call | tf_op jit(solution)/shard_map/trailing/pallas_call | solution.py:241
  (2 shorter events, 0.0 us)
Async XLA Ops:
  18.6 36.1 %all-to-all-start.1 = ((f32[16,8,8,128]{3,2,1,0:T(8,128)}), f32[16,8,8,128]{3,2,1,0:T(8,128)S(1)}, u32[]{:S(2)}, u32[]{:S(2)}) async-start(f32[16,8,8,128]{3,2,1,0:T(8,128)} %broadcast_in_dim.15), calls=%async_computation.1 | async-start | bytes 1048576 | tf_op jit(solution)/shard_map/gather_rows/all_to_all | solution.py:313
  54.6 29.9 %copy-start.1 = (f32[16,8,8,128]{3,2,1,0:T(8,128)}, f32[16,8,8,128]{3,2,1,0:T(8,128)S(1)}, u32[]{:S(2)}) copy-start(f32[16,8,8,128]{3,2,1,0:T(8,128)S(1)} %all-to-all-done.1.own_ref) | copy-start | bytes 1572868
  55.4 25.1 %all-to-all-start.2 = ((f32[32,2,8,128]{3,2,1,0:T(8,128)}), f32[32,2,8,128]{3,2,1,0:T(8,128)S(1)}, u32[]{:S(2)}, u32[]{:S(2)}) async-start(f32[32,2,8,128]{3,2,1,0:T(8,128)} %broadcast_in_dim.17), calls=%async_computation.2 | async-start | bytes 524288 | tf_op jit(solution)/shard_map/spread_diagonal/all_to_all | solution.py:290
  71.6 12.9 %collective-permute-start = (f32[16,8,8,128]{3,2,1,0:T(8,128)S(1)}, f32[16,8,8,128]{3,2,1,0:T(8,128)}, u32[]{:S(2)}, u32[]{:S(2)}) collective-permute-start(f32[16,8,8,128]{3,2,1,0:T(8,128)S(1)} %all-to-all-done.1.own_ref), channel_id=1, source_target_pairs={{0,1},{1,0},{2,3},{3,2},{4,5},{5,4},{6,7},{7,6},{8,9},{9,8},{10,11... | collective-permute-start | bytes 1572872 | tf_op jit(solution)/shard_map/swap_panels/ppermute | solution.py:319
  80.6 15.6 %copy-start = (f32[1024,512]{1,0:T(8,128)S(1)}, f32[1024,512]{1,0:T(8,128)}, u32[]{:S(2)}) copy-start(f32[1024,512]{1,0:T(8,128)} %matrix_ref.1) | copy-start | bytes 6291460
  80.6 15.6 %all-to-all-start.3 = ((f32[32,4,8,128]{3,2,1,0:T(8,128)}), f32[32,4,8,128]{3,2,1,0:T(8,128)S(1)}, u32[]{:S(2)}, u32[]{:S(2)}) async-start(f32[32,4,8,128]{3,2,1,0:T(8,128)} %bitcast.22), calls=%async_computation.3 | async-start | bytes 1048576 | tf_op jit(solution)/shard_map/exchange_cols/all_to_all | solution.py:290

commit v11 on v10

--- a/solution.py
+++ b/solution.py
@@ -286,6 +286,33 @@
     )(*in_vmem(planes))
 
 
+def first_tiles_kernel(matrix_ref, panel_ref, sems):
+    tile_cols, wraps = matrix_ref.shape[:2]
+    copies = []
+    for w in range(wraps):
+        for b in range(tile_cols):
+            at = w * tile_cols + b
+            source = matrix_ref.at[b, w, :, :, pl.ds(0, TILE)]
+            copies.append(pltpu.make_async_copy(source, panel_ref.at[:, at], sems.at[at]))
+    for copy in copies:
+        copy.start()
+    for copy in copies:
+        copy.wait()
+
+
+def first_tiles(matrix):
+    tile_cols, wraps, chips, group, _ = matrix.shape
+    return pl.pallas_call(
+        first_tiles_kernel,
+        out_shape=pltpu.VMEM((chips, wraps * tile_cols, group, TILE), matrix.dtype),
+        in_specs=[pl.BlockSpec(memory_space=pltpu.HBM)],
+        out_specs=pl.BlockSpec(memory_space=pltpu.VMEM),
+        scratch_shapes=[pltpu.SemaphoreType.DMA((wraps * tile_cols,))],
+        compiler_params=pltpu.CompilerParams(vmem_limit_bytes=2 * 2**20),
+        name="first_tiles",
+    )(*in_hbm(matrix))
+
+
 def exchange(chunks, axis):
     return lax.all_to_all(chunks, axis, 0, 0, tiled=True)
 
@@ -304,8 +331,7 @@
     wraps = grid_cols // grid_rows
     place = jnp.stack([lax.axis_index("row"), lax.axis_index("col")]).astype(jnp.int32)
     with jax.named_scope("scatter_rows"):
-        panel = matrix[:, :TILE].reshape(tile_cols, wraps, chips, GROUP, TILE)
-        panel = panel.transpose(2, 1, 0, 3, 4).reshape(chips, wraps * tile_cols, GROUP, TILE)
+        panel = first_tiles(matrix.reshape(tile_cols, wraps, chips, GROUP, cols_count))
         same_core = [list(range(p, grid_cols, PANELS)) for p in range(PANELS)]
         piece = lax.all_to_all(panel, "col", 0, 0, tiled=True, axis_index_groups=same_core)[0]
     with jax.named_scope("gather_rows"):

time: 101 us -> 101 us (level)
  Pallas kernels: 15 us -> 16.2 us
  local copies, waits for them, and re-layouts: 2.77 us -> 1.64 us
    pallas_call x0 -> x1, Pallas kernels: none -> 1.13 us  [first_tiles(): pl.pallas_call(first_tiles_kernel, out_shape=pltpu.VMEM((chips, wraps * t...]
    slice x1 -> x0, local copies, waits for them, and re-layouts: 1.08 us -> none  [on_device(): panel = matrix[:, :TILE].reshape(tile_cols, wraps, chips, GROUP, TILE)]
where the time goes in v11:
time: 101 us; the launch traced here: 100 us
  blocking collectives  49.1 us (49%)
  starting transfers between devices  25.7 us (25%)
  Pallas kernels  16.2 us (16%)
  waiting for transfers between devices  7.57 us (7%)
  local copies, waits for them, and re-layouts  1.64 us (2%)
    all_gather x1, blocking collectives, on_device(): planes = lax.all_gather(piece, 'row', tiled=True)  32.5 us
    all_to_all x2, starting transfers between devices, exchange(): return lax.all_to_all(chunks, axis, 0, 0, tiled=True)  20 us
    all_to_all x1, blocking collectives, on_device(): lax.all_to_all(panel, 'col', 0, 0, tiled=True, axis_index_groups=same_core)  16.6 us
    pallas_call x1, Pallas kernels, panels(): pl.pallas_call(functools.partial(panels_kernel, wraps), out_shape=[pltpu....  10.1 us
    all_to_all x2, waiting for transfers between devices, exchange(): return lax.all_to_all(chunks, axis, 0, 0, tiled=True)  7.57 us
    pallas_call x1, Pallas kernels, trailing(): pl.pallas_call(functools.partial(trailing_kernel, grid_rows, grid_cols),...  4.15 us
    all_to_all x1, starting transfers between devices, on_device(): lax.all_to_all(copies, 'col', 0, 0, tiled=True, axis_index_groups=same_core)  3.57 us
    ppermute x1, starting transfers between devices, on_device(): other = lax.ppermute(own, 'col', [(c, c ^ 1) for c in range(grid_cols)])  2.15 us
  transfers between devices with their start and end apart: 4, of which 2 were waited for; matrix products, arithmetic and copies ran while one was open for 0% of the time, Pallas kernels for 11%

profile of v11, /device:TPU:1, one launch (start us, length us, event | category | flops | bytes accessed | tf_op | source)
XLA Modules:
  0.0 100.3 jit_solution(173791203606198968)
XLA Ops:
  0.0 1.1 %first_tiles.1 = f32[16,8,8,128]{3,2,1,0:T(8,128)S(1)} custom-call(f32[4,2,16,8,512]{4,3,2,1,0:T(8,128)} %bitcast.15), custom_call_target="tpu_custom_call" | custom-call | tf_op jit(solution)/shard_map/scatter_rows/first_tiles/pallas_call | solution.py:305
  1.1 16.6 %all_to_all.20 = f32[16,8,8,128]{3,2,1,0:T(8,128)S(1)} all-to-all(f32[16,8,8,128]{3,2,1,0:T(8,128)S(1)} %first_tiles.1), channel_id=1, replica_groups={{0,2,4,6,8,10,12,14,16,18,20,22,24,26,28,30},{1,3,5,7,9,11,13,15,17,19,..., dimensions={0} | all-to-all | bytes 1048576 | tf_op jit(solution)/shard_map/scatter_rows/all_to_all | solution.py:336
  17.7 0.8 broadcast_in_dim.15
  18.6 3.6 %all-to-all-start.1 = ((f32[16,8,8,128]{3,2,1,0:T(8,128)}), f32[16,8,8,128]{3,2,1,0:T(8,128)S(1)}, u32[]{:S(2)}, u32[]{:S(2)}) async-start(f32[16,8,8,128]{3,2,1,0:T(8,128)} %broadcast_in_dim.15), calls=%async_computation.1 | async-start | bytes 1048576 | tf_op jit(solution)/shard_map/gather_rows/all_to_all | solution.py:339
  22.2 32.5 %all-gather = f32[1,128,8,128]{3,2,0,1:T(8,128)S(1)} all-gather(f32[1,8,8,128]{3,2,0,1:T(8,128)S(1)} %get-tuple-element.17), channel_id=2, replica_groups=mesh['row'=16,'col'=32] {'row'}, dimensions={1}, use_global_device_ids=true | all-gather | bytes 557056 | tf_op jit(solution)/shard_map/gather_planes/all_gather | solution.py:341
  54.6 0.0 all-to-all-done.1.own_ref
  54.6 0.0 copy-start.1
  54.7 0.8 broadcast_in_dim.17
  55.4 16.1 %all-to-all-start.2 = ((f32[32,2,8,128]{3,2,1,0:T(8,128)}), f32[32,2,8,128]{3,2,1,0:T(8,128)S(1)}, u32[]{:S(2)}, u32[]{:S(2)}) async-start(f32[32,2,8,128]{3,2,1,0:T(8,128)} %broadcast_in_dim.17), calls=%async_computation.2 | async-start | bytes 524288 | tf_op jit(solution)/shard_map/spread_diagonal/all_to_all | solution.py:317
  71.6 2.1 %collective-permute-start = (f32[16,8,8,128]{3,2,1,0:T(8,128)S(1)}, f32[16,8,8,128]{3,2,1,0:T(8,128)}, u32[]{:S(2)}, u32[]{:S(2)}) collective-permute-start(f32[16,8,8,128]{3,2,1,0:T(8,128)S(1)} %all-to-all-done.1.own_ref), channel_id=1, source_target_pairs={{0,1},{1,0},{2,3},{3,2},{4,5},{5,4},{6,7},{7,6},{8,9},{9,8},{10,11... | collective-permute-start | bytes 1572872 | tf_op jit(solution)/shard_map/swap_panels/ppermute | solution.py:345
  73.8 0.8 by_wrap.1
  74.6 6.0 %all-to-all-done.2 = f32[32,2,8,128]{3,2,1,0:T(8,128)S(1)} async-done(((f32[32,2,8,128]{3,2,1,0:T(8,128)}), f32[32,2,8,128]{3,2,1,0:T(8,128)S(1)}, u32[]{:S(2)}, u32[]{:S(2)}) %all-to-all-start.2) | async-done | bytes 262176 | tf_op jit(solution)/shard_map/spread_diagonal/all_to_all | solution.py:317
  80.6 0.0 copy-start
  80.6 3.9 %all-to-all-start.3 = ((f32[32,4,8,128]{3,2,1,0:T(8,128)}), f32[32,4,8,128]{3,2,1,0:T(8,128)S(1)}, u32[]{:S(2)}, u32[]{:S(2)}) async-start(f32[32,4,8,128]{3,2,1,0:T(8,128)} %bitcast.20), calls=%async_computation.3 | async-start | bytes 1048576 | tf_op jit(solution)/shard_map/exchange_cols/all_to_all | solution.py:317
  84.5 0.1 pad_add_fusion.place_ref
  84.5 0.0 collective-permute-done.other_ref
  84.5 0.0 copy-done.1
  84.5 10.1 %panels.1 = (f32[256,256]{1,0:T(8,128)S(1)}, f32[1024,256]{1,0:T(8,128)}) custom-call(s32[2]{0:T(128)S(1)} %pad_add_fusion.place_ref, f32[16,2,2,8,128]{4,3,2,1,0:T(8,128)S(1)} %bitcast.19, f32[16,8,8,128]{3,2,1,0:T(8,128)} %copy-done.1, f32[16,8,8,128]{3,2,1,0:T(8,128)} %collective-permute-done.other_ref), custom_call_target="tpu_custom_call" | custom-call | flops 872415232 | bytes 2883584 | tf_op jit(solution)/shard_map/panels/pallas_call | solution.py:149
  94.6 1.6 %all-to-all-done.3 = f32[32,4,8,128]{3,2,1,0:T(8,128)S(1)} async-done(((f32[32,4,8,128]{3,2,1,0:T(8,128)}), f32[32,4,8,128]{3,2,1,0:T(8,128)S(1)}, u32[]{:S(2)}, u32[]{:S(2)}) %all-to-all-start.3) | async-done | bytes 524320 | tf_op jit(solution)/shard_map/exchange_cols/all_to_all | solution.py:317
  96.2 0.0 copy-done
  96.2 4.1 %trailing.1 = f32[1024,512]{1,0:T(8,128)} custom-call(s32[2]{0:T(128)S(1)} %pad_add_fusion.place_ref, f32[1024,512]{1,0:T(8,128)S(1)} %copy-done, f32[1024,256]{1,0:T(8,128)} %get-tuple-element.14.lower_hbm_ref, f32[16,2,1,4,8,128]{5,4,3,2,1,0:T(8,128)S(1)} %bitcast.18, f32[256,256]{1,0:T(8,128)S(1)} %get-tuple-element.16.inverse_ref), custom_call_target="tpu_custom_call" | custom-call | tf_op jit(solution)/shard_map/trailing/pallas_call | solution.py:241
  (2 shorter events, 0.0 us)
Async XLA Ops:
  18.6 36.1 %all-to-all-start.1 = ((f32[16,8,8,128]{3,2,1,0:T(8,128)}), f32[16,8,8,128]{3,2,1,0:T(8,128)S(1)}, u32[]{:S(2)}, u32[]{:S(2)}) async-start(f32[16,8,8,128]{3,2,1,0:T(8,128)} %broadcast_in_dim.15), calls=%async_computation.1 | async-start | bytes 1048576 | tf_op jit(solution)/shard_map/gather_rows/all_to_all | solution.py:339
  54.6 29.9 %copy-start.1 = (f32[16,8,8,128]{3,2,1,0:T(8,128)}, f32[16,8,8,128]{3,2,1,0:T(8,128)S(1)}, u32[]{:S(2)}) copy-start(f32[16,8,8,128]{3,2,1,0:T(8,128)S(1)} %all-to-all-done.1.own_ref) | copy-start | bytes 1572868
  55.4 25.1 %all-to-all-start.2 = ((f32[32,2,8,128]{3,2,1,0:T(8,128)}), f32[32,2,8,128]{3,2,1,0:T(8,128)S(1)}, u32[]{:S(2)}, u32[]{:S(2)}) async-start(f32[32,2,8,128]{3,2,1,0:T(8,128)} %broadcast_in_dim.17), calls=%async_computation.2 | async-start | bytes 524288 | tf_op jit(solution)/shard_map/spread_diagonal/all_to_all | solution.py:317
  71.6 12.9 %collective-permute-start = (f32[16,8,8,128]{3,2,1,0:T(8,128)S(1)}, f32[16,8,8,128]{3,2,1,0:T(8,128)}, u32[]{:S(2)}, u32[]{:S(2)}) collective-permute-start(f32[16,8,8,128]{3,2,1,0:T(8,128)S(1)} %all-to-all-done.1.own_ref), channel_id=1, source_target_pairs={{0,1},{1,0},{2,3},{3,2},{4,5},{5,4},{6,7},{7,6},{8,9},{9,8},{10,11... | collective-permute-start | bytes 1572872 | tf_op jit(solution)/shard_map/swap_panels/ppermute | solution.py:345
  80.6 15.6 %copy-start = (f32[1024,512]{1,0:T(8,128)S(1)}, f32[1024,512]{1,0:T(8,128)}, u32[]{:S(2)}) copy-start(f32[1024,512]{1,0:T(8,128)} %matrix_ref.1) | copy-start | bytes 6291460
  80.6 15.6 %all-to-all-start.3 = ((f32[32,4,8,128]{3,2,1,0:T(8,128)}), f32[32,4,8,128]{3,2,1,0:T(8,128)S(1)}, u32[]{:S(2)}, u32[]{:S(2)}) async-start(f32[32,4,8,128]{3,2,1,0:T(8,128)} %bitcast.20), calls=%async_computation.3 | async-start | bytes 1048576 | tf_op jit(solution)/shard_map/exchange_cols/all_to_all | solution.py:317
